TPU v7x, 512 devices: a whole 4x8x8 slice. The times are simulated.
512 devices in a mesh: expert: 64 (over z, y), tensor: 8 (over x, core).
Axes of the slice: x: 4, y: 8, z: 8, core: 2. Of those that a mesh axis runs over, the one named last changes fastest.
Arguments:
- tokens: bfloat16 [3072, 4096], P('expert', 'tensor'), may hold values from -6 to 6
- cotangent: bfloat16 [3072, 4096], P('expert', 'tensor'), may hold values from -6 to 6
- expert_ids: int32 [3072, 8], P('expert'), may hold values from 0 to 63, all different within a row; in each aligned block of 48 rows (0 to 47, 48 to 95, ...) at most 8 rows name the same one
- gate_values: float32 [3072, 8], P('expert'), may hold values from 0.05 to 1
- w_gate: bfloat16 [64, 768, 4096], P('expert', 'tensor'), may hold values from -0.09375 to 0.09375
- w_up: bfloat16 [64, 768, 4096], P('expert', 'tensor'), may hold values from -0.09375 to 0.09375
- w_down: bfloat16 [64, 768, 4096], P('expert', 'tensor'), may hold values from -0.21875 to 0.21875
Outputs:
- grad_tokens: bfloat16 [3072, 4096], P('expert', 'tensor')
- grad_gate: bfloat16 [64, 768, 4096], P('expert', 'tensor')
- grad_up: bfloat16 [64, 768, 4096], P('expert', 'tensor')
- grad_down: bfloat16 [64, 768, 4096], P('expert', 'tensor')
Inputs may be any that keep to these rules, and one draw needn't show every extreme that they name: `expert_ids`: each row names 8 different experts. Among the 48 tokens of one index of the expert axis no expert is named more than 8 times, and in every draw some expert is named exactly 8 times there.
All inputs are finite; a program needn't handle non-finite values.
Results may differ from a plain program's by a relative error of at most 0.019.
Values may be sent and summed in bfloat16 or wider, within the bound.
No kernel may reach another device: no remote copies, remote signals or barrier semaphores. Data moves between devices by JAX's collectives and lax.ppermute only.
A program may use at most 64 MiB of HBM per device.

v0:
```python
import jax
import jax.numpy as jnp
from jax import lax
from jax.sharding import PartitionSpec as P

TOP = 8


def expert_backward(rows_x, rows_d, w_gate, w_up, w_down):
    gate_pre = jnp.einsum("secd,ehd->sech", rows_x, w_gate, preferred_element_type=jnp.float32)
    up_pre = jnp.einsum("secd,ehd->sech", rows_x, w_up, preferred_element_type=jnp.float32)
    sigmoid = jax.nn.sigmoid(gate_pre)
    active = gate_pre * sigmoid
    hidden = (active * up_pre).astype(jnp.bfloat16)
    hidden_grad = jnp.einsum("secd,ehd->sech", rows_d, w_down, preferred_element_type=jnp.float32)
    up_grad = (hidden_grad * active).astype(jnp.bfloat16)
    gate_grad = (hidden_grad * up_pre * sigmoid * (1.0 + gate_pre * (1.0 - sigmoid))).astype(
        jnp.bfloat16
    )
    grad_gate = jnp.einsum(
        "sech,secd->ehd", gate_grad, rows_x, preferred_element_type=jnp.float32
    ).astype(jnp.bfloat16)
    grad_up = jnp.einsum(
        "sech,secd->ehd", up_grad, rows_x, preferred_element_type=jnp.float32
    ).astype(jnp.bfloat16)
    grad_down = jnp.einsum(
        "sech,secd->ehd", hidden, rows_d, preferred_element_type=jnp.float32
    ).astype(jnp.bfloat16)
    partial_value = jnp.einsum(
        "sech,ehd->secd", gate_grad, w_gate, preferred_element_type=jnp.float32
    )
    partial_value = partial_value + jnp.einsum(
        "sech,ehd->secd", up_grad, w_up, preferred_element_type=jnp.float32
    )
    return (partial_value, grad_gate, grad_up, grad_down)


def on_device(tokens, cotangent, expert_ids, gate_values, w_gate, w_up, w_down):
    tok_count = expert_ids.shape[0]
    local_count = w_gate.shape[0]
    groups = lax.axis_size("expert")
    experts = local_count * groups
    capacity = 4 * tok_count * TOP // (3 * experts)
    feat_width = tokens.shape[1]
    flat_ids = expert_ids.reshape(-1)
    onehot = (flat_ids[:, None] == jnp.arange(experts, dtype=jnp.int32)[None, :]).astype(jnp.int32)
    before = jnp.cumsum(onehot, axis=0) - onehot
    slot_pos = jnp.sum(before * onehot, axis=1)
    target = flat_ids * capacity + slot_pos
    matches = (target[None, :] == jnp.arange(experts * capacity, dtype=jnp.int32)[:, None]).reshape(
        experts * capacity, tok_count, TOP
    )
    by_token = jnp.any(matches, axis=2)
    occupied = jnp.any(by_token, axis=1)
    token_iota = jnp.arange(tok_count, dtype=jnp.int32)
    owner = jnp.sum(jnp.where(by_token, token_iota[None, :], 0), axis=1)
    slot_weight = jnp.sum(jnp.sum(jnp.where(matches, gate_values[None, :, :], 0.0), axis=2), axis=1)
    full_x, full_d = (
        lax.all_gather(tokens, "tensor", axis=1, tiled=True),
        lax.all_gather(cotangent, "tensor", axis=1, tiled=True),
    )
    sent_x = jnp.where(occupied[:, None], full_x[owner], jnp.zeros((), jnp.bfloat16))
    sent_d = (slot_weight[:, None] * full_d[owner].astype(jnp.float32)).astype(jnp.bfloat16)
    buffer_shape = (groups, local_count, capacity, full_x.shape[1])
    sent_x, sent_d = (sent_x.reshape(buffer_shape), sent_d.reshape(buffer_shape))
    rows_x, rows_d = (
        lax.all_to_all(sent_x, "expert", split_axis=0, concat_axis=0, tiled=True),
        lax.all_to_all(sent_d, "expert", split_axis=0, concat_axis=0, tiled=True),
    )
    partial_value, grad_gate, grad_up, grad_down = expert_backward(
        rows_x, rows_d, w_gate, w_up, w_down
    )
    summed = lax.psum(partial_value.astype(jnp.bfloat16), "tensor").astype(jnp.float32)
    returned = lax.dynamic_slice_in_dim(
        summed, lax.axis_index("tensor") * feat_width, feat_width, 3
    ).astype(jnp.bfloat16)
    arrived = lax.all_to_all(returned, "expert", split_axis=0, concat_axis=0, tiled=True).reshape(
        experts * capacity, feat_width
    )
    masked = jnp.where(occupied[:, None], arrived.astype(jnp.float32), jnp.zeros((), jnp.float32))
    grad_tokens = jax.ops.segment_sum(masked, owner, num_segments=tok_count).astype(jnp.bfloat16)
    return (grad_tokens, grad_gate, grad_up, grad_down)


def solution(mesh):
    return jax.shard_map(
        on_device,
        mesh=mesh,
        in_specs=(
            P("expert", "tensor"),
            P("expert", "tensor"),
            P("expert", None),
            P("expert", None),
            P("expert", "tensor", None),
            P("expert", "tensor", None),
            P("expert", "tensor", None),
        ),
        out_specs=(
            P("expert", "tensor"),
            P("expert", "tensor", None),
            P("expert", "tensor", None),
            P("expert", "tensor", None),
        ),
        check_vma=False,
    )
```

profile of v0, /device:TPU:1, one launch (start us, length us, event | category | flops | bytes accessed | tf_op | source)
XLA Modules:
  0.0 445.1 jit_solution(7881900945583448381)
XLA Ops:
  8.2 0.9 reduce-window.6
  11.0 19.9 %all_gather.7 = bf16[48,4096]{1,0:T(8,128)(2,1)S(1)} all-gather(bf16[48,512]{1,0:T(8,128)(2,1)} %param.7), channel_id=1, replica_groups=mesh['expert'=64,'tensor'=8] {'tensor'}, dimensions={1}, use_global_device_ids=true | all-gather | bytes 442368 | tf_op jit(solution)/shard_map/all_gather | solution.py:59
  30.9 4.3 gather_fusion.1
  35.2 4.5 %bitcast_select_fusion = bf16[64,1,8,4096]{3,2,1,0:T(8,128)(2,1)} fusion(bf16[512,4096]{1,0:T(8,128)(2,1)} %gather_fusion.1, pred[64,8]{1,0:T(8,128)(4,1)S(1)} %broadcast_in_dim.73), kind=kLoop, calls=%fused_computation.16 | loop fusion | flops 2097152 | bytes 8389120 | tf_op jit(solution)/shard_map/jit(_where)/select_n | solution.py:62
  39.7 11.7 %all-to-all-start.1 = ((bf16[64,1,8,4096]{3,2,1,0:T(8,128)(2,1)}), bf16[64,1,8,4096]{3,2,1,0:T(8,128)(2,1)}, u32[]{:S(2)}, u32[]{:S(2)}) async-start(bf16[64,1,8,4096]{3,2,1,0:T(8,128)(2,1)} %bitcast_select_fusion), calls=%async_computation.1 | async-start | bytes 8388608 | tf_op jit(solution)/shard_map/all_to_all | solution.py:67
  51.8 13.3 %all_gather.6 = bf16[48,4096]{1,0:T(8,128)(2,1)S(1)} all-gather(bf16[48,512]{1,0:T(8,128)(2,1)S(1)} %copy-done.2), channel_id=1, replica_groups=mesh['expert'=64,'tensor'=8] {'tensor'}, dimensions={1}, use_global_device_ids=true | all-gather | bytes 442368 | tf_op jit(solution)/shard_map/all_gather | solution.py:60
  65.0 4.4 gather_fusion
  69.4 5.6 %fusion = bf16[64,1,8,4096]{3,2,1,0:T(8,128)(2,1)} fusion(bf16[512,4096]{1,0:T(8,128)(2,1)} %gather_fusion, f32[64,8]{1,0:T(8,128)S(1)} %mul.57), kind=kLoop, calls=%fused_computation.4 | loop fusion | flops 6291456 | bytes 8390656 | tf_op jit(solution)/shard_map/convert_element_type | solution.py:63
  75.0 80.7 %all-to-all-done.1 = bf16[64,1,8,4096]{3,2,1,0:T(8,128)(2,1)} async-done(((bf16[64,1,8,4096]{3,2,1,0:T(8,128)(2,1)}), bf16[64,1,8,4096]{3,2,1,0:T(8,128)(2,1)}, u32[]{:S(2)}, u32[]{:S(2)}) %all-to-all-start.1) | async-done | bytes 4194336 | tf_op jit(solution)/shard_map/all_to_all | solution.py:67
  155.7 37.5 %all-to-all-start = ((bf16[64,1,8,4096]{3,2,1,0:T(8,128)(2,1)}), bf16[64,1,8,4096]{3,2,1,0:T(8,128)(2,1)}, u32[]{:S(2)}, u32[]{:S(2)}) async-start(bf16[64,1,8,4096]{3,2,1,0:T(8,128)(2,1)} %fusion), calls=%async_computation | async-start | bytes 8388608 | tf_op jit(solution)/shard_map/all_to_all | solution.py:68
  193.5 3.6 fusion.23
  197.0 3.4 fusion.20
  200.5 98.1 %all-to-all-done = bf16[64,1,8,4096]{3,2,1,0:T(8,128)(2,1)} async-done(((bf16[64,1,8,4096]{3,2,1,0:T(8,128)(2,1)}), bf16[64,1,8,4096]{3,2,1,0:T(8,128)(2,1)}, u32[]{:S(2)}, u32[]{:S(2)}) %all-to-all-start) | async-done | bytes 4194336 | tf_op jit(solution)/shard_map/all_to_all | solution.py:68
  298.6 3.4 fusion.40
  302.1 1.2 fusion.27
  303.3 3.2 fusion.1
  306.6 97.1 %all-reduce.2.cloned.1.call-done = bf16[64,1,8,4096]{3,2,0,1:T(8,128)(2,1)} async-done(((bf16[64,1,8,4096]{3,2,0,1:T(8,128)(2,1)}), bf16[64,1,8,4096]{3,2,0,1:T(8,128)(2,1)}) %all-reduce.2.cloned.1.call-update) | async-done | bytes 4194320 | tf_op jit(solution)/shard_map/psum | solution.py:73
  403.7 1.9 fusion.35
  405.6 13.2 %all-to-all-start.2 = ((bf16[64,1,8,512]{3,2,1,0:T(8,128)(2,1)}), bf16[64,1,8,512]{3,2,1,0:T(8,128)(2,1)S(1)}, u32[]{:S(2)}, u32[]{:S(2)}) async-start(bf16[64,1,8,512]{3,2,1,0:T(8,128)(2,1)} %fusion.35), calls=%async_computation.2 | async-start | bytes 1048576 | tf_op jit(solution)/shard_map/all_to_all | solution.py:77
  418.8 3.9 fusion.6
  422.7 3.9 fusion.7
  426.7 3.9 fusion.5
  430.6 3.2 all-to-all-done.2
  433.8 3.8 scatter_custom_fusion
  (32 shorter events, 4.1 us)
Async XLA Ops:
  7.2 186.3 %copy-start = (bf16[1,96,4096]{2,1,0:T(8,128)(2,1)S(1)}, bf16[1,96,4096]{2,1,0:T(8,128)(2,1)}, u32[]{:S(2)}) copy-start(bf16[1,96,4096]{2,1,0:T(8,128)(2,1)} %param.11) | copy-start | bytes 2359300
  39.7 11.7 %copy-start.3 = (f32[48,8]{0,1:T(8,128)S(1)}, f32[48,8]{0,1:T(8,128)}, u32[]{:S(2)}) copy-start(f32[48,8]{0,1:T(8,128)} %param.10) | copy-start | bytes 4612
  39.7 12.1 %copy-start.2 = (bf16[48,512]{1,0:T(8,128)(2,1)S(1)}, bf16[48,512]{1,0:T(8,128)(2,1)}, u32[]{:S(2)}) copy-start(bf16[48,512]{1,0:T(8,128)(2,1)} %param.8) | copy-start | bytes 147460
  39.7 116.0 %all-to-all-start.1 = ((bf16[64,1,8,4096]{3,2,1,0:T(8,128)(2,1)}), bf16[64,1,8,4096]{3,2,1,0:T(8,128)(2,1)}, u32[]{:S(2)}, u32[]{:S(2)}) async-start(bf16[64,1,8,4096]{3,2,1,0:T(8,128)(2,1)} %bitcast_select_fusion), calls=%async_computation.1 | async-start | bytes 8388608 | tf_op jit(solution)/shard_map/all_to_all | solution.py:67
  155.7 142.9 %all-to-all-start = ((bf16[64,1,8,4096]{3,2,1,0:T(8,128)(2,1)}), bf16[64,1,8,4096]{3,2,1,0:T(8,128)(2,1)}, u32[]{:S(2)}, u32[]{:S(2)}) async-start(bf16[64,1,8,4096]{3,2,1,0:T(8,128)(2,1)} %fusion), calls=%async_computation | async-start | bytes 8388608 | tf_op jit(solution)/shard_map/all_to_all | solution.py:68
  193.2 3.8 copy-start.1
  193.2 105.4 %copy-start.4 = (bf16[1,96,4096]{2,1,0:T(8,128)(2,1)S(1)}, bf16[1,96,4096]{2,1,0:T(8,128)(2,1)}, u32[]{:S(2)}) copy-start(bf16[1,96,4096]{2,1,0:T(8,128)(2,1)} %param.13) | copy-start | bytes 2359300
  193.2 210.5 %all-reduce.2.cloned.1.call-start = ((), (), s32[]{:S(2)}) async-start(), calls=%async_computation.3 | async-start | bytes 8388608 | tf_op jit(solution)/shard_map/psum | solution.py:73
  405.6 28.3 %all-to-all-start.2 = ((bf16[64,1,8,512]{3,2,1,0:T(8,128)(2,1)}), bf16[64,1,8,512]{3,2,1,0:T(8,128)(2,1)S(1)}, u32[]{:S(2)}, u32[]{:S(2)}) async-start(bf16[64,1,8,512]{3,2,1,0:T(8,128)(2,1)} %fusion.35), calls=%async_computation.2 | async-start | bytes 1048576 | tf_op jit(solution)/shard_map/all_to_all | solution.py:77
Sparse Core Ops, SparseCore 0:
  306.7 96.9 all-reduce.1
where the time goes:
time: 450 us; the launch traced here: 445 us
  waiting for transfers between devices  279 us (62%)
  starting transfers between devices  62.6 us (14%)
  blocking collectives  33.2 us (7%)
  matrix products  26.7 us (6%)
  other arithmetic  18.7 us (4%)
  between operations  14.2 us (3%)
  local copies, waits for them, and re-layouts  10.5 us (2%)
    all_to_all x1, waiting for transfers between devices, on_device(): lax.all_to_all(sent_d, 'expert', split_axis=0, concat_axis=0, tiled=True)  98.1 us
    psum x1, waiting for transfers between devices, on_device(): lax.psum(partial_value.astype(jnp.bfloat16), 'tensor').astype(jnp.float32)  97.1 us
    all_to_all x1, waiting for transfers between devices, on_device(): lax.all_to_all(sent_x, 'expert', split_axis=0, concat_axis=0, tiled=True)  80.7 us
    all_to_all x1, starting transfers between devices, on_device(): lax.all_to_all(sent_d, 'expert', split_axis=0, concat_axis=0, tiled=True)  37.5 us
    all_gather x1, blocking collectives, on_device(): lax.all_gather(tokens, 'tensor', axis=1, tiled=True)  19.9 us
    all_gather x1, blocking collectives, on_device(): lax.all_gather(cotangent, 'tensor', axis=1, tiled=True)  13.3 us
    all_to_all x1, starting transfers between devices, on_device(): lax.all_to_all(returned, 'expert', split_axis=0, concat_axis=0, tiled=True)  13.2 us
    all_to_all x1, starting transfers between devices, on_device(): lax.all_to_all(sent_x, 'expert', split_axis=0, concat_axis=0, tiled=True)  11.7 us
  transfers between devices with their start and end apart: 4, of which 4 were waited for; matrix products, arithmetic and copies ran while one was open for 7% of the time, Pallas kernels for 0%

commit v1 on v0

v1 whole, which is shorter than its diff:
```python
import jax
import jax.numpy as jnp
from jax import lax
from jax.experimental import pallas as pl
from jax.experimental.pallas import tpu as pltpu
from jax.sharding import PartitionSpec as P

TOP = 8
CAP = 8
X_CHIPS = 4
F32, BF16 = jnp.float32, jnp.bfloat16
VMEM = pl.BlockSpec(memory_space=pltpu.VMEM)
ANY = pl.BlockSpec(memory_space=pl.ANY)


def dot(a, b, ca, cb):
    return lax.dot_general(a, b, (((ca,), (cb,)), ((), ())), preferred_element_type=F32)


def pieces(v):
    out = []
    for _ in range(3):
        part = v.astype(BF16)
        out.append(part)
        v = v - part.astype(F32)
    return out


def dispatch_kernel(ids_ref, gate_ref, tok_ref, cot_ref, wg_ref, wu_ref, wd_ref,
                    sent_ref, place_ref, m0, m1, m2, m3, sems):
    chip = lax.axis_index("tensor") // 2
    hid = wg_ref.shape[0]
    feats = wg_ref.shape[1] // X_CHIPS
    copies = []
    for s, m in enumerate((m0, m1, m2, m3)):
        start = pl.multiple_of(lax.rem(chip + s, X_CHIPS) * feats, feats)
        for j, w in enumerate((wg_ref, wu_ref, wd_ref)):
            copies.append(pltpu.make_async_copy(
                w.at[:, pl.ds(start, feats)], m.at[pl.ds(j * hid, hid), :], sems.at[s, j]))
            copies[-1].start()
    toks, width = tok_ref.shape
    slots = sent_ref.shape[0]
    experts = slots // CAP
    ids = ids_ref[...]
    gates = gate_ref[...]
    expert_iota = lax.broadcasted_iota(jnp.int32, (toks, experts), 1)
    chosen = jnp.zeros((toks, experts), F32)
    weight = jnp.zeros((toks, experts), F32)
    for k in range(TOP):
        hit = ids[:, k:k + 1] == expert_iota
        chosen = chosen + hit.astype(F32)
        weight = weight + jnp.where(hit, gates[:, k:k + 1], 0.0)
    row = lax.broadcasted_iota(jnp.int32, (toks, toks), 0)
    col = lax.broadcasted_iota(jnp.int32, (toks, toks), 1)
    earlier = (col < row).astype(F32).astype(BF16)
    chosen_b = chosen.astype(BF16)
    slot = dot(earlier, chosen_b, 1, 0)
    spread = (lax.broadcasted_iota(jnp.int32, (experts, slots), 1) // CAP
              == lax.broadcasted_iota(jnp.int32, (experts, slots), 0)).astype(F32).astype(BF16)
    chosen_s = dot(chosen_b, spread, 1, 0)
    slot_s = dot(slot.astype(BF16), spread, 1, 0)
    capacity = (lax.broadcasted_iota(jnp.int32, (toks, slots), 1) % CAP).astype(F32)
    place = jnp.where((chosen_s > 0.5) & (slot_s == capacity), 1.0, 0.0)
    place_b = place.astype(BF16)
    place_ref[...] = place_b
    sent_ref[:, :width] = dot(place_b, tok_ref[...], 0, 0).astype(BF16)
    ones = jnp.ones((toks, 128), BF16)
    scale = jnp.zeros((slots, 128), F32)
    for part in pieces(weight):
        spread_part = dot(part, spread, 1, 0) * place
        scale = scale + dot(spread_part.astype(BF16), ones, 0, 0)
    rows_d = dot(place_b, cot_ref[...], 0, 0)
    for j in range(width // 128):
        sent_ref[:, width + j * 128:width + (j + 1) * 128] = (
            scale * rows_d[:, j * 128:(j + 1) * 128]).astype(BF16)
    for c in copies:
        c.wait()


def partial_kernel(own_ref, oth_ref, m0, m1, m2, m3, p0, p1, p2, p3):
    core = lax.rem(lax.axis_index("tensor"), 2)
    width = own_ref.shape[1] // 2
    hid = m0.shape[0] // 3
    mine = pl.ds(pl.multiple_of(core * width, width), width)
    theirs = pl.ds(pl.multiple_of((1 - core) * width, width), width)
    for m, p in ((m2, p2), (m1, p1), (m3, p3), (m0, p0)):
        gu = dot(m[:2 * hid, mine], own_ref[:, :width], 1, 1)
        gu = gu + dot(m[:2 * hid, theirs], oth_ref[:, :width], 1, 1)
        p[:2 * hid, :] = gu.astype(p.dtype)
        dn = dot(m[2 * hid:, mine], own_ref[:, width:], 1, 1)
        dn = dn + dot(m[2 * hid:, theirs], oth_ref[:, width:], 1, 1)
        p[2 * hid:, :] = dn.astype(p.dtype)


def act_kernel(p0, r1, r2, r3, gu_ref, hidden_ref):
    hid = hidden_ref.shape[0]
    total = p0[...] + r1[...].astype(F32) + r2[...].astype(F32) + r3[...].astype(F32)
    gate_pre, up_pre, hidden_grad = total[:hid], total[hid:2 * hid], total[2 * hid:]
    sigmoid = jax.nn.sigmoid(gate_pre)
    active = gate_pre * sigmoid
    hidden_ref[...] = (active * up_pre).astype(BF16)
    gu_ref[hid:, :] = (hidden_grad * active).astype(BF16)
    gu_ref[:hid, :] = (hidden_grad * up_pre * sigmoid * (1.0 + gate_pre * (1.0 - sigmoid))).astype(BF16)


def row_kernel(g0, g1, g2, g3, m0, m1, m2, m3, keep_ref, send_ref):
    core = lax.rem(lax.axis_index("tensor"), 2)
    width = keep_ref.shape[1]
    two = g0.shape[0]
    mine = pl.ds(pl.multiple_of(core * width, width), width)
    theirs = pl.ds(pl.multiple_of((1 - core) * width, width), width)
    for part, out in ((theirs, send_ref), (mine, keep_ref)):
        total = None
        for g, m in ((g0, m0), (g1, m1), (g2, m2), (g3, m3)):
            term = dot(g[...], m[:two, part], 0, 0)
            total = term if total is None else total + term
        out[...] = total.astype(out.dtype)


def grad_kernel(gu_ref, hidden_ref, rows_ref, gg_ref, gup_ref, gd_ref):
    hid = hidden_ref.shape[0]
    width = gg_ref.shape[1]
    both = dot(gu_ref[...], rows_ref[0, :, :width], 1, 0)
    gg_ref[...] = both[:hid].astype(BF16)
    gup_ref[...] = both[hid:].astype(BF16)
    gd_ref[...] = dot(hidden_ref[...], rows_ref[0, :, width:], 1, 0).astype(BF16)


def combine_kernel(place_ref, arrived_ref, out_ref):
    out_ref[...] = dot(place_ref[...], arrived_ref[...], 1, 0).astype(BF16)


def call(kernel, outs, n_in, scratch=(), in_specs=None, out_specs=None, flops=0, nbytes=0):
    return pl.pallas_call(
        kernel,
        out_shape=[jax.ShapeDtypeStruct(s, d) for s, d in outs],
        in_specs=in_specs or [VMEM] * n_in,
        out_specs=out_specs or [VMEM] * len(outs),
        scratch_shapes=list(scratch),
        compiler_params=pltpu.CompilerParams(vmem_limit_bytes=40 << 20),
        cost_estimate=pl.CostEstimate(flops=flops, bytes_accessed=nbytes, transcendentals=0),
    )


def on_device(tokens, cotangent, expert_ids, gate_values, w_gate, w_up, w_down):
    toks, width = tokens.shape
    hid, feats = w_gate.shape[1], w_gate.shape[2]
    groups = lax.axis_size("expert")
    n_tensor = lax.axis_size("tensor")
    slots = groups * CAP
    chip_feats = feats // X_CHIPS
    w_gate, w_up, w_down = (w.reshape(hid, feats) for w in (w_gate, w_up, w_down))

    def shift(v, s):
        return lax.ppermute(v, "tensor", [(i, (i + 2 * s) % n_tensor) for i in range(n_tensor)])

    def sibling(v):
        return lax.ppermute(v, "tensor", [(i, i ^ 1) for i in range(n_tensor)])

    message = ((3 * hid, chip_feats), BF16)
    sent, place, *blocks = call(
        dispatch_kernel,
        [((slots, 2 * width), BF16), ((toks, slots), BF16)] + [message] * X_CHIPS,
        7,
        scratch=[pltpu.SemaphoreType.DMA((X_CHIPS, 3))],
        in_specs=[VMEM] * 4 + [ANY] * 3,
        out_specs=[VMEM] * 2 + [ANY] * X_CHIPS,
        flops=10**8, nbytes=6 << 20,
    )(expert_ids, gate_values, tokens, cotangent, w_gate, w_up, w_down)
    rows = lax.all_to_all(sent.reshape(groups, CAP, 2 * width), "expert", 0, 0, tiled=True)
    rows = rows.reshape(slots, 2 * width)
    weights = [blocks[0]] + [shift(blocks[s], s) for s in range(1, X_CHIPS)]
    every = lax.all_gather(rows, "tensor", axis=0)
    other = sibling(rows)
    parts = call(
        partial_kernel,
        [((3 * hid, slots), F32)] + [((3 * hid, slots), BF16)] * 3,
        6, flops=12 * 10**8, nbytes=6 << 20,
    )(rows, other, *weights)
    got = [shift(parts[s], -s) for s in range(1, X_CHIPS)]
    gate_up, hidden = call(
        act_kernel, [((2 * hid, slots), BF16), ((hid, slots), BF16)], 4,
        flops=10**7, nbytes=2 << 20,
    )(parts[0], *got)
    gathered = [gate_up] + [shift(gate_up, s) for s in range(1, X_CHIPS)]
    keep, send = call(
        row_kernel, [((slots, width), F32), ((slots, width), BF16)], 8,
        flops=8 * 10**8, nbytes=5 << 20,
    )(*gathered, *weights)
    row_grad = (keep + sibling(send).astype(F32)).astype(BF16)
    arrived = lax.all_to_all(row_grad.reshape(groups, CAP, width), "expert", 0, 0, tiled=True)
    grads = pl.pallas_call(
        grad_kernel,
        grid=(n_tensor,),
        out_shape=[jax.ShapeDtypeStruct((hid, feats), BF16)] * 3,
        in_specs=[
            pl.BlockSpec((2 * hid, slots), lambda q: (0, 0)),
            pl.BlockSpec((hid, slots), lambda q: (0, 0)),
            pl.BlockSpec((1, slots, 2 * width), lambda q: (q, 0, 0)),
        ],
        out_specs=[pl.BlockSpec((hid, width), lambda q: (0, q))] * 3,
        compiler_params=pltpu.CompilerParams(vmem_limit_bytes=40 << 20),
        cost_estimate=pl.CostEstimate(flops=12 * 10**8, bytes_accessed=11 << 20, transcendentals=0),
    )(gate_up, hidden, every)
    (grad_tokens,) = call(
        combine_kernel, [((toks, width), BF16)], 2, flops=10**7, nbytes=1 << 20,
    )(place, arrived.reshape(slots, width))
    return (grad_tokens, *(g.reshape(1, hid, feats) for g in grads))


def solution(mesh):
    return jax.shard_map(
        on_device,
        mesh=mesh,
        in_specs=(
            P("expert", "tensor"),
            P("expert", "tensor"),
            P("expert", None),
            P("expert", None),
            P("expert", "tensor", None),
            P("expert", "tensor", None),
            P("expert", "tensor", None),
        ),
        out_specs=(
            P("expert", "tensor"),
            P("expert", "tensor", None),
            P("expert", "tensor", None),
            P("expert", "tensor", None),
        ),
        check_vma=False,
    )
```

time: 450 us -> 208 us (0.46)
  waiting for transfers between devices: 279 us -> 61.9 us
  blocking collectives: 33.2 us -> 67.7 us
  matrix products: 26.7 us -> 0 us
  starting transfers between devices: 62.6 us -> 39.4 us
  other arithmetic: 18.7 us -> 0.16 us
  Pallas kernels: 0 us -> 11.1 us
    all_to_all x3 -> x0, waiting for transfers between devices: 182 us -> none  [the longest x1 98.1 us: on_device(): lax.all_to_all(sent_d, 'expert', split_axis=0, concat_axis=0, tiled=True)]
    psum x1 -> x0, waiting for transfers between devices: 97.1 us -> none  [on_device(): lax.psum(partial_value.astype(jnp.bfloat16), 'tensor').astype(jnp.float32)]
    all_to_all x0 -> x2, blocking collectives: none -> 67.7 us  [the longest x1 44.5 us: on_device(): lax.all_to_all(sent.reshape(groups, CAP, 2 * width), 'expert', 0, 0, tile...]
    all_to_all x3 -> x0, starting transfers between devices: 62.4 us -> none  [the longest x1 37.5 us: on_device(): lax.all_to_all(sent_d, 'expert', split_axis=0, concat_axis=0, tiled=True)]
    ppermute x0 -> x11, waiting for transfers between devices: none -> 61.9 us  [the longest x9 60.4 us: shift(): lax.ppermute(v, 'tensor', [(i, (i + 2 * s) % n_tensor) for i in range(n_t...]
    ppermute x0 -> x11, starting transfers between devices: none -> 39.3 us  [the longest x9 30.5 us: shift(): lax.ppermute(v, 'tensor', [(i, (i + 2 * s) % n_tensor) for i in range(n_t...]
    all_gather x2 -> x0, blocking collectives: 33.2 us -> none  [the longest x1 19.9 us: on_device(): lax.all_gather(tokens, 'tensor', axis=1, tiled=True)]
    dot_general x8 -> x0, matrix products: 26.7 us -> none  [the longest x1 3.94 us: expert_backward(): jnp.einsum('sech,secd->ehd', hidden, rows_d, preferred_element_type=jnp.f...]
  transfers between devices with their start and end apart: 4 -> 12, of which waited for: 4 -> 8; matrix products, arithmetic and copies ran while one was open for 7% -> 0% of each run, Pallas kernels for 0% -> 2%
where the time goes in v1:
time: 208 us; the launch traced here: 206 us
  blocking collectives  67.7 us (33%)
  waiting for transfers between devices  61.9 us (30%)
  starting transfers between devices  39.4 us (19%)
  between operations  14.2 us (7%)
  local copies, waits for them, and re-layouts  11.1 us (5%)
  Pallas kernels  11.1 us (5%)
    ppermute x9, waiting for transfers between devices, shift(): lax.ppermute(v, 'tensor', [(i, (i + 2 * s) % n_tensor) for i in range(n_t...  60.4 us
    all_to_all x1, blocking collectives, on_device(): lax.all_to_all(sent.reshape(groups, CAP, 2 * width), 'expert', 0, 0, tile...  44.5 us
    ppermute x9, starting transfers between devices, shift(): lax.ppermute(v, 'tensor', [(i, (i + 2 * s) % n_tensor) for i in range(n_t...  30.5 us
    all_to_all x1, blocking collectives, on_device(): lax.all_to_all(row_grad.reshape(groups, CAP, width), 'expert', 0, 0, tile...  23.2 us
    unnamed x16, local copies, waits for them, and re-layouts  11.1 us
    ppermute x2, starting transfers between devices, sibling(): return lax.ppermute(v, 'tensor', [(i, i ^ 1) for i in range(n_tensor)])  8.82 us
    pallas_call x1, Pallas kernels, on_device(): pl.pallas_call(grad_kernel, grid=(n_tensor,), out_shape=[jax.ShapeDtypeSt...  4.31 us
  transfers between devices with their start and end apart: 12, of which 8 were waited for; matrix products, arithmetic and copies ran while one was open for 0% of the time, Pallas kernels for 2%

profile of v1, /device:TPU:1, one launch (start us, length us, event | category | flops | bytes accessed | tf_op | source)
XLA Modules:
  0.0 205.5 jit_solution(14609292559169493123)
XLA Ops:
  13.7 1.7 shard_map.102
  15.4 44.5 %all_to_all.10 = bf16[64,8,1024]{2,1,0:T(8,128)(2,1)} all-to-all(bf16[64,8,1024]{2,1,0:T(8,128)(2,1)S(1)} %bitcast.16), channel_id=1, replica_groups=mesh['expert'=64,'tensor'=8] {'expert'}, dimensions={0} | all-to-all | bytes 2097152 | tf_op jit(solution)/shard_map/all_to_all | solution.py:170
  59.9 5.2 %collective-permute-start = (bf16[512,1024]{1,0:T(8,128)(2,1)}, bf16[512,1024]{1,0:T(8,128)(2,1)S(1)}, u32[]{:S(2)}, u32[]{:S(2)}) collective-permute-start(bf16[512,1024]{1,0:T(8,128)(2,1)} %bitcast.13), channel_id=1, source_target_pairs={{0,1},{1,0},{2,3},{3,2},{4,5},{5,4},{6,7},{7,6},{8,9},{9,8},{10,11... | collective-permute-start | bytes 3145736 | tf_op jit(solution)/shard_map/ppermute | solution.py:158
  65.1 3.1 %collective-permute-start.1 = (bf16[288,1024]{1,0:T(8,128)(2,1)S(1)}, bf16[288,1024]{1,0:T(8,128)(2,1)S(1)}, u32[]{:S(2)}, u32[]{:S(2)}) collective-permute-start(bf16[288,1024]{1,0:T(8,128)(2,1)S(1)} %get-tuple-element.24), channel_id=1, source_target_pairs={{0,2},{1,3},{2,4},{3,5},{4,6},{5,7},{6,0},{7,1},{8,10},{9,11},{10,... | collective-permute-start | bytes 1769480 | tf_op jit(solution)/shard_map/ppermute | solution.py:155
  68.3 4.4 %collective-permute-start.2 = (bf16[288,1024]{1,0:T(8,128)(2,1)S(1)}, bf16[288,1024]{1,0:T(8,128)(2,1)S(1)}, u32[]{:S(2)}, u32[]{:S(2)}) collective-permute-start(bf16[288,1024]{1,0:T(8,128)(2,1)S(1)} %get-tuple-element.25), channel_id=1, source_target_pairs={{0,4},{1,5},{2,6},{3,7},{4,0},{5,1},{6,2},{7,3},{8,12},{9,13},{10,... | collective-permute-start | bytes 1769480 | tf_op jit(solution)/shard_map/ppermute | solution.py:155
  72.6 3.1 %collective-permute-start.3 = (bf16[288,1024]{1,0:T(8,128)(2,1)S(1)}, bf16[288,1024]{1,0:T(8,128)(2,1)S(1)}, u32[]{:S(2)}, u32[]{:S(2)}) collective-permute-start(bf16[288,1024]{1,0:T(8,128)(2,1)S(1)} %get-tuple-element.26), channel_id=1, source_target_pairs={{0,6},{1,7},{2,0},{3,1},{4,2},{5,3},{6,4},{7,5},{8,14},{9,15},{10,... | collective-permute-start | bytes 1769480 | tf_op jit(solution)/shard_map/ppermute | solution.py:155
  75.7 13.7 %collective-permute-done.1.m1 = bf16[288,1024]{1,0:T(8,128)(2,1)S(1)} collective-permute-done((bf16[288,1024]{1,0:T(8,128)(2,1)S(1)}, bf16[288,1024]{1,0:T(8,128)(2,1)S(1)}, u32[]{:S(2)}, u32[]{:S(2)}) %collective-permute-start.1) | collective-permute-done | bytes 589856 | tf_op jit(solution)/shard_map/ppermute | solution.py:155
  89.4 26.9 %collective-permute-done.2.m2 = bf16[288,1024]{1,0:T(8,128)(2,1)S(1)} collective-permute-done((bf16[288,1024]{1,0:T(8,128)(2,1)S(1)}, bf16[288,1024]{1,0:T(8,128)(2,1)S(1)}, u32[]{:S(2)}, u32[]{:S(2)}) %collective-permute-start.2) | collective-permute-done | bytes 589856 | tf_op jit(solution)/shard_map/ppermute | solution.py:155
  116.3 3.4 %collective-permute-done.3.m3 = bf16[288,1024]{1,0:T(8,128)(2,1)S(1)} collective-permute-done((bf16[288,1024]{1,0:T(8,128)(2,1)S(1)}, bf16[288,1024]{1,0:T(8,128)(2,1)S(1)}, u32[]{:S(2)}, u32[]{:S(2)}) %collective-permute-start.3) | collective-permute-done | bytes 589856 | tf_op jit(solution)/shard_map/ppermute | solution.py:155
  120.9 2.8 %shard_map.103 = (f32[288,512]{1,0:T(8,128)S(1)}, bf16[288,512]{1,0:T(8,128)(2,1)S(1)}, bf16[288,512]{1,0:T(8,128)(2,1)S(1)}, bf16[288,512]{1,0:T(8,128)(2,1)S(1)}) custom-call(bf16[512,1024]{1,0:T(8,128)(2,1)S(1)} %bitcast.14, bf16[512,1024]{1,0:T(8,128)(2,1)S(1)} %collective-permute-done.oth_ref, bf16[288,1024]{1,0:T(8,128)(2,1)S(1)} %get-tuple-element.23.m0, ...), custom_call_target="tpu_custom_call" | custom-call | flops 1200000000 | bytes 6291456 | tf_op jit(solution)/shard_map/pallas_call | solution.py:175
  123.7 3.0 %collective-permute-start.4 = (bf16[288,512]{1,0:T(8,128)(2,1)S(1)}, bf16[288,512]{1,0:T(8,128)(2,1)S(1)}, u32[]{:S(2)}, u32[]{:S(2)}) collective-permute-start(bf16[288,512]{1,0:T(8,128)(2,1)S(1)} %get-tuple-element.28), channel_id=1, source_target_pairs={{0,6},{1,7},{2,0},{3,1},{4,2},{5,3},{6,4},{7,5},{8,14},{9,15},{10,... | collective-permute-start | bytes 884744 | tf_op jit(solution)/shard_map/ppermute | solution.py:155
  126.7 3.9 %collective-permute-start.5 = (bf16[288,512]{1,0:T(8,128)(2,1)S(1)}, bf16[288,512]{1,0:T(8,128)(2,1)S(1)}, u32[]{:S(2)}, u32[]{:S(2)}) collective-permute-start(bf16[288,512]{1,0:T(8,128)(2,1)S(1)} %get-tuple-element.29), channel_id=1, source_target_pairs={{0,4},{1,5},{2,6},{3,7},{4,0},{5,1},{6,2},{7,3},{8,12},{9,13},{10,... | collective-permute-start | bytes 884744 | tf_op jit(solution)/shard_map/ppermute | solution.py:155
  130.6 2.8 %collective-permute-start.6 = (bf16[288,512]{1,0:T(8,128)(2,1)S(1)}, bf16[288,512]{1,0:T(8,128)(2,1)S(1)}, u32[]{:S(2)}, u32[]{:S(2)}) collective-permute-start(bf16[288,512]{1,0:T(8,128)(2,1)S(1)} %get-tuple-element.30), channel_id=1, source_target_pairs={{0,2},{1,3},{2,4},{3,5},{4,6},{5,7},{6,0},{7,1},{8,10},{9,11},{10,... | collective-permute-start | bytes 884744 | tf_op jit(solution)/shard_map/ppermute | solution.py:155
  133.4 4.4 %collective-permute-done.4.r1 = bf16[288,512]{1,0:T(8,128)(2,1)S(1)} collective-permute-done((bf16[288,512]{1,0:T(8,128)(2,1)S(1)}, bf16[288,512]{1,0:T(8,128)(2,1)S(1)}, u32[]{:S(2)}, u32[]{:S(2)}) %collective-permute-start.4) | collective-permute-done | bytes 294944 | tf_op jit(solution)/shard_map/ppermute | solution.py:155
  137.8 6.3 %collective-permute-done.6.r3 = bf16[288,512]{1,0:T(8,128)(2,1)S(1)} collective-permute-done((bf16[288,512]{1,0:T(8,128)(2,1)S(1)}, bf16[288,512]{1,0:T(8,128)(2,1)S(1)}, u32[]{:S(2)}, u32[]{:S(2)}) %collective-permute-start.6) | collective-permute-done | bytes 294944 | tf_op jit(solution)/shard_map/ppermute | solution.py:155
  144.3 4.1 %collective-permute-start.7 = (bf16[192,512]{1,0:T(8,128)(2,1)S(1)}, bf16[192,512]{1,0:T(8,128)(2,1)S(1)}, u32[]{:S(2)}, u32[]{:S(2)}) collective-permute-start(bf16[192,512]{1,0:T(8,128)(2,1)S(1)} %get-tuple-element.31.g0.gu_ref), channel_id=1, source_target_pairs={{0,2},{1,3},{2,4},{3,5},{4,6},{5,7},{6,0},{7,1},{8,10},{9,11},{10,... | collective-permute-start | bytes 589832 | tf_op jit(solution)/shard_map/ppermute | solution.py:155
  148.4 3.3 %collective-permute-start.8 = (bf16[192,512]{1,0:T(8,128)(2,1)S(1)}, bf16[192,512]{1,0:T(8,128)(2,1)S(1)}, u32[]{:S(2)}, u32[]{:S(2)}) collective-permute-start(bf16[192,512]{1,0:T(8,128)(2,1)S(1)} %get-tuple-element.31.g0.gu_ref), channel_id=1, source_target_pairs={{0,4},{1,5},{2,6},{3,7},{4,0},{5,1},{6,2},{7,3},{8,12},{9,13},{10,... | collective-permute-start | bytes 589832 | tf_op jit(solution)/shard_map/ppermute | solution.py:155
  151.7 2.9 %collective-permute-start.9 = (bf16[192,512]{1,0:T(8,128)(2,1)S(1)}, bf16[192,512]{1,0:T(8,128)(2,1)S(1)}, u32[]{:S(2)}, u32[]{:S(2)}) collective-permute-start(bf16[192,512]{1,0:T(8,128)(2,1)S(1)} %get-tuple-element.31.g0.gu_ref), channel_id=1, source_target_pairs={{0,6},{1,7},{2,0},{3,1},{4,2},{5,3},{6,4},{7,5},{8,14},{9,15},{10,... | collective-permute-start | bytes 589832 | tf_op jit(solution)/shard_map/ppermute | solution.py:155
  154.6 3.4 %collective-permute-done.8.g2 = bf16[192,512]{1,0:T(8,128)(2,1)S(1)} collective-permute-done((bf16[192,512]{1,0:T(8,128)(2,1)S(1)}, bf16[192,512]{1,0:T(8,128)(2,1)S(1)}, u32[]{:S(2)}, u32[]{:S(2)}) %collective-permute-start.8) | collective-permute-done | bytes 196640 | tf_op jit(solution)/shard_map/ppermute | solution.py:155
  158.1 2.3 %collective-permute-done.9.g3 = bf16[192,512]{1,0:T(8,128)(2,1)S(1)} collective-permute-done((bf16[192,512]{1,0:T(8,128)(2,1)S(1)}, bf16[192,512]{1,0:T(8,128)(2,1)S(1)}, u32[]{:S(2)}, u32[]{:S(2)}) %collective-permute-start.9) | collective-permute-done | bytes 196640 | tf_op jit(solution)/shard_map/ppermute | solution.py:155
  161.7 3.6 %collective-permute-start.10 = (bf16[512,512]{1,0:T(8,128)(2,1)S(1)}, bf16[512,512]{1,0:T(8,128)(2,1)S(1)}, u32[]{:S(2)}, u32[]{:S(2)}) collective-permute-start(bf16[512,512]{1,0:T(8,128)(2,1)S(1)} %get-tuple-element.33), channel_id=1, source_target_pairs={{0,1},{1,0},{2,3},{3,2},{4,5},{5,4},{6,7},{7,6},{8,9},{9,8},{10,11... | collective-permute-start | bytes 1572872 | tf_op jit(solution)/shard_map/ppermute | solution.py:158
  167.0 23.2 %all_to_all.11 = bf16[64,8,512]{2,1,0:T(8,128)(2,1)S(1)} all-to-all(bf16[64,8,512]{2,1,0:T(8,128)(2,1)S(1)} %fusion), channel_id=1, replica_groups=mesh['expert'=64,'tensor'=8] {'expert'}, dimensions={0} | all-to-all | bytes 1048576 | tf_op jit(solution)/shard_map/all_to_all | solution.py:191
  191.0 3.4 %copy-done.1 = bf16[8,512,1024]{2,1,0:T(8,128)(2,1)S(1)} copy-done((bf16[8,512,1024]{2,1,0:T(8,128)(2,1)S(1)}, bf16[8,512,1024]{2,1,0:T(8,128)(2,1)}, u32[]{:S(2)}) %copy-start.1) | copy-done | bytes 8388632
  194.4 4.3 %shard_map.107 = (bf16[96,4096]{1,0:T(8,128)(2,1)}, bf16[96,4096]{1,0:T(8,128)(2,1)}, bf16[96,4096]{1,0:T(8,128)(2,1)}) custom-call(bf16[192,512]{1,0:T(8,128)(2,1)S(1)} %get-tuple-element.31.g0.gu_ref, bf16[96,512]{1,0:T(8,128)(2,1)S(1)} %get-tuple-element.34.hidden_ref, bf16[8,512,1024]{2,1,0:T(8,128)(2,1)S(1)} %copy-done.1), custom_call_target="tpu_custom_call" | custom-call | flops 1200000000 | bytes 11534336 | tf_op jit(solution)/shard_map/pallas_call | solution.py:192
  (26 shorter events, 11.8 us)
Async XLA Ops:
  7.2 183.8 %all-gather.2.cloned.1.call-start = ((), (), s32[]{:S(2)}) async-start(), calls=%async_computation.2 | async-start | bytes 9437184 | tf_op jit(solution)/shard_map/all_gather | solution.py:173
  8.7 1.1 copy-start.2
  9.9 1.1 copy-start.3
  11.0 1.1 copy-start.4
  12.1 0.8 copy-start.5
  12.9 0.8 copy-start.6
  59.9 59.7 %collective-permute-start = (bf16[512,1024]{1,0:T(8,128)(2,1)}, bf16[512,1024]{1,0:T(8,128)(2,1)S(1)}, u32[]{:S(2)}, u32[]{:S(2)}) collective-permute-start(bf16[512,1024]{1,0:T(8,128)(2,1)} %bitcast.13), channel_id=1, source_target_pairs={{0,1},{1,0},{2,3},{3,2},{4,5},{5,4},{6,7},{7,6},{8,9},{9,8},{10,11... | collective-permute-start | bytes 3145736 | tf_op jit(solution)/shard_map/ppermute | solution.py:158
  65.1 24.3 %collective-permute-start.1 = (bf16[288,1024]{1,0:T(8,128)(2,1)S(1)}, bf16[288,1024]{1,0:T(8,128)(2,1)S(1)}, u32[]{:S(2)}, u32[]{:S(2)}) collective-permute-start(bf16[288,1024]{1,0:T(8,128)(2,1)S(1)} %get-tuple-element.24), channel_id=1, source_target_pairs={{0,2},{1,3},{2,4},{3,5},{4,6},{5,7},{6,0},{7,1},{8,10},{9,11},{10,... | collective-permute-start | bytes 1769480 | tf_op jit(solution)/shard_map/ppermute | solution.py:155
  68.3 48.0 %collective-permute-start.2 = (bf16[288,1024]{1,0:T(8,128)(2,1)S(1)}, bf16[288,1024]{1,0:T(8,128)(2,1)S(1)}, u32[]{:S(2)}, u32[]{:S(2)}) collective-permute-start(bf16[288,1024]{1,0:T(8,128)(2,1)S(1)} %get-tuple-element.25), channel_id=1, source_target_pairs={{0,4},{1,5},{2,6},{3,7},{4,0},{5,1},{6,2},{7,3},{8,12},{9,13},{10,... | collective-permute-start | bytes 1769480 | tf_op jit(solution)/shard_map/ppermute | solution.py:155
  72.6 47.0 %collective-permute-start.3 = (bf16[288,1024]{1,0:T(8,128)(2,1)S(1)}, bf16[288,1024]{1,0:T(8,128)(2,1)S(1)}, u32[]{:S(2)}, u32[]{:S(2)}) collective-permute-start(bf16[288,1024]{1,0:T(8,128)(2,1)S(1)} %get-tuple-element.26), channel_id=1, source_target_pairs={{0,6},{1,7},{2,0},{3,1},{4,2},{5,3},{6,4},{7,5},{8,14},{9,15},{10,... | collective-permute-start | bytes 1769480 | tf_op jit(solution)/shard_map/ppermute | solution.py:155
  119.6 1.2 copy-start
  123.7 14.1 %collective-permute-start.4 = (bf16[288,512]{1,0:T(8,128)(2,1)S(1)}, bf16[288,512]{1,0:T(8,128)(2,1)S(1)}, u32[]{:S(2)}, u32[]{:S(2)}) collective-permute-start(bf16[288,512]{1,0:T(8,128)(2,1)S(1)} %get-tuple-element.28), channel_id=1, source_target_pairs={{0,6},{1,7},{2,0},{3,1},{4,2},{5,3},{6,4},{7,5},{8,14},{9,15},{10,... | collective-permute-start | bytes 884744 | tf_op jit(solution)/shard_map/ppermute | solution.py:155
  126.7 11.1 %collective-permute-start.5 = (bf16[288,512]{1,0:T(8,128)(2,1)S(1)}, bf16[288,512]{1,0:T(8,128)(2,1)S(1)}, u32[]{:S(2)}, u32[]{:S(2)}) collective-permute-start(bf16[288,512]{1,0:T(8,128)(2,1)S(1)} %get-tuple-element.29), channel_id=1, source_target_pairs={{0,4},{1,5},{2,6},{3,7},{4,0},{5,1},{6,2},{7,3},{8,12},{9,13},{10,... | collective-permute-start | bytes 884744 | tf_op jit(solution)/shard_map/ppermute | solution.py:155
  130.6 13.5 %collective-permute-start.6 = (bf16[288,512]{1,0:T(8,128)(2,1)S(1)}, bf16[288,512]{1,0:T(8,128)(2,1)S(1)}, u32[]{:S(2)}, u32[]{:S(2)}) collective-permute-start(bf16[288,512]{1,0:T(8,128)(2,1)S(1)} %get-tuple-element.30), channel_id=1, source_target_pairs={{0,2},{1,3},{2,4},{3,5},{4,6},{5,7},{6,0},{7,1},{8,10},{9,11},{10,... | collective-permute-start | bytes 884744 | tf_op jit(solution)/shard_map/ppermute | solution.py:155
  144.3 10.3 %collective-permute-start.7 = (bf16[192,512]{1,0:T(8,128)(2,1)S(1)}, bf16[192,512]{1,0:T(8,128)(2,1)S(1)}, u32[]{:S(2)}, u32[]{:S(2)}) collective-permute-start(bf16[192,512]{1,0:T(8,128)(2,1)S(1)} %get-tuple-element.31.g0.gu_ref), channel_id=1, source_target_pairs={{0,2},{1,3},{2,4},{3,5},{4,6},{5,7},{6,0},{7,1},{8,10},{9,11},{10,... | collective-permute-start | bytes 589832 | tf_op jit(solution)/shard_map/ppermute | solution.py:155
  148.4 9.7 %collective-permute-start.8 = (bf16[192,512]{1,0:T(8,128)(2,1)S(1)}, bf16[192,512]{1,0:T(8,128)(2,1)S(1)}, u32[]{:S(2)}, u32[]{:S(2)}) collective-permute-start(bf16[192,512]{1,0:T(8,128)(2,1)S(1)} %get-tuple-element.31.g0.gu_ref), channel_id=1, source_target_pairs={{0,4},{1,5},{2,6},{3,7},{4,0},{5,1},{6,2},{7,3},{8,12},{9,13},{10,... | collective-permute-start | bytes 589832 | tf_op jit(solution)/shard_map/ppermute | solution.py:155
  151.7 8.7 %collective-permute-start.9 = (bf16[192,512]{1,0:T(8,128)(2,1)S(1)}, bf16[192,512]{1,0:T(8,128)(2,1)S(1)}, u32[]{:S(2)}, u32[]{:S(2)}) collective-permute-start(bf16[192,512]{1,0:T(8,128)(2,1)S(1)} %get-tuple-element.31.g0.gu_ref), channel_id=1, source_target_pairs={{0,6},{1,7},{2,0},{3,1},{4,2},{5,3},{6,4},{7,5},{8,14},{9,15},{10,... | collective-permute-start | bytes 589832 | tf_op jit(solution)/shard_map/ppermute | solution.py:155
  161.7 5.1 %collective-permute-start.10 = (bf16[512,512]{1,0:T(8,128)(2,1)S(1)}, bf16[512,512]{1,0:T(8,128)(2,1)S(1)}, u32[]{:S(2)}, u32[]{:S(2)}) collective-permute-start(bf16[512,512]{1,0:T(8,128)(2,1)S(1)} %get-tuple-element.33), channel_id=1, source_target_pairs={{0,1},{1,0},{2,3},{3,2},{4,5},{5,4},{6,7},{7,6},{8,9},{9,8},{10,11... | collective-permute-start | bytes 1572872 | tf_op jit(solution)/shard_map/ppermute | solution.py:158
  191.0 3.4 %copy-start.1 = (bf16[8,512,1024]{2,1,0:T(8,128)(2,1)S(1)}, bf16[8,512,1024]{2,1,0:T(8,128)(2,1)}, u32[]{:S(2)}) copy-start(bf16[8,512,1024]{2,1,0:T(8,128)(2,1)} %all-gather.2.cloned.1.call-done.rows_ref) | copy-start | bytes 25165828
Sparse Core Ops, SparseCore 0:
  60.0 77.3 all-gather.1

commit v2 on v1

--- a/solution.py
+++ b/solution.py
@@ -11,19 +11,11 @@
 F32, BF16 = jnp.float32, jnp.bfloat16
 VMEM = pl.BlockSpec(memory_space=pltpu.VMEM)
 ANY = pl.BlockSpec(memory_space=pl.ANY)
+HBM = pl.BlockSpec(memory_space=pltpu.HBM)
 
 
 def dot(a, b, ca, cb):
     return lax.dot_general(a, b, (((ca,), (cb,)), ((), ())), preferred_element_type=F32)
-
-
-def pieces(v):
-    out = []
-    for _ in range(3):
-        part = v.astype(BF16)
-        out.append(part)
-        v = v - part.astype(F32)
-    return out
 
 
 def dispatch_kernel(ids_ref, gate_ref, tok_ref, cot_ref, wg_ref, wu_ref, wd_ref,
@@ -43,36 +35,25 @@
     experts = slots // CAP
     ids = ids_ref[...]
     gates = gate_ref[...]
-    expert_iota = lax.broadcasted_iota(jnp.int32, (toks, experts), 1)
-    chosen = jnp.zeros((toks, experts), F32)
-    weight = jnp.zeros((toks, experts), F32)
+    expert_iota = lax.broadcasted_iota(jnp.int32, (experts, toks), 0)
+    chosen = jnp.zeros((experts, toks), F32)
+    weight = jnp.zeros((experts, toks), F32)
     for k in range(TOP):
-        hit = ids[:, k:k + 1] == expert_iota
-        chosen = chosen + hit.astype(F32)
-        weight = weight + jnp.where(hit, gates[:, k:k + 1], 0.0)
+        hit = ids[k:k + 1, :] == expert_iota
+        chosen = chosen + jnp.where(hit, 1.0, 0.0)
+        weight = weight + jnp.where(hit, gates[k:k + 1, :], 0.0)
     row = lax.broadcasted_iota(jnp.int32, (toks, toks), 0)
     col = lax.broadcasted_iota(jnp.int32, (toks, toks), 1)
-    earlier = (col < row).astype(F32).astype(BF16)
-    chosen_b = chosen.astype(BF16)
-    slot = dot(earlier, chosen_b, 1, 0)
-    spread = (lax.broadcasted_iota(jnp.int32, (experts, slots), 1) // CAP
-              == lax.broadcasted_iota(jnp.int32, (experts, slots), 0)).astype(F32).astype(BF16)
-    chosen_s = dot(chosen_b, spread, 1, 0)
-    slot_s = dot(slot.astype(BF16), spread, 1, 0)
-    capacity = (lax.broadcasted_iota(jnp.int32, (toks, slots), 1) % CAP).astype(F32)
-    place = jnp.where((chosen_s > 0.5) & (slot_s == capacity), 1.0, 0.0)
-    place_b = place.astype(BF16)
+    earlier = jnp.where(row < col, 1.0, 0.0).astype(BF16)
+    slot = dot(chosen.astype(BF16), earlier, 1, 0)
+    slot = jnp.where(chosen > 0.5, slot, -1.0)
+    capacity = lax.broadcasted_iota(jnp.int32, (experts, CAP, toks), 1).astype(F32)
+    place = jnp.where(slot[:, None, :] == capacity, 1.0, 0.0)
+    scale = jnp.sum((place * weight[:, None, :]).reshape(slots, toks), axis=1, keepdims=True)
+    place_b = place.reshape(slots, toks).astype(BF16)
     place_ref[...] = place_b
-    sent_ref[:, :width] = dot(place_b, tok_ref[...], 0, 0).astype(BF16)
-    ones = jnp.ones((toks, 128), BF16)
-    scale = jnp.zeros((slots, 128), F32)
-    for part in pieces(weight):
-        spread_part = dot(part, spread, 1, 0) * place
-        scale = scale + dot(spread_part.astype(BF16), ones, 0, 0)
-    rows_d = dot(place_b, cot_ref[...], 0, 0)
-    for j in range(width // 128):
-        sent_ref[:, width + j * 128:width + (j + 1) * 128] = (
-            scale * rows_d[:, j * 128:(j + 1) * 128]).astype(BF16)
+    sent_ref[:, :width] = dot(place_b, tok_ref[...], 1, 0).astype(BF16)
+    sent_ref[:, width:] = (scale * dot(place_b, cot_ref[...], 1, 0)).astype(BF16)
     for c in copies:
         c.wait()
 
@@ -127,7 +108,7 @@
 
 
 def combine_kernel(place_ref, arrived_ref, out_ref):
-    out_ref[...] = dot(place_ref[...], arrived_ref[...], 1, 0).astype(BF16)
+    out_ref[...] = dot(place_ref[...], arrived_ref[...], 0, 0).astype(BF16)
 
 
 def call(kernel, outs, n_in, scratch=(), in_specs=None, out_specs=None, flops=0, nbytes=0):
@@ -142,6 +123,10 @@
     )
 
 
+def in_hbm(v):
+    return pltpu.with_memory_space_constraint(v, pltpu.HBM)
+
+
 def on_device(tokens, cotangent, expert_ids, gate_values, w_gate, w_up, w_down):
     toks, width = tokens.shape
     hid, feats = w_gate.shape[1], w_gate.shape[2]
@@ -149,7 +134,7 @@
     n_tensor = lax.axis_size("tensor")
     slots = groups * CAP
     chip_feats = feats // X_CHIPS
-    w_gate, w_up, w_down = (w.reshape(hid, feats) for w in (w_gate, w_up, w_down))
+    w_gate, w_up, w_down = (in_hbm(w.reshape(hid, feats)) for w in (w_gate, w_up, w_down))
 
     def shift(v, s):
         return lax.ppermute(v, "tensor", [(i, (i + 2 * s) % n_tensor) for i in range(n_tensor)])
@@ -160,16 +145,18 @@
     message = ((3 * hid, chip_feats), BF16)
     sent, place, *blocks = call(
         dispatch_kernel,
-        [((slots, 2 * width), BF16), ((toks, slots), BF16)] + [message] * X_CHIPS,
+        [((slots, 2 * width), BF16), ((slots, toks), BF16)] + [message] * X_CHIPS,
         7,
         scratch=[pltpu.SemaphoreType.DMA((X_CHIPS, 3))],
-        in_specs=[VMEM] * 4 + [ANY] * 3,
+        in_specs=[VMEM] * 4 + [HBM] * 3,
         out_specs=[VMEM] * 2 + [ANY] * X_CHIPS,
         flops=10**8, nbytes=6 << 20,
-    )(expert_ids, gate_values, tokens, cotangent, w_gate, w_up, w_down)
+    )(in_hbm(expert_ids.T), in_hbm(gate_values.T), in_hbm(tokens), in_hbm(cotangent), w_gate, w_up, w_down)
     rows = lax.all_to_all(sent.reshape(groups, CAP, 2 * width), "expert", 0, 0, tiled=True)
-    rows = rows.reshape(slots, 2 * width)
-    weights = [blocks[0]] + [shift(blocks[s], s) for s in range(1, X_CHIPS)]
+    rows = in_hbm(rows.reshape(slots, 2 * width))
+    moved = {s: shift(blocks[s], s) for s in (2, 1, 3)}
+    rows, *weights = lax.optimization_barrier((rows, moved[1], moved[2], moved[3]))
+    weights = [blocks[0]] + weights
     every = lax.all_gather(rows, "tensor", axis=0)
     other = sibling(rows)
     parts = call(
@@ -201,7 +188,8 @@
         out_specs=[pl.BlockSpec((hid, width), lambda q: (0, q))] * 3,
         compiler_params=pltpu.CompilerParams(vmem_limit_bytes=40 << 20),
         cost_estimate=pl.CostEstimate(flops=12 * 10**8, bytes_accessed=11 << 20, transcendentals=0),
-    )(gate_up, hidden, every)
+    )(gate_up, hidden, in_hbm(every))
+    arrived, *grads = lax.optimization_barrier((arrived, *grads))
     (grad_tokens,) = call(
         combine_kernel, [((toks, width), BF16)], 2, flops=10**7, nbytes=1 << 20,
     )(place, arrived.reshape(slots, width))

time: 208 us -> 212 us (1.019)
  blocking collectives: 67.7 us -> 0 us
  Pallas kernels: 11.1 us -> 53.4 us
  starting transfers between devices: 39.4 us -> 67.7 us
  waiting for transfers between devices: 61.9 us -> 73.5 us
  local copies, waits for them, and re-layouts: 11.1 us -> 1 us
    all_to_all x2 -> x0, blocking collectives: 67.7 us -> none  [the longest x1 44.5 us: on_device(): lax.all_to_all(sent.reshape(groups, CAP, 2 * width), 'expert', 0, 0, tile...]
    pallas_call x1, Pallas kernels: 1.67 us -> 38.8 us  [on_device(): call(dispatch_kernel, [((slots, 2 * width), BF16), ((slots, toks), BF16)]...]
    all_to_all x0 -> x2, starting transfers between devices: none -> 29.4 us  [the longest x1 17.4 us: on_device(): lax.all_to_all(sent.reshape(groups, CAP, 2 * width), 'expert', 0, 0, tile...]
    unnamed x16 -> x2, local copies, waits for them, and re-layouts: 11.1 us -> 1 us
    all_to_all x0 -> x2, waiting for transfers between devices: none -> 9.7 us  [the longest x1 9.7 us: on_device(): lax.all_to_all(row_grad.reshape(groups, CAP, width), 'expert', 0, 0, tile...]
    pallas_call x1, Pallas kernels: 4.31 us -> 7.92 us  [on_device(): pl.pallas_call(grad_kernel, grid=(n_tensor,), out_shape=[jax.ShapeDtypeSt...]
    ppermute x2, waiting for transfers between devices: 1.52 us -> 3.99 us  [sibling(): return lax.ppermute(v, 'tensor', [(i, i ^ 1) for i in range(n_tensor)])]
  transfers between devices with their start and end apart: 12 -> 14, of which waited for: 8 -> 12; matrix products, arithmetic and copies ran while one was open for 0% -> 0% of each run, Pallas kernels for 2% -> 7%
where the time goes in v2:
time: 212 us; the launch traced here: 211 us
  waiting for transfers between devices  73.5 us (35%)
  starting transfers between devices  67.7 us (32%)
  Pallas kernels  53.4 us (25%)
  between operations  14.2 us (7%)
    ppermute x9, waiting for transfers between devices, shift(): lax.ppermute(v, 'tensor', [(i, (i + 2 * s) % n_tensor) for i in range(n_t...  59.7 us
    pallas_call x1, Pallas kernels, on_device(): call(dispatch_kernel, [((slots, 2 * width), BF16), ((slots, toks), BF16)]...  38.8 us
    ppermute x9, starting transfers between devices, shift(): lax.ppermute(v, 'tensor', [(i, (i + 2 * s) % n_tensor) for i in range(n_t...  30.6 us
    all_to_all x1, starting transfers between devices, on_device(): lax.all_to_all(sent.reshape(groups, CAP, 2 * width), 'expert', 0, 0, tile...  17.4 us
    all_to_all x1, starting transfers between devices, on_device(): lax.all_to_all(row_grad.reshape(groups, CAP, width), 'expert', 0, 0, tile...  12 us
    all_to_all x1, waiting for transfers between devices, on_device(): lax.all_to_all(row_grad.reshape(groups, CAP, width), 'expert', 0, 0, tile...  9.7 us
    pallas_call x1, Pallas kernels, on_device(): pl.pallas_call(grad_kernel, grid=(n_tensor,), out_shape=[jax.ShapeDtypeSt...  7.92 us
    ppermute x2, starting transfers between devices, sibling(): return lax.ppermute(v, 'tensor', [(i, i ^ 1) for i in range(n_tensor)])  7.68 us
  transfers between devices with their start and end apart: 14, of which 12 were waited for; matrix products, arithmetic and copies ran while one was open for 0% of the time, Pallas kernels for 7%

profile of v2, /device:TPU:1, one launch (start us, length us, event | category | flops | bytes accessed | tf_op | source)
XLA Modules:
  0.0 210.7 jit_solution(5755280841817100717)
XLA Ops:
  7.2 38.8 %shard_map.102 = (bf16[512,1024]{1,0:T(8,128)(2,1)}, bf16[512,48]{1,0:T(8,128)(2,1)S(1)}, bf16[288,1024]{1,0:T(8,128)(2,1)S(1)}, bf16[288,1024]{1,0:T(8,128)(2,1...) custom-call(s32[8,48]{1,0:T(8,128)} %bitcast.19, f32[8,48]{1,0:T(8,128)} %bitcast.20, ...), custom_call_target="tpu_custom_call" | custom-call | flops 100000000 | bytes 6291456 | tf_op jit(solution)/shard_map/pallas_call | solution.py:146
  46.0 17.4 %all-to-all-start = ((bf16[64,8,1024]{2,1,0:T(8,128)(2,1)}), bf16[64,8,1024]{2,1,0:T(8,128)(2,1)}, u32[]{:S(2)}, u32[]{:S(2)}) async-start(bf16[64,8,1024]{2,1,0:T(8,128)(2,1)} %bitcast.5), calls=%async_computation | async-start | bytes 2097152 | tf_op jit(solution)/shard_map/all_to_all | solution.py:155
  63.5 3.1 %collective-permute-start = (bf16[288,1024]{1,0:T(8,128)(2,1)}, bf16[288,1024]{1,0:T(8,128)(2,1)S(1)}, u32[]{:S(2)}, u32[]{:S(2)}) collective-permute-start(bf16[288,1024]{1,0:T(8,128)(2,1)} %get-tuple-element.31), channel_id=1, source_target_pairs={{0,2},{1,3},{2,4},{3,5},{4,6},{5,7},{6,0},{7,1},{8,10},{9,11},{10,... | collective-permute-start | bytes 1769480 | tf_op jit(solution)/shard_map/ppermute | solution.py:140
  66.6 4.4 %collective-permute-start.1 = (bf16[288,1024]{1,0:T(8,128)(2,1)}, bf16[288,1024]{1,0:T(8,128)(2,1)S(1)}, u32[]{:S(2)}, u32[]{:S(2)}) collective-permute-start(bf16[288,1024]{1,0:T(8,128)(2,1)} %get-tuple-element.32), channel_id=1, source_target_pairs={{0,4},{1,5},{2,6},{3,7},{4,0},{5,1},{6,2},{7,3},{8,12},{9,13},{10,... | collective-permute-start | bytes 1769480 | tf_op jit(solution)/shard_map/ppermute | solution.py:140
  70.9 3.1 %collective-permute-start.2 = (bf16[288,1024]{1,0:T(8,128)(2,1)S(1)}, bf16[288,1024]{1,0:T(8,128)(2,1)S(1)}, u32[]{:S(2)}, u32[]{:S(2)}) collective-permute-start(bf16[288,1024]{1,0:T(8,128)(2,1)S(1)} %get-tuple-element.33), channel_id=1, source_target_pairs={{0,6},{1,7},{2,0},{3,1},{4,2},{5,3},{6,4},{7,5},{8,14},{9,15},{10,... | collective-permute-start | bytes 1769480 | tf_op jit(solution)/shard_map/ppermute | solution.py:140
  74.0 6.7 %collective-permute-done.m1 = bf16[288,1024]{1,0:T(8,128)(2,1)S(1)} collective-permute-done((bf16[288,1024]{1,0:T(8,128)(2,1)}, bf16[288,1024]{1,0:T(8,128)(2,1)S(1)}, u32[]{:S(2)}, u32[]{:S(2)}) %collective-permute-start) | collective-permute-done | bytes 589856 | tf_op jit(solution)/shard_map/ppermute | solution.py:140
  80.7 13.5 %collective-permute-done.1.m2 = bf16[288,1024]{1,0:T(8,128)(2,1)S(1)} collective-permute-done((bf16[288,1024]{1,0:T(8,128)(2,1)}, bf16[288,1024]{1,0:T(8,128)(2,1)S(1)}, u32[]{:S(2)}, u32[]{:S(2)}) %collective-permute-start.1) | collective-permute-done | bytes 589856 | tf_op jit(solution)/shard_map/ppermute | solution.py:140
  96.2 3.5 %collective-permute-start.3 = (bf16[512,1024]{1,0:T(8,128)(2,1)}, bf16[512,1024]{1,0:T(8,128)(2,1)S(1)}, u32[]{:S(2)}, u32[]{:S(2)}) collective-permute-start(bf16[512,1024]{1,0:T(8,128)(2,1)} %bitcast.6.own_ref), channel_id=1, source_target_pairs={{0,1},{1,0},{2,3},{3,2},{4,5},{5,4},{6,7},{7,6},{8,9},{9,8},{10,11... | collective-permute-start | bytes 3145736 | tf_op jit(solution)/shard_map/ppermute | solution.py:143
  99.6 2.5 %collective-permute-done.3.oth_ref = bf16[512,1024]{1,0:T(8,128)(2,1)S(1)} collective-permute-done((bf16[512,1024]{1,0:T(8,128)(2,1)}, bf16[512,1024]{1,0:T(8,128)(2,1)S(1)}, u32[]{:S(2)}, u32[]{:S(2)}) %collective-permute-start.3) | collective-permute-done | bytes 1048608 | tf_op jit(solution)/shard_map/ppermute | solution.py:143
  103.1 4.3 %shard_map.103 = (f32[288,512]{1,0:T(8,128)S(1)}, bf16[288,512]{1,0:T(8,128)(2,1)S(1)}, bf16[288,512]{1,0:T(8,128)(2,1)S(1)}, bf16[288,512]{1,0:T(8,128)(2,1)S(1)}) custom-call(bf16[512,1024]{1,0:T(8,128)(2,1)} %bitcast.6.own_ref, bf16[512,1024]{1,0:T(8,128)(2,1)} %copy-done, bf16[288,1024]{1,0:T(8,128)(2,1)S(1)} %get-tuple-element.35.m0, ...), custom_call_target="tpu_custom_call" | custom-call | flops 1200000000 | bytes 6291456 | tf_op jit(solution)/shard_map/pallas_call | solution.py:162
  107.4 4.3 %collective-permute-start.4 = (bf16[288,512]{1,0:T(8,128)(2,1)S(1)}, bf16[288,512]{1,0:T(8,128)(2,1)S(1)}, u32[]{:S(2)}, u32[]{:S(2)}) collective-permute-start(bf16[288,512]{1,0:T(8,128)(2,1)S(1)} %get-tuple-element.40), channel_id=1, source_target_pairs={{0,6},{1,7},{2,0},{3,1},{4,2},{5,3},{6,4},{7,5},{8,14},{9,15},{10,... | collective-permute-start | bytes 884744 | tf_op jit(solution)/shard_map/ppermute | solution.py:140
  111.7 3.4 %collective-permute-start.5 = (bf16[288,512]{1,0:T(8,128)(2,1)S(1)}, bf16[288,512]{1,0:T(8,128)(2,1)S(1)}, u32[]{:S(2)}, u32[]{:S(2)}) collective-permute-start(bf16[288,512]{1,0:T(8,128)(2,1)S(1)} %get-tuple-element.41), channel_id=1, source_target_pairs={{0,4},{1,5},{2,6},{3,7},{4,0},{5,1},{6,2},{7,3},{8,12},{9,13},{10,... | collective-permute-start | bytes 884744 | tf_op jit(solution)/shard_map/ppermute | solution.py:140
  117.1 3.1 %collective-permute-done.4.r1 = bf16[288,512]{1,0:T(8,128)(2,1)S(1)} collective-permute-done((bf16[288,512]{1,0:T(8,128)(2,1)S(1)}, bf16[288,512]{1,0:T(8,128)(2,1)S(1)}, u32[]{:S(2)}, u32[]{:S(2)}) %collective-permute-start.4) | collective-permute-done | bytes 294944 | tf_op jit(solution)/shard_map/ppermute | solution.py:140
  120.2 9.8 %collective-permute-done.5.r2 = bf16[288,512]{1,0:T(8,128)(2,1)S(1)} collective-permute-done((bf16[288,512]{1,0:T(8,128)(2,1)S(1)}, bf16[288,512]{1,0:T(8,128)(2,1)S(1)}, u32[]{:S(2)}, u32[]{:S(2)}) %collective-permute-start.5) | collective-permute-done | bytes 294944 | tf_op jit(solution)/shard_map/ppermute | solution.py:140
  130.0 10.6 %collective-permute-done.6.r3 = bf16[288,512]{1,0:T(8,128)(2,1)S(1)} collective-permute-done((bf16[288,512]{1,0:T(8,128)(2,1)S(1)}, bf16[288,512]{1,0:T(8,128)(2,1)S(1)}, u32[]{:S(2)}, u32[]{:S(2)}) %collective-permute-start.6) | collective-permute-done | bytes 294944 | tf_op jit(solution)/shard_map/ppermute | solution.py:140
  140.8 4.2 %collective-permute-start.7 = (bf16[192,512]{1,0:T(8,128)(2,1)S(1)}, bf16[192,512]{1,0:T(8,128)(2,1)S(1)}, u32[]{:S(2)}, u32[]{:S(2)}) collective-permute-start(bf16[192,512]{1,0:T(8,128)(2,1)S(1)} %get-tuple-element.43.g0.gu_ref), channel_id=1, source_target_pairs={{0,2},{1,3},{2,4},{3,5},{4,6},{5,7},{6,0},{7,1},{8,10},{9,11},{10,... | collective-permute-start | bytes 589832 | tf_op jit(solution)/shard_map/ppermute | solution.py:140
  145.0 3.2 %collective-permute-start.8 = (bf16[192,512]{1,0:T(8,128)(2,1)S(1)}, bf16[192,512]{1,0:T(8,128)(2,1)S(1)}, u32[]{:S(2)}, u32[]{:S(2)}) collective-permute-start(bf16[192,512]{1,0:T(8,128)(2,1)S(1)} %get-tuple-element.43.g0.gu_ref), channel_id=1, source_target_pairs={{0,4},{1,5},{2,6},{3,7},{4,0},{5,1},{6,2},{7,3},{8,12},{9,13},{10,... | collective-permute-start | bytes 589832 | tf_op jit(solution)/shard_map/ppermute | solution.py:140
  148.2 3.0 %collective-permute-start.9 = (bf16[192,512]{1,0:T(8,128)(2,1)S(1)}, bf16[192,512]{1,0:T(8,128)(2,1)S(1)}, u32[]{:S(2)}, u32[]{:S(2)}) collective-permute-start(bf16[192,512]{1,0:T(8,128)(2,1)S(1)} %get-tuple-element.43.g0.gu_ref), channel_id=1, source_target_pairs={{0,6},{1,7},{2,0},{3,1},{4,2},{5,3},{6,4},{7,5},{8,14},{9,15},{10,... | collective-permute-start | bytes 589832 | tf_op jit(solution)/shard_map/ppermute | solution.py:140
  151.3 3.3 %collective-permute-done.7.g1 = bf16[192,512]{1,0:T(8,128)(2,1)S(1)} collective-permute-done((bf16[192,512]{1,0:T(8,128)(2,1)S(1)}, bf16[192,512]{1,0:T(8,128)(2,1)S(1)}, u32[]{:S(2)}, u32[]{:S(2)}) %collective-permute-start.7) | collective-permute-done | bytes 196640 | tf_op jit(solution)/shard_map/ppermute | solution.py:140
  154.5 9.3 %collective-permute-done.8.g2 = bf16[192,512]{1,0:T(8,128)(2,1)S(1)} collective-permute-done((bf16[192,512]{1,0:T(8,128)(2,1)S(1)}, bf16[192,512]{1,0:T(8,128)(2,1)S(1)}, u32[]{:S(2)}, u32[]{:S(2)}) %collective-permute-start.8) | collective-permute-done | bytes 196640 | tf_op jit(solution)/shard_map/ppermute | solution.py:140
  166.7 4.2 %collective-permute-start.10 = (bf16[512,512]{1,0:T(8,128)(2,1)S(1)}, bf16[512,512]{1,0:T(8,128)(2,1)S(1)}, u32[]{:S(2)}, u32[]{:S(2)}) collective-permute-start(bf16[512,512]{1,0:T(8,128)(2,1)S(1)} %get-tuple-element.45), channel_id=1, source_target_pairs={{0,1},{1,0},{2,3},{3,2},{4,5},{5,4},{6,7},{7,6},{8,9},{9,8},{10,11... | collective-permute-start | bytes 1572872 | tf_op jit(solution)/shard_map/ppermute | solution.py:143
  173.4 12.0 %all-to-all-start.1 = ((bf16[64,8,512]{2,1,0:T(8,128)(2,1)}), bf16[64,8,512]{2,1,0:T(8,128)(2,1)S(1)}, u32[]{:S(2)}, u32[]{:S(2)}) async-start(bf16[64,8,512]{2,1,0:T(8,128)(2,1)} %fusion), calls=%async_computation.1 | async-start | bytes 1048576 | tf_op jit(solution)/shard_map/all_to_all | solution.py:178
  185.4 7.9 %shard_map.106 = (bf16[96,4096]{1,0:T(8,128)(2,1)}, bf16[96,4096]{1,0:T(8,128)(2,1)}, bf16[96,4096]{1,0:T(8,128)(2,1)}) custom-call(bf16[192,512]{1,0:T(8,128)(2,1)S(1)} %get-tuple-element.43.g0.gu_ref, bf16[96,512]{1,0:T(8,128)(2,1)S(1)} %get-tuple-element.46.hidden_ref, bf16[8,512,1024]{2,1,0:T(8,128)(2,1)} %bitcast.15), custom_call_target="tpu_custom_call" | custom-call | flops 1200000000 | bytes 11534336 | tf_op jit(solution)/shard_map/pallas_call | solution.py:179
  193.3 9.7 %all-to-all-done.1 = bf16[64,8,512]{2,1,0:T(8,128)(2,1)S(1)} async-done(((bf16[64,8,512]{2,1,0:T(8,128)(2,1)}), bf16[64,8,512]{2,1,0:T(8,128)(2,1)S(1)}, u32[]{:S(2)}, u32[]{:S(2)}) %all-to-all-start.1) | async-done | bytes 524320 | tf_op jit(solution)/shard_map/all_to_all | solution.py:178
  (14 shorter events, 11.2 us)
Async XLA Ops:
  46.0 50.1 %all-to-all-start = ((bf16[64,8,1024]{2,1,0:T(8,128)(2,1)}), bf16[64,8,1024]{2,1,0:T(8,128)(2,1)}, u32[]{:S(2)}, u32[]{:S(2)}) async-start(bf16[64,8,1024]{2,1,0:T(8,128)(2,1)} %bitcast.5), calls=%async_computation | async-start | bytes 2097152 | tf_op jit(solution)/shard_map/all_to_all | solution.py:155
  63.4 122.0 %all-gather.3.cloned.1.call-start = ((), (), s32[]{:S(2)}) async-start(), calls=%async_computation.2 | async-start | bytes 9437184 | tf_op jit(solution)/shard_map/all_gather | solution.py:160
  63.5 17.3 %collective-permute-start = (bf16[288,1024]{1,0:T(8,128)(2,1)}, bf16[288,1024]{1,0:T(8,128)(2,1)S(1)}, u32[]{:S(2)}, u32[]{:S(2)}) collective-permute-start(bf16[288,1024]{1,0:T(8,128)(2,1)} %get-tuple-element.31), channel_id=1, source_target_pairs={{0,2},{1,3},{2,4},{3,5},{4,6},{5,7},{6,0},{7,1},{8,10},{9,11},{10,... | collective-permute-start | bytes 1769480 | tf_op jit(solution)/shard_map/ppermute | solution.py:140
  66.6 27.7 %collective-permute-start.1 = (bf16[288,1024]{1,0:T(8,128)(2,1)}, bf16[288,1024]{1,0:T(8,128)(2,1)S(1)}, u32[]{:S(2)}, u32[]{:S(2)}) collective-permute-start(bf16[288,1024]{1,0:T(8,128)(2,1)} %get-tuple-element.32), channel_id=1, source_target_pairs={{0,4},{1,5},{2,6},{3,7},{4,0},{5,1},{6,2},{7,3},{8,12},{9,13},{10,... | collective-permute-start | bytes 1769480 | tf_op jit(solution)/shard_map/ppermute | solution.py:140
  70.9 25.2 %collective-permute-start.2 = (bf16[288,1024]{1,0:T(8,128)(2,1)S(1)}, bf16[288,1024]{1,0:T(8,128)(2,1)S(1)}, u32[]{:S(2)}, u32[]{:S(2)}) collective-permute-start(bf16[288,1024]{1,0:T(8,128)(2,1)S(1)} %get-tuple-element.33), channel_id=1, source_target_pairs={{0,6},{1,7},{2,0},{3,1},{4,2},{5,3},{6,4},{7,5},{8,14},{9,15},{10,... | collective-permute-start | bytes 1769480 | tf_op jit(solution)/shard_map/ppermute | solution.py:140
  96.2 5.9 %collective-permute-start.3 = (bf16[512,1024]{1,0:T(8,128)(2,1)}, bf16[512,1024]{1,0:T(8,128)(2,1)S(1)}, u32[]{:S(2)}, u32[]{:S(2)}) collective-permute-start(bf16[512,1024]{1,0:T(8,128)(2,1)} %bitcast.6.own_ref), channel_id=1, source_target_pairs={{0,1},{1,0},{2,3},{3,2},{4,5},{5,4},{6,7},{7,6},{8,9},{9,8},{10,11... | collective-permute-start | bytes 3145736 | tf_op jit(solution)/shard_map/ppermute | solution.py:143
  102.1 1.0 copy-start
  107.4 12.7 %collective-permute-start.4 = (bf16[288,512]{1,0:T(8,128)(2,1)S(1)}, bf16[288,512]{1,0:T(8,128)(2,1)S(1)}, u32[]{:S(2)}, u32[]{:S(2)}) collective-permute-start(bf16[288,512]{1,0:T(8,128)(2,1)S(1)} %get-tuple-element.40), channel_id=1, source_target_pairs={{0,6},{1,7},{2,0},{3,1},{4,2},{5,3},{6,4},{7,5},{8,14},{9,15},{10,... | collective-permute-start | bytes 884744 | tf_op jit(solution)/shard_map/ppermute | solution.py:140
  111.7 18.3 %collective-permute-start.5 = (bf16[288,512]{1,0:T(8,128)(2,1)S(1)}, bf16[288,512]{1,0:T(8,128)(2,1)S(1)}, u32[]{:S(2)}, u32[]{:S(2)}) collective-permute-start(bf16[288,512]{1,0:T(8,128)(2,1)S(1)} %get-tuple-element.41), channel_id=1, source_target_pairs={{0,4},{1,5},{2,6},{3,7},{4,0},{5,1},{6,2},{7,3},{8,12},{9,13},{10,... | collective-permute-start | bytes 884744 | tf_op jit(solution)/shard_map/ppermute | solution.py:140
  115.1 25.4 %collective-permute-start.6 = (bf16[288,512]{1,0:T(8,128)(2,1)S(1)}, bf16[288,512]{1,0:T(8,128)(2,1)S(1)}, u32[]{:S(2)}, u32[]{:S(2)}) collective-permute-start(bf16[288,512]{1,0:T(8,128)(2,1)S(1)} %get-tuple-element.42), channel_id=1, source_target_pairs={{0,2},{1,3},{2,4},{3,5},{4,6},{5,7},{6,0},{7,1},{8,10},{9,11},{10,... | collective-permute-start | bytes 884744 | tf_op jit(solution)/shard_map/ppermute | solution.py:140
  140.8 13.7 %collective-permute-start.7 = (bf16[192,512]{1,0:T(8,128)(2,1)S(1)}, bf16[192,512]{1,0:T(8,128)(2,1)S(1)}, u32[]{:S(2)}, u32[]{:S(2)}) collective-permute-start(bf16[192,512]{1,0:T(8,128)(2,1)S(1)} %get-tuple-element.43.g0.gu_ref), channel_id=1, source_target_pairs={{0,2},{1,3},{2,4},{3,5},{4,6},{5,7},{6,0},{7,1},{8,10},{9,11},{10,... | collective-permute-start | bytes 589832 | tf_op jit(solution)/shard_map/ppermute | solution.py:140
  145.0 18.8 %collective-permute-start.8 = (bf16[192,512]{1,0:T(8,128)(2,1)S(1)}, bf16[192,512]{1,0:T(8,128)(2,1)S(1)}, u32[]{:S(2)}, u32[]{:S(2)}) collective-permute-start(bf16[192,512]{1,0:T(8,128)(2,1)S(1)} %get-tuple-element.43.g0.gu_ref), channel_id=1, source_target_pairs={{0,4},{1,5},{2,6},{3,7},{4,0},{5,1},{6,2},{7,3},{8,12},{9,13},{10,... | collective-permute-start | bytes 589832 | tf_op jit(solution)/shard_map/ppermute | solution.py:140
  148.2 17.1 %collective-permute-start.9 = (bf16[192,512]{1,0:T(8,128)(2,1)S(1)}, bf16[192,512]{1,0:T(8,128)(2,1)S(1)}, u32[]{:S(2)}, u32[]{:S(2)}) collective-permute-start(bf16[192,512]{1,0:T(8,128)(2,1)S(1)} %get-tuple-element.43.g0.gu_ref), channel_id=1, source_target_pairs={{0,6},{1,7},{2,0},{3,1},{4,2},{5,3},{6,4},{7,5},{8,14},{9,15},{10,... | collective-permute-start | bytes 589832 | tf_op jit(solution)/shard_map/ppermute | solution.py:140
  166.7 5.7 %collective-permute-start.10 = (bf16[512,512]{1,0:T(8,128)(2,1)S(1)}, bf16[512,512]{1,0:T(8,128)(2,1)S(1)}, u32[]{:S(2)}, u32[]{:S(2)}) collective-permute-start(bf16[512,512]{1,0:T(8,128)(2,1)S(1)} %get-tuple-element.45), channel_id=1, source_target_pairs={{0,1},{1,0},{2,3},{3,2},{4,5},{5,4},{6,7},{7,6},{8,9},{9,8},{10,11... | collective-permute-start | bytes 1572872 | tf_op jit(solution)/shard_map/ppermute | solution.py:143
  173.4 29.6 %all-to-all-start.1 = ((bf16[64,8,512]{2,1,0:T(8,128)(2,1)}), bf16[64,8,512]{2,1,0:T(8,128)(2,1)S(1)}, u32[]{:S(2)}, u32[]{:S(2)}) async-start(bf16[64,8,512]{2,1,0:T(8,128)(2,1)} %fusion), calls=%async_computation.1 | async-start | bytes 1048576 | tf_op jit(solution)/shard_map/all_to_all | solution.py:178
Sparse Core Ops, SparseCore 0:
  96.3 77.7 all-gather.2

commit v3 on v2

v3 whole, which is shorter than its diff:
```python
import jax
import jax.numpy as jnp
from jax import lax
from jax.experimental import pallas as pl
from jax.experimental.pallas import tpu as pltpu
from jax.sharding import PartitionSpec as P

TOP = 8
CAP = 8
X_CHIPS = 4
F32, BF16 = jnp.float32, jnp.bfloat16
VMEM = pl.BlockSpec(memory_space=pltpu.VMEM)
HBM = pl.BlockSpec(memory_space=pltpu.HBM)


def dot(a, b, ca, cb):
    return lax.dot_general(a, b, (((ca,), (cb,)), ((), ())), preferred_element_type=F32)


def halves(width):
    core = lax.rem(lax.axis_index("tensor"), 2)
    mine = pl.ds(pl.multiple_of(core * width, width), width)
    theirs = pl.ds(pl.multiple_of((1 - core) * width, width), width)
    return mine, theirs


def owner(s):
    return lax.rem(lax.axis_index("tensor") // 2 + X_CHIPS - s, X_CHIPS)


def dispatch_kernel(ids_ref, gate_ref, tok_ref, cot_ref, wg_ref, wu_ref, wd_ref,
                    sent_ref, place_ref, b0, b1, b2, b3, sems):
    hid = wg_ref.shape[0]
    feats = b0.shape[1]
    chip = lax.axis_index("tensor") // 2
    copies = []
    for s, block in enumerate((b0, b1, b2, b3)):
        start = pl.multiple_of(lax.rem(chip + s, X_CHIPS) * feats, feats)
        for j, w in enumerate((wg_ref, wu_ref, wd_ref)):
            copies.append(pltpu.make_async_copy(
                w.at[:, pl.ds(start, feats)], block.at[pl.ds(j * hid, hid), :], sems.at[s, j]))
            copies[-1].start()
    toks, width = tok_ref.shape
    slots = sent_ref.shape[0]
    experts = slots // CAP
    ids = ids_ref[...]
    gates = gate_ref[...]
    expert_iota = lax.broadcasted_iota(jnp.int32, (experts, toks), 0)
    chosen = jnp.zeros((experts, toks), F32)
    weight = jnp.zeros((experts, toks), F32)
    for k in range(TOP):
        hit = ids[k:k + 1, :] == expert_iota
        chosen = chosen + jnp.where(hit, 1.0, 0.0)
        weight = weight + jnp.where(hit, gates[k:k + 1, :], 0.0)
    row = lax.broadcasted_iota(jnp.int32, (toks, toks), 0)
    col = lax.broadcasted_iota(jnp.int32, (toks, toks), 1)
    earlier = jnp.where(row < col, 1.0, 0.0).astype(BF16)
    slot = dot(chosen.astype(BF16), earlier, 1, 0)
    slot = jnp.where(chosen > 0.5, slot, -1.0)
    capacity = lax.broadcasted_iota(jnp.int32, (experts, CAP, toks), 1).astype(F32)
    place = jnp.where(slot[:, None, :] == capacity, 1.0, 0.0)
    scale = jnp.sum((place * weight[:, None, :]).reshape(slots, toks), axis=1, keepdims=True)
    place_b = place.reshape(slots, toks).astype(BF16)
    place_ref[...] = place_b
    sent_ref[:, :width] = dot(place_b, tok_ref[...], 1, 0).astype(BF16)
    sent_ref[:, width:] = (scale * dot(place_b, cot_ref[...], 1, 0)).astype(BF16)
    for c in copies:
        c.wait()


def partial_kernel(own_ref, oth_ref, w0, w1, w2, w3, p_ref):
    width = own_ref.shape[1] // 2
    hid = w0.shape[0] // 3
    mine, theirs = halves(width)
    for s, w_ref in enumerate((w0, w1, w2, w3)):
        q = owner(s)
        gu = dot(w_ref[:2 * hid, mine], own_ref[:, :width], 1, 1)
        gu = gu + dot(w_ref[:2 * hid, theirs], oth_ref[:, :width], 1, 1)
        p_ref[q, :2 * hid, :] = gu.astype(BF16)
        dn = dot(w_ref[2 * hid:, mine], own_ref[:, width:], 1, 1)
        dn = dn + dot(w_ref[2 * hid:, theirs], oth_ref[:, width:], 1, 1)
        p_ref[q, 2 * hid:, :] = dn.astype(BF16)


def act_kernel(p_ref, out_ref):
    hid = p_ref.shape[1] // 3
    total = p_ref[0].astype(F32)
    for q in range(1, X_CHIPS):
        total = total + p_ref[q].astype(F32)
    gate_pre, up_pre, hidden_grad = total[:hid], total[hid:2 * hid], total[2 * hid:]
    sigmoid = jax.nn.sigmoid(gate_pre)
    active = gate_pre * sigmoid
    gate_grad = hidden_grad * up_pre * sigmoid * (1.0 + gate_pre * (1.0 - sigmoid))
    for q in range(X_CHIPS):
        out_ref[q, :hid, :] = gate_grad.astype(BF16)
        out_ref[q, hid:2 * hid, :] = (hidden_grad * active).astype(BF16)
        out_ref[q, 2 * hid:, :] = (active * up_pre).astype(BF16)


def row_kernel(g_ref, w0, w1, w2, w3, keep_ref, send_ref):
    width = keep_ref.shape[1]
    two = 2 * (g_ref.shape[1] // 3)
    mine, theirs = halves(width)
    for part, out in ((theirs, send_ref), (mine, keep_ref)):
        total = None
        for s, w_ref in enumerate((w0, w1, w2, w3)):
            term = dot(g_ref[owner(s), :two, :], w_ref[:two, part], 0, 0)
            total = term if total is None else total + term
        out[...] = total.astype(out.dtype)


def grad_kernel(g_ref, own_ref, oth_ref, o0, o1, o2, o3):
    width = own_ref.shape[1] // 2
    two = 2 * (g_ref.shape[1] // 3)
    mine, theirs = halves(width)
    for s, out_ref in enumerate((o0, o1, o2, o3)):
        q = owner(s)
        for cols, rows in ((mine, own_ref), (theirs, oth_ref)):
            out_ref[:two, cols] = dot(g_ref[q, :two, :], rows[:, :width], 1, 0).astype(BF16)
            out_ref[two:, cols] = dot(g_ref[q, two:, :], rows[:, width:], 1, 0).astype(BF16)


def assemble_kernel(b0, b1, b2, b3, gg_ref, gu_ref, gd_ref):
    hid = gg_ref.shape[0]
    feats = b0.shape[1]
    chip = lax.axis_index("tensor") // 2
    for s, b in enumerate((b0, b1, b2, b3)):
        cols = pl.ds(pl.multiple_of(lax.rem(chip + s, X_CHIPS) * feats, feats), feats)
        gg_ref[:, cols] = b[:hid, :]
        gu_ref[:, cols] = b[hid:2 * hid, :]
        gd_ref[:, cols] = b[2 * hid:, :]


def combine_kernel(place_ref, arrived_ref, out_ref):
    out_ref[...] = dot(place_ref[...], arrived_ref[...], 0, 0).astype(BF16)


def call(kernel, outs, n_in, scratch=(), in_specs=None, flops=0, nbytes=0):
    return pl.pallas_call(
        kernel,
        out_shape=[jax.ShapeDtypeStruct(s, d) for s, d in outs],
        in_specs=in_specs or [VMEM] * n_in,
        out_specs=[VMEM] * len(outs),
        scratch_shapes=list(scratch),
        compiler_params=pltpu.CompilerParams(vmem_limit_bytes=16 << 20),
        cost_estimate=pl.CostEstimate(flops=flops, bytes_accessed=nbytes, transcendentals=0),
    )


def in_hbm(v):
    return pltpu.with_memory_space_constraint(v, pltpu.HBM)


def on_device(tokens, cotangent, expert_ids, gate_values, w_gate, w_up, w_down):
    toks, width = tokens.shape
    hid, feats = w_gate.shape[1], w_gate.shape[2]
    groups = lax.axis_size("expert")
    n_tensor = lax.axis_size("tensor")
    slots = groups * CAP
    chip_feats = feats // X_CHIPS
    w_gate, w_up, w_down = (in_hbm(w.reshape(hid, feats)) for w in (w_gate, w_up, w_down))
    same_core = [[i for i in range(n_tensor) if i % 2 == c] for c in range(2)]

    def over_x(v):
        return lax.all_to_all(v, "tensor", 0, 0, axis_index_groups=same_core, tiled=True)

    def shift(v, s):
        return lax.ppermute(v, "tensor", [(i, (i + 2 * s) % n_tensor) for i in range(n_tensor)])

    def sibling(v):
        return lax.ppermute(v, "tensor", [(i, i ^ 1) for i in range(n_tensor)])

    wide = (3 * hid, chip_feats)
    sent, place, *blocks = call(
        dispatch_kernel,
        [((slots, 2 * width), BF16), ((slots, toks), BF16)] + [(wide, BF16)] * X_CHIPS,
        7,
        scratch=[pltpu.SemaphoreType.DMA((X_CHIPS, 3))],
        in_specs=[VMEM] * 4 + [HBM] * 3,
        flops=10**8, nbytes=6 << 20,
    )(in_hbm(expert_ids.T), in_hbm(gate_values.T), in_hbm(tokens), in_hbm(cotangent), w_gate, w_up, w_down)
    rows = lax.all_to_all(sent.reshape(groups, CAP, 2 * width), "expert", 0, 0, tiled=True)
    rows = rows.reshape(slots, 2 * width)
    got = {s: shift(blocks[s], s) for s in (2, 1, 3)}
    rows, *weights = lax.optimization_barrier((rows, got[1], got[2], got[3]))
    weights = [blocks[0]] + weights
    other = sibling(rows)
    (parts,) = call(partial_kernel, [((X_CHIPS, 3 * hid, slots), BF16)], 6, flops=12 * 10**8, nbytes=6 << 20)(rows, other, *weights)
    (acts,) = call(act_kernel, [((X_CHIPS, 3 * hid, slots), BF16)], 1, flops=10**7, nbytes=2 << 20)(over_x(parts))
    gathered = (over_x(acts),)
    keep, send = call(
        row_kernel, [((slots, width), F32), ((slots, width), BF16)], 5,
        flops=8 * 10**8, nbytes=5 << 20,
    )(*gathered, *weights)
    grads = call(grad_kernel, [(wide, BF16)] * X_CHIPS, 3, flops=12 * 10**8, nbytes=6 << 20)(*gathered, rows, other)
    row_grad = (keep + sibling(send).astype(F32)).astype(BF16)
    arrived = lax.all_to_all(row_grad.reshape(groups, CAP, width), "expert", 0, 0, tiled=True)
    got = {s: shift(grads[s], -s) for s in (2, 1, 3)}
    outs = call(assemble_kernel, [((hid, feats), BF16)] * 3, 4, nbytes=5 << 20)(grads[0], got[1], got[2], got[3])
    (grad_tokens,) = call(
        combine_kernel, [((toks, width), BF16)], 2, flops=10**7, nbytes=1 << 20,
    )(place, arrived.reshape(slots, width))
    return (grad_tokens, *(g.reshape(1, hid, feats) for g in outs))


def solution(mesh):
    return jax.shard_map(
        on_device,
        mesh=mesh,
        in_specs=(
            P("expert", "tensor"),
            P("expert", "tensor"),
            P("expert", None),
            P("expert", None),
            P("expert", "tensor", None),
            P("expert", "tensor", None),
            P("expert", "tensor", None),
        ),
        out_specs=(
            P("expert", "tensor"),
            P("expert", "tensor", None),
            P("expert", "tensor", None),
            P("expert", "tensor", None),
        ),
        check_vma=False,
    )
```

time: 212 us -> 162 us (0.76)
  Pallas kernels: 53.4 us -> 12.8 us
  blocking collectives: 0 us -> 36.8 us
  waiting for transfers between devices: 73.5 us -> 52.2 us
  between operations: 14.2 us -> 0.82 us
  starting transfers between devices: 67.7 us -> 55.6 us
    all_to_all x0 -> x2, blocking collectives: none -> 36.8 us  [over_x(): lax.all_to_all(v, 'tensor', 0, 0, axis_index_groups=same_core, tiled=True)]
    pallas_call x1, Pallas kernels: 38.8 us -> 4.29 us  [on_device(): call(dispatch_kernel, [((slots, 2 * width), BF16), ((slots, toks), BF16)]...]
    ppermute x9 -> x6, starting transfers between devices: 30.6 us -> 18.3 us  [shift(): lax.ppermute(v, 'tensor', [(i, (i + 2 * s) % n_tensor) for i in range(n_t...]
    ppermute x9 -> x6, waiting for transfers between devices: 59.7 us -> 48.5 us  [shift(): lax.ppermute(v, 'tensor', [(i, (i + 2 * s) % n_tensor) for i in range(n_t...]
    all_to_all x1, waiting for transfers between devices: 9.7 us -> 0.01 us  [on_device(): lax.all_to_all(row_grad.reshape(groups, CAP, width), 'expert', 0, 0, tile...]
    pallas_call x4 -> x5, Pallas kernels: 13.8 us -> 7.62 us  [the longest x1 2.79 us: on_device(): call(partial_kernel, [((X_CHIPS, 3 * hid, slots), BF16)], 6, flops=12 * 1...]
  transfers between devices with their start and end apart: 14 -> 10, of which waited for: 12 -> 8; matrix products, arithmetic and copies ran while one was open for 0% -> 0% of each run, Pallas kernels for 7% -> 2%
where the time goes in v3:
time: 162 us; the launch traced here: 161 us
  starting transfers between devices  55.6 us (34%)
  waiting for transfers between devices  52.2 us (32%)
  blocking collectives  36.8 us (23%)
  Pallas kernels  12.8 us (8%)
  local copies, waits for them, and re-layouts  2.24 us (1%)
    ppermute x6, waiting for transfers between devices, shift(): lax.ppermute(v, 'tensor', [(i, (i + 2 * s) % n_tensor) for i in range(n_t...  48.5 us
    all_to_all x2, blocking collectives, over_x(): lax.all_to_all(v, 'tensor', 0, 0, axis_index_groups=same_core, tiled=True)  36.8 us
    ppermute x6, starting transfers between devices, shift(): lax.ppermute(v, 'tensor', [(i, (i + 2 * s) % n_tensor) for i in range(n_t...  18.3 us
    all_to_all x1, starting transfers between devices, on_device(): lax.all_to_all(sent.reshape(groups, CAP, 2 * width), 'expert', 0, 0, tile...  17.1 us
    all_to_all x1, starting transfers between devices, on_device(): lax.all_to_all(row_grad.reshape(groups, CAP, width), 'expert', 0, 0, tile...  12.1 us
    ppermute x2, starting transfers between devices, sibling(): return lax.ppermute(v, 'tensor', [(i, i ^ 1) for i in range(n_tensor)])  7.96 us
    pallas_call x1, Pallas kernels, on_device(): call(dispatch_kernel, [((slots, 2 * width), BF16), ((slots, toks), BF16)]...  4.29 us
    ppermute x2, waiting for transfers between devices, sibling(): return lax.ppermute(v, 'tensor', [(i, i ^ 1) for i in range(n_tensor)])  3.78 us
  transfers between devices with their start and end apart: 10, of which 8 were waited for; matrix products, arithmetic and copies ran while one was open for 0% of the time, Pallas kernels for 2%

profile of v3, /device:TPU:1, one launch (start us, length us, event | category | flops | bytes accessed | tf_op | source)
XLA Modules:
  0.0 161.4 jit_solution(11228622631922052564)
XLA Ops:
  0.6 4.3 %shard_map.102 = (bf16[512,1024]{1,0:T(8,128)(2,1)}, bf16[512,48]{1,0:T(8,128)(2,1)S(1)}, bf16[288,1024]{1,0:T(8,128)(2,1)S(1)}, bf16[288,1024]{1,0:T(8,128)(2,1...) custom-call(s32[8,48]{1,0:T(8,128)} %bitcast.20, f32[8,48]{1,0:T(8,128)} %bitcast.21, ...), custom_call_target="tpu_custom_call" | custom-call | flops 100000000 | bytes 6291456 | tf_op jit(solution)/shard_map/pallas_call | solution.py:174
  4.9 17.1 %all-to-all-start = ((bf16[64,8,1024]{2,1,0:T(8,128)(2,1)}), bf16[64,8,1024]{2,1,0:T(8,128)(2,1)S(1)}, u32[]{:S(2)}, u32[]{:S(2)}) async-start(bf16[64,8,1024]{2,1,0:T(8,128)(2,1)} %bitcast.5), calls=%async_computation | async-start | bytes 2097152 | tf_op jit(solution)/shard_map/all_to_all | solution.py:182
  22.1 3.1 %collective-permute-start = (bf16[288,1024]{1,0:T(8,128)(2,1)}, bf16[288,1024]{1,0:T(8,128)(2,1)S(1)}, u32[]{:S(2)}, u32[]{:S(2)}) collective-permute-start(bf16[288,1024]{1,0:T(8,128)(2,1)} %get-tuple-element.25), channel_id=1, source_target_pairs={{0,2},{1,3},{2,4},{3,5},{4,6},{5,7},{6,0},{7,1},{8,10},{9,11},{10,... | collective-permute-start | bytes 1769480 | tf_op jit(solution)/shard_map/ppermute | solution.py:168
  25.2 4.4 %collective-permute-start.1 = (bf16[288,1024]{1,0:T(8,128)(2,1)}, bf16[288,1024]{1,0:T(8,128)(2,1)S(1)}, u32[]{:S(2)}, u32[]{:S(2)}) collective-permute-start(bf16[288,1024]{1,0:T(8,128)(2,1)} %get-tuple-element.26), channel_id=1, source_target_pairs={{0,4},{1,5},{2,6},{3,7},{4,0},{5,1},{6,2},{7,3},{8,12},{9,13},{10,... | collective-permute-start | bytes 1769480 | tf_op jit(solution)/shard_map/ppermute | solution.py:168
  29.6 3.1 %collective-permute-start.2 = (bf16[288,1024]{1,0:T(8,128)(2,1)}, bf16[288,1024]{1,0:T(8,128)(2,1)S(1)}, u32[]{:S(2)}, u32[]{:S(2)}) collective-permute-start(bf16[288,1024]{1,0:T(8,128)(2,1)} %copy-done.6), channel_id=1, source_target_pairs={{0,6},{1,7},{2,0},{3,1},{4,2},{5,3},{6,4},{7,5},{8,14},{9,15},{10,... | collective-permute-start | bytes 1769480 | tf_op jit(solution)/shard_map/ppermute | solution.py:168
  32.7 6.6 %collective-permute-done.w1 = bf16[288,1024]{1,0:T(8,128)(2,1)S(1)} collective-permute-done((bf16[288,1024]{1,0:T(8,128)(2,1)}, bf16[288,1024]{1,0:T(8,128)(2,1)S(1)}, u32[]{:S(2)}, u32[]{:S(2)}) %collective-permute-start) | collective-permute-done | bytes 589856 | tf_op jit(solution)/shard_map/ppermute | solution.py:168
  39.3 13.6 %collective-permute-done.1.w2 = bf16[288,1024]{1,0:T(8,128)(2,1)S(1)} collective-permute-done((bf16[288,1024]{1,0:T(8,128)(2,1)}, bf16[288,1024]{1,0:T(8,128)(2,1)S(1)}, u32[]{:S(2)}, u32[]{:S(2)}) %collective-permute-start.1) | collective-permute-done | bytes 589856 | tf_op jit(solution)/shard_map/ppermute | solution.py:168
  52.9 2.0 %collective-permute-done.2.w3 = bf16[288,1024]{1,0:T(8,128)(2,1)S(1)} collective-permute-done((bf16[288,1024]{1,0:T(8,128)(2,1)}, bf16[288,1024]{1,0:T(8,128)(2,1)S(1)}, u32[]{:S(2)}, u32[]{:S(2)}) %collective-permute-start.2) | collective-permute-done | bytes 589856 | tf_op jit(solution)/shard_map/ppermute | solution.py:168
  54.9 3.3 %collective-permute-start.3 = (bf16[512,1024]{1,0:T(8,128)(2,1)S(1)}, bf16[512,1024]{1,0:T(8,128)(2,1)S(1)}, u32[]{:S(2)}, u32[]{:S(2)}) collective-permute-start(bf16[512,1024]{1,0:T(8,128)(2,1)S(1)} %bitcast.13), channel_id=1, source_target_pairs={{0,1},{1,0},{2,3},{3,2},{4,5},{5,4},{6,7},{7,6},{8,9},{9,8},{10,11... | collective-permute-start | bytes 3145736 | tf_op jit(solution)/shard_map/ppermute | solution.py:171
  58.3 2.3 %collective-permute-done.3.oth_ref = bf16[512,1024]{1,0:T(8,128)(2,1)S(1)} collective-permute-done((bf16[512,1024]{1,0:T(8,128)(2,1)S(1)}, bf16[512,1024]{1,0:T(8,128)(2,1)S(1)}, u32[]{:S(2)}, u32[]{:S(2)}) %collective-permute-start.3) | collective-permute-done | bytes 1048608 | tf_op jit(solution)/shard_map/ppermute | solution.py:171
  60.5 2.8 %shard_map.103 = bf16[4,288,512]{2,1,0:T(8,128)(2,1)S(1)} custom-call(bf16[512,1024]{1,0:T(8,128)(2,1)S(1)} %bitcast.14, bf16[512,1024]{1,0:T(8,128)(2,1)S(1)} %collective-permute-done.3.oth_ref, bf16[288,1024]{1,0:T(8,128)(2,1)S(1)} %get-tuple-element.29.w0, bf16[288,1024]{1,0:T(8,128)(2,1)S(1)} %collective-permute-done.w1, ...), custom_call_target="tpu_custom_call" | custom-call | flops 1200000000 | bytes 6291456 | tf_op jit(solution)/shard_map/pallas_call | solution.py:188
  64.3 19.5 %all_to_all.20.p_ref = bf16[4,288,512]{2,1,0:T(8,128)(2,1)S(1)} all-to-all(bf16[4,288,512]{2,1,0:T(8,128)(2,1)S(1)} %shard_map.103), channel_id=1, replica_groups={{0,2,4,6},{1,3,5,7},{8,10,12,14},{9,11,13,15},{16,18,20,22},{17,19,21,2..., dimensions={0} | all-to-all | bytes 2359296 | tf_op jit(solution)/shard_map/all_to_all | solution.py:165
  84.1 17.3 %all_to_all.21.g_ref = bf16[4,288,512]{2,1,0:T(8,128)(2,1)S(1)} all-to-all(bf16[4,288,512]{2,1,0:T(8,128)(2,1)S(1)} %shard_map.104), channel_id=1, replica_groups={{0,2,4,6},{1,3,5,7},{8,10,12,14},{9,11,13,15},{16,18,20,22},{17,19,21,2..., dimensions={0} | all-to-all | bytes 2359296 | tf_op jit(solution)/shard_map/all_to_all | solution.py:165
  102.7 4.6 %collective-permute-start.4 = (bf16[512,512]{1,0:T(8,128)(2,1)S(1)}, bf16[512,512]{1,0:T(8,128)(2,1)S(1)}, u32[]{:S(2)}, u32[]{:S(2)}) collective-permute-start(bf16[512,512]{1,0:T(8,128)(2,1)S(1)} %get-tuple-element.34), channel_id=1, source_target_pairs={{0,1},{1,0},{2,3},{3,2},{4,5},{5,4},{6,7},{7,6},{8,9},{9,8},{10,11... | collective-permute-start | bytes 1572872 | tf_op jit(solution)/shard_map/ppermute | solution.py:171
  107.3 1.5 collective-permute-done.4
  109.8 12.1 %all-to-all-start.3 = ((bf16[64,8,512]{2,1,0:T(8,128)(2,1)}), bf16[64,8,512]{2,1,0:T(8,128)(2,1)S(1)}, u32[]{:S(2)}, u32[]{:S(2)}) async-start(bf16[64,8,512]{2,1,0:T(8,128)(2,1)} %fusion), calls=%async_computation.3 | async-start | bytes 1048576 | tf_op jit(solution)/shard_map/all_to_all | solution.py:197
  123.2 1.7 %shard_map.107 = (bf16[288,1024]{1,0:T(8,128)(2,1)S(1)}, bf16[288,1024]{1,0:T(8,128)(2,1)S(1)}, bf16[288,1024]{1,0:T(8,128)(2,1)S(1)}, bf16[288,1024]{1,0:T(8,128)(2,1)S(1)}) custom-call(bf16[4,288,512]{2,1,0:T(8,128)(2,1)S(1)} %all_to_all.21.g_ref, bf16[512,1024]{1,0:T(8,128)(2,1)S(1)} %bitcast.15, bf16[512,1024]{1,0:T(8,128)(2,1)S(1)} %copy-done.5), custom_call_target="tpu_custom_call" | custom-call | flops 1200000000 | bytes 6291456 | tf_op jit(solution)/shard_map/pallas_call | solution.py:195
  124.9 2.8 %collective-permute-start.5 = (bf16[288,1024]{1,0:T(8,128)(2,1)S(1)}, bf16[288,1024]{1,0:T(8,128)(2,1)S(1)}, u32[]{:S(2)}, u32[]{:S(2)}) collective-permute-start(bf16[288,1024]{1,0:T(8,128)(2,1)S(1)} %get-tuple-element.36), channel_id=1, source_target_pairs={{0,6},{1,7},{2,0},{3,1},{4,2},{5,3},{6,4},{7,5},{8,14},{9,15},{10,... | collective-permute-start | bytes 1769480 | tf_op jit(solution)/shard_map/ppermute | solution.py:168
  127.7 3.1 %collective-permute-start.6 = (bf16[288,1024]{1,0:T(8,128)(2,1)S(1)}, bf16[288,1024]{1,0:T(8,128)(2,1)S(1)}, u32[]{:S(2)}, u32[]{:S(2)}) collective-permute-start(bf16[288,1024]{1,0:T(8,128)(2,1)S(1)} %get-tuple-element.37), channel_id=1, source_target_pairs={{0,4},{1,5},{2,6},{3,7},{4,0},{5,1},{6,2},{7,3},{8,12},{9,13},{10,... | collective-permute-start | bytes 1769480 | tf_op jit(solution)/shard_map/ppermute | solution.py:168
  130.8 1.9 %collective-permute-start.7 = (bf16[288,1024]{1,0:T(8,128)(2,1)S(1)}, bf16[288,1024]{1,0:T(8,128)(2,1)S(1)}, u32[]{:S(2)}, u32[]{:S(2)}) collective-permute-start(bf16[288,1024]{1,0:T(8,128)(2,1)S(1)} %get-tuple-element.38), channel_id=1, source_target_pairs={{0,2},{1,3},{2,4},{3,5},{4,6},{5,7},{6,0},{7,1},{8,10},{9,11},{10,... | collective-permute-start | bytes 1769480 | tf_op jit(solution)/shard_map/ppermute | solution.py:168
  132.7 8.3 %collective-permute-done.5.b1 = bf16[288,1024]{1,0:T(8,128)(2,1)S(1)} collective-permute-done((bf16[288,1024]{1,0:T(8,128)(2,1)S(1)}, bf16[288,1024]{1,0:T(8,128)(2,1)S(1)}, u32[]{:S(2)}, u32[]{:S(2)}) %collective-permute-start.5) | collective-permute-done | bytes 589856 | tf_op jit(solution)/shard_map/ppermute | solution.py:168
  141.0 4.0 %collective-permute-done.6.b2 = bf16[288,1024]{1,0:T(8,128)(2,1)S(1)} collective-permute-done((bf16[288,1024]{1,0:T(8,128)(2,1)S(1)}, bf16[288,1024]{1,0:T(8,128)(2,1)S(1)}, u32[]{:S(2)}, u32[]{:S(2)}) %collective-permute-start.6) | collective-permute-done | bytes 589856 | tf_op jit(solution)/shard_map/ppermute | solution.py:168
  145.0 14.0 %collective-permute-done.7.b3 = bf16[288,1024]{1,0:T(8,128)(2,1)S(1)} collective-permute-done((bf16[288,1024]{1,0:T(8,128)(2,1)S(1)}, bf16[288,1024]{1,0:T(8,128)(2,1)S(1)}, u32[]{:S(2)}, u32[]{:S(2)}) %collective-permute-start.7) | collective-permute-done | bytes 589856 | tf_op jit(solution)/shard_map/ppermute | solution.py:168
  159.0 1.6 shard_map.108
  (20 shorter events, 5.6 us)
Async XLA Ops:
  4.9 17.2 %copy-start.6 = (bf16[288,1024]{1,0:T(8,128)(2,1)}, bf16[288,1024]{1,0:T(8,128)(2,1)S(1)}, u32[]{:S(2)}) copy-start(bf16[288,1024]{1,0:T(8,128)(2,1)S(1)} %get-tuple-element.27) | copy-start | bytes 1769476
  4.9 50.0 %all-to-all-start = ((bf16[64,8,1024]{2,1,0:T(8,128)(2,1)}), bf16[64,8,1024]{2,1,0:T(8,128)(2,1)S(1)}, u32[]{:S(2)}, u32[]{:S(2)}) async-start(bf16[64,8,1024]{2,1,0:T(8,128)(2,1)} %bitcast.5), calls=%async_computation | async-start | bytes 2097152 | tf_op jit(solution)/shard_map/all_to_all | solution.py:182
  22.1 17.2 %collective-permute-start = (bf16[288,1024]{1,0:T(8,128)(2,1)}, bf16[288,1024]{1,0:T(8,128)(2,1)S(1)}, u32[]{:S(2)}, u32[]{:S(2)}) collective-permute-start(bf16[288,1024]{1,0:T(8,128)(2,1)} %get-tuple-element.25), channel_id=1, source_target_pairs={{0,2},{1,3},{2,4},{3,5},{4,6},{5,7},{6,0},{7,1},{8,10},{9,11},{10,... | collective-permute-start | bytes 1769480 | tf_op jit(solution)/shard_map/ppermute | solution.py:168
  25.2 27.7 %collective-permute-start.1 = (bf16[288,1024]{1,0:T(8,128)(2,1)}, bf16[288,1024]{1,0:T(8,128)(2,1)S(1)}, u32[]{:S(2)}, u32[]{:S(2)}) collective-permute-start(bf16[288,1024]{1,0:T(8,128)(2,1)} %get-tuple-element.26), channel_id=1, source_target_pairs={{0,4},{1,5},{2,6},{3,7},{4,0},{5,1},{6,2},{7,3},{8,12},{9,13},{10,... | collective-permute-start | bytes 1769480 | tf_op jit(solution)/shard_map/ppermute | solution.py:168
  29.6 25.3 %collective-permute-start.2 = (bf16[288,1024]{1,0:T(8,128)(2,1)}, bf16[288,1024]{1,0:T(8,128)(2,1)S(1)}, u32[]{:S(2)}, u32[]{:S(2)}) collective-permute-start(bf16[288,1024]{1,0:T(8,128)(2,1)} %copy-done.6), channel_id=1, source_target_pairs={{0,6},{1,7},{2,0},{3,1},{4,2},{5,3},{6,4},{7,5},{8,14},{9,15},{10,... | collective-permute-start | bytes 1769480 | tf_op jit(solution)/shard_map/ppermute | solution.py:168
  52.9 10.4 %copy-start = (bf16[288,1024]{1,0:T(8,128)(2,1)}, bf16[288,1024]{1,0:T(8,128)(2,1)S(1)}, u32[]{:S(2)}) copy-start(bf16[288,1024]{1,0:T(8,128)(2,1)S(1)} %collective-permute-done.1.w2) | copy-start | bytes 1769476
  54.9 8.4 %copy-start.2 = (bf16[288,1024]{1,0:T(8,128)(2,1)}, bf16[288,1024]{1,0:T(8,128)(2,1)S(1)}, u32[]{:S(2)}) copy-start(bf16[288,1024]{1,0:T(8,128)(2,1)S(1)} %collective-permute-done.2.w3) | copy-start | bytes 1769476
  54.9 5.6 %collective-permute-start.3 = (bf16[512,1024]{1,0:T(8,128)(2,1)S(1)}, bf16[512,1024]{1,0:T(8,128)(2,1)S(1)}, u32[]{:S(2)}, u32[]{:S(2)}) collective-permute-start(bf16[512,1024]{1,0:T(8,128)(2,1)S(1)} %bitcast.13), channel_id=1, source_target_pairs={{0,1},{1,0},{2,3},{3,2},{4,5},{5,4},{6,7},{7,6},{8,9},{9,8},{10,11... | collective-permute-start | bytes 3145736 | tf_op jit(solution)/shard_map/ppermute | solution.py:171
  63.3 1.0 copy-start.4
  84.1 17.3 %copy-start.1 = (bf16[288,1024]{1,0:T(8,128)(2,1)S(1)}, bf16[288,1024]{1,0:T(8,128)(2,1)}, u32[]{:S(2)}) copy-start(bf16[288,1024]{1,0:T(8,128)(2,1)} %copy-done) | copy-start | bytes 1769476
  84.1 17.3 %copy-start.3 = (bf16[288,1024]{1,0:T(8,128)(2,1)S(1)}, bf16[288,1024]{1,0:T(8,128)(2,1)}, u32[]{:S(2)}) copy-start(bf16[288,1024]{1,0:T(8,128)(2,1)} %copy-done.2) | copy-start | bytes 1769476
  102.7 6.1 %collective-permute-start.4 = (bf16[512,512]{1,0:T(8,128)(2,1)S(1)}, bf16[512,512]{1,0:T(8,128)(2,1)S(1)}, u32[]{:S(2)}, u32[]{:S(2)}) collective-permute-start(bf16[512,512]{1,0:T(8,128)(2,1)S(1)} %get-tuple-element.34), channel_id=1, source_target_pairs={{0,1},{1,0},{2,3},{3,2},{4,5},{5,4},{6,7},{7,6},{8,9},{9,8},{10,11... | collective-permute-start | bytes 1572872 | tf_op jit(solution)/shard_map/ppermute | solution.py:171
  109.8 50.7 %all-to-all-start.3 = ((bf16[64,8,512]{2,1,0:T(8,128)(2,1)}), bf16[64,8,512]{2,1,0:T(8,128)(2,1)S(1)}, u32[]{:S(2)}, u32[]{:S(2)}) async-start(bf16[64,8,512]{2,1,0:T(8,128)(2,1)} %fusion), calls=%async_computation.3 | async-start | bytes 1048576 | tf_op jit(solution)/shard_map/all_to_all | solution.py:197
  122.0 1.2 copy-start.5
  124.9 16.1 %collective-permute-start.5 = (bf16[288,1024]{1,0:T(8,128)(2,1)S(1)}, bf16[288,1024]{1,0:T(8,128)(2,1)S(1)}, u32[]{:S(2)}, u32[]{:S(2)}) collective-permute-start(bf16[288,1024]{1,0:T(8,128)(2,1)S(1)} %get-tuple-element.36), channel_id=1, source_target_pairs={{0,6},{1,7},{2,0},{3,1},{4,2},{5,3},{6,4},{7,5},{8,14},{9,15},{10,... | collective-permute-start | bytes 1769480 | tf_op jit(solution)/shard_map/ppermute | solution.py:168
  127.7 17.3 %collective-permute-start.6 = (bf16[288,1024]{1,0:T(8,128)(2,1)S(1)}, bf16[288,1024]{1,0:T(8,128)(2,1)S(1)}, u32[]{:S(2)}, u32[]{:S(2)}) collective-permute-start(bf16[288,1024]{1,0:T(8,128)(2,1)S(1)} %get-tuple-element.37), channel_id=1, source_target_pairs={{0,4},{1,5},{2,6},{3,7},{4,0},{5,1},{6,2},{7,3},{8,12},{9,13},{10,... | collective-permute-start | bytes 1769480 | tf_op jit(solution)/shard_map/ppermute | solution.py:168
  130.8 28.2 %collective-permute-start.7 = (bf16[288,1024]{1,0:T(8,128)(2,1)S(1)}, bf16[288,1024]{1,0:T(8,128)(2,1)S(1)}, u32[]{:S(2)}, u32[]{:S(2)}) collective-permute-start(bf16[288,1024]{1,0:T(8,128)(2,1)S(1)} %get-tuple-element.38), channel_id=1, source_target_pairs={{0,2},{1,3},{2,4},{3,5},{4,6},{5,7},{6,0},{7,1},{8,10},{9,11},{10,... | collective-permute-start | bytes 1769480 | tf_op jit(solution)/shard_map/ppermute | solution.py:168

commit v4 on v3

--- a/solution.py
+++ b/solution.py
@@ -11,6 +11,7 @@
 F32, BF16 = jnp.float32, jnp.bfloat16
 VMEM = pl.BlockSpec(memory_space=pltpu.VMEM)
 HBM = pl.BlockSpec(memory_space=pltpu.HBM)
+ANY = pl.BlockSpec(memory_space=pl.ANY)
 
 
 def dot(a, b, ca, cb):
@@ -109,7 +110,7 @@
         out[...] = total.astype(out.dtype)
 
 
-def grad_kernel(g_ref, own_ref, oth_ref, o0, o1, o2, o3):
+def grad_kernel(g_ref, own_ref, oth_ref, kept_ref, o1, o2, o3, o0, sem):
     width = own_ref.shape[1] // 2
     two = 2 * (g_ref.shape[1] // 3)
     mine, theirs = halves(width)
@@ -118,29 +119,37 @@
         for cols, rows in ((mine, own_ref), (theirs, oth_ref)):
             out_ref[:two, cols] = dot(g_ref[q, :two, :], rows[:, :width], 1, 0).astype(BF16)
             out_ref[two:, cols] = dot(g_ref[q, two:, :], rows[:, width:], 1, 0).astype(BF16)
-
-
-def assemble_kernel(b0, b1, b2, b3, gg_ref, gu_ref, gd_ref):
+        if s == 0:
+            copy = pltpu.make_async_copy(o0, kept_ref, sem)
+            copy.start()
+    copy.wait()
+
+
+def assemble_kernel(b0, b1, b2, b3, gg_ref, gu_ref, gd_ref, sems):
     hid = gg_ref.shape[0]
     feats = b0.shape[1]
     chip = lax.axis_index("tensor") // 2
+    copies = []
     for s, b in enumerate((b0, b1, b2, b3)):
-        cols = pl.ds(pl.multiple_of(lax.rem(chip + s, X_CHIPS) * feats, feats), feats)
-        gg_ref[:, cols] = b[:hid, :]
-        gu_ref[:, cols] = b[hid:2 * hid, :]
-        gd_ref[:, cols] = b[2 * hid:, :]
+        start = pl.multiple_of(lax.rem(chip + s, X_CHIPS) * feats, feats)
+        for j, out in enumerate((gg_ref, gu_ref, gd_ref)):
+            copies.append(pltpu.make_async_copy(
+                b.at[pl.ds(j * hid, hid), :], out.at[:, pl.ds(start, feats)], sems.at[s, j]))
+            copies[-1].start()
+    for c in copies:
+        c.wait()
 
 
 def combine_kernel(place_ref, arrived_ref, out_ref):
     out_ref[...] = dot(place_ref[...], arrived_ref[...], 0, 0).astype(BF16)
 
 
-def call(kernel, outs, n_in, scratch=(), in_specs=None, flops=0, nbytes=0):
+def call(kernel, outs, n_in, scratch=(), in_specs=None, out_specs=None, flops=0, nbytes=0):
     return pl.pallas_call(
         kernel,
         out_shape=[jax.ShapeDtypeStruct(s, d) for s, d in outs],
         in_specs=in_specs or [VMEM] * n_in,
-        out_specs=[VMEM] * len(outs),
+        out_specs=out_specs or [VMEM] * len(outs),
         scratch_shapes=list(scratch),
         compiler_params=pltpu.CompilerParams(vmem_limit_bytes=16 << 20),
         cost_estimate=pl.CostEstimate(flops=flops, bytes_accessed=nbytes, transcendentals=0),
@@ -182,21 +191,31 @@
     rows = lax.all_to_all(sent.reshape(groups, CAP, 2 * width), "expert", 0, 0, tiled=True)
     rows = rows.reshape(slots, 2 * width)
     got = {s: shift(blocks[s], s) for s in (2, 1, 3)}
-    rows, *weights = lax.optimization_barrier((rows, got[1], got[2], got[3]))
-    weights = [blocks[0]] + weights
+    rows, w2, w1, w3 = lax.optimization_barrier((rows, got[2], got[1], got[3]))
+    weights = (blocks[0], w1, w2, w3)
     other = sibling(rows)
     (parts,) = call(partial_kernel, [((X_CHIPS, 3 * hid, slots), BF16)], 6, flops=12 * 10**8, nbytes=6 << 20)(rows, other, *weights)
     (acts,) = call(act_kernel, [((X_CHIPS, 3 * hid, slots), BF16)], 1, flops=10**7, nbytes=2 << 20)(over_x(parts))
     gathered = (over_x(acts),)
+    grads = call(
+        grad_kernel, [(wide, BF16)] * X_CHIPS, 3,
+        scratch=[pltpu.VMEM(wide, BF16), pltpu.SemaphoreType.DMA(())],
+        out_specs=[HBM] + [VMEM] * 3, flops=12 * 10**8, nbytes=6 << 20,
+    )(*gathered, rows, other)
+    gathered, *grads = lax.optimization_barrier((gathered, *grads))
     keep, send = call(
         row_kernel, [((slots, width), F32), ((slots, width), BF16)], 5,
         flops=8 * 10**8, nbytes=5 << 20,
     )(*gathered, *weights)
-    grads = call(grad_kernel, [(wide, BF16)] * X_CHIPS, 3, flops=12 * 10**8, nbytes=6 << 20)(*gathered, rows, other)
     row_grad = (keep + sibling(send).astype(F32)).astype(BF16)
     arrived = lax.all_to_all(row_grad.reshape(groups, CAP, width), "expert", 0, 0, tiled=True)
     got = {s: shift(grads[s], -s) for s in (2, 1, 3)}
-    outs = call(assemble_kernel, [((hid, feats), BF16)] * 3, 4, nbytes=5 << 20)(grads[0], got[1], got[2], got[3])
+    outs = call(
+        assemble_kernel, [((hid, feats), BF16)] * 3, 4,
+        scratch=[pltpu.SemaphoreType.DMA((X_CHIPS, 3))],
+        in_specs=[ANY] * 4, flops=2 * 10**11, nbytes=5 << 20,
+    )(grads[0], got[1], got[2], got[3])
+    arrived, *outs = lax.optimization_barrier((arrived, *outs))
     (grad_tokens,) = call(
         combine_kernel, [((toks, width), BF16)], 2, flops=10**7, nbytes=1 << 20,
     )(place, arrived.reshape(slots, width))

time: 162 us -> 151 us (0.932); the launches traced: 161 us -> 148 us
  waiting for transfers between devices: 52.2 us -> 37.9 us
  Pallas kernels: 12.8 us -> 15.6 us
    ppermute x6, waiting for transfers between devices: 48.5 us -> 33.5 us  [shift(): lax.ppermute(v, 'tensor', [(i, (i + 2 * s) % n_tensor) for i in range(n_t...]
    all_to_all x1, waiting for transfers between devices: 0.01 us -> 2.17 us  [on_device(): lax.all_to_all(row_grad.reshape(groups, CAP, width), 'expert', 0, 0, tile...]
    pallas_call x2, Pallas kernels: 3.26 us -> 5.06 us  [the longest x1 3.18 us: on_device(): call(grad_kernel, [(wide, BF16)] * X_CHIPS, 3, scratch=[pltpu.VMEM(wide,...]
  transfers between devices with their start and end apart: 10 -> 10, of which waited for: 8 -> 5; matrix products, arithmetic and copies ran while one was open for 0% -> 1% of each run, Pallas kernels for 2% -> 1%
where the time goes in v4:
time: 151 us; the launch traced here: 148 us
  starting transfers between devices  55.6 us (37%)
  waiting for transfers between devices  37.9 us (25%)
  blocking collectives  36.5 us (24%)
  Pallas kernels  15.6 us (10%)
    all_to_all x2, blocking collectives, over_x(): lax.all_to_all(v, 'tensor', 0, 0, axis_index_groups=same_core, tiled=True)  36.5 us
    ppermute x6, waiting for transfers between devices, shift(): lax.ppermute(v, 'tensor', [(i, (i + 2 * s) % n_tensor) for i in range(n_t...  33.5 us
    ppermute x6, starting transfers between devices, shift(): lax.ppermute(v, 'tensor', [(i, (i + 2 * s) % n_tensor) for i in range(n_t...  19 us
    all_to_all x1, starting transfers between devices, on_device(): lax.all_to_all(sent.reshape(groups, CAP, 2 * width), 'expert', 0, 0, tile...  17.1 us
    all_to_all x1, starting transfers between devices, on_device(): lax.all_to_all(row_grad.reshape(groups, CAP, width), 'expert', 0, 0, tile...  12.4 us
    ppermute x2, starting transfers between devices, sibling(): return lax.ppermute(v, 'tensor', [(i, i ^ 1) for i in range(n_tensor)])  7.14 us
    pallas_call x1, Pallas kernels, on_device(): call(dispatch_kernel, [((slots, 2 * width), BF16), ((slots, toks), BF16)]...  4.29 us
    pallas_call x1, Pallas kernels, on_device(): call(grad_kernel, [(wide, BF16)] * X_CHIPS, 3, scratch=[pltpu.VMEM(wide,...  3.18 us
  transfers between devices with their start and end apart: 10, of which 5 were waited for; matrix products, arithmetic and copies ran while one was open for 1% of the time, Pallas kernels for 1%

profile of v4, /device:TPU:1, one launch (start us, length us, event | category | flops | bytes accessed | tf_op | source)
XLA Modules:
  0.0 148.3 jit_solution(9323753464008248615)
XLA Ops:
  0.6 4.3 %shard_map.102 = (bf16[512,1024]{1,0:T(8,128)(2,1)}, bf16[512,48]{1,0:T(8,128)(2,1)S(1)}, bf16[288,1024]{1,0:T(8,128)(2,1)S(1)}, bf16[288,1024]{1,0:T(8,128)(2,1...) custom-call(s32[8,48]{1,0:T(8,128)} %bitcast.19, f32[8,48]{1,0:T(8,128)} %bitcast.20, ...), custom_call_target="tpu_custom_call" | custom-call | flops 100000000 | bytes 6291456 | tf_op jit(solution)/shard_map/pallas_call | solution.py:183
  5.7 17.1 %all-to-all-start = ((bf16[64,8,1024]{2,1,0:T(8,128)(2,1)}), bf16[64,8,1024]{2,1,0:T(8,128)(2,1)S(1)}, u32[]{:S(2)}, u32[]{:S(2)}) async-start(bf16[64,8,1024]{2,1,0:T(8,128)(2,1)} %bitcast.5), calls=%async_computation | async-start | bytes 2097152 | tf_op jit(solution)/shard_map/all_to_all | solution.py:191
  22.9 4.7 %collective-permute-start = (bf16[288,1024]{1,0:T(8,128)(2,1)}, bf16[288,1024]{1,0:T(8,128)(2,1)S(1)}, u32[]{:S(2)}, u32[]{:S(2)}) collective-permute-start(bf16[288,1024]{1,0:T(8,128)(2,1)} %get-tuple-element.34), channel_id=1, source_target_pairs={{0,4},{1,5},{2,6},{3,7},{4,0},{5,1},{6,2},{7,3},{8,12},{9,13},{10,... | collective-permute-start | bytes 1769480 | tf_op jit(solution)/shard_map/ppermute | solution.py:177
  27.6 2.2 %collective-permute-start.1 = (bf16[288,1024]{1,0:T(8,128)(2,1)}, bf16[288,1024]{1,0:T(8,128)(2,1)S(1)}, u32[]{:S(2)}, u32[]{:S(2)}) collective-permute-start(bf16[288,1024]{1,0:T(8,128)(2,1)} %get-tuple-element.35), channel_id=1, source_target_pairs={{0,2},{1,3},{2,4},{3,5},{4,6},{5,7},{6,0},{7,1},{8,10},{9,11},{10,... | collective-permute-start | bytes 1769480 | tf_op jit(solution)/shard_map/ppermute | solution.py:177
  29.8 4.3 %collective-permute-start.2 = (bf16[288,1024]{1,0:T(8,128)(2,1)}, bf16[288,1024]{1,0:T(8,128)(2,1)S(1)}, u32[]{:S(2)}, u32[]{:S(2)}) collective-permute-start(bf16[288,1024]{1,0:T(8,128)(2,1)} %copy-done), channel_id=1, source_target_pairs={{0,6},{1,7},{2,0},{3,1},{4,2},{5,3},{6,4},{7,5},{8,14},{9,15},{10,... | collective-permute-start | bytes 1769480 | tf_op jit(solution)/shard_map/ppermute | solution.py:177
  34.1 6.4 %collective-permute-done.w2 = bf16[288,1024]{1,0:T(8,128)(2,1)S(1)} collective-permute-done((bf16[288,1024]{1,0:T(8,128)(2,1)}, bf16[288,1024]{1,0:T(8,128)(2,1)S(1)}, u32[]{:S(2)}, u32[]{:S(2)}) %collective-permute-start) | collective-permute-done | bytes 589856 | tf_op jit(solution)/shard_map/ppermute | solution.py:177
  40.4 14.0 %collective-permute-done.1.w1 = bf16[288,1024]{1,0:T(8,128)(2,1)S(1)} collective-permute-done((bf16[288,1024]{1,0:T(8,128)(2,1)}, bf16[288,1024]{1,0:T(8,128)(2,1)S(1)}, u32[]{:S(2)}, u32[]{:S(2)}) %collective-permute-start.1) | collective-permute-done | bytes 589856 | tf_op jit(solution)/shard_map/ppermute | solution.py:177
  54.4 2.5 %collective-permute-start.3 = (bf16[512,1024]{1,0:T(8,128)(2,1)S(1)}, bf16[512,1024]{1,0:T(8,128)(2,1)S(1)}, u32[]{:S(2)}, u32[]{:S(2)}) collective-permute-start(bf16[512,1024]{1,0:T(8,128)(2,1)S(1)} %bitcast.13), channel_id=1, source_target_pairs={{0,1},{1,0},{2,3},{3,2},{4,5},{5,4},{6,7},{7,6},{8,9},{9,8},{10,11... | collective-permute-start | bytes 3145736 | tf_op jit(solution)/shard_map/ppermute | solution.py:180
  56.9 2.3 %collective-permute-done.3.oth_ref = bf16[512,1024]{1,0:T(8,128)(2,1)S(1)} collective-permute-done((bf16[512,1024]{1,0:T(8,128)(2,1)S(1)}, bf16[512,1024]{1,0:T(8,128)(2,1)S(1)}, u32[]{:S(2)}, u32[]{:S(2)}) %collective-permute-start.3) | collective-permute-done | bytes 1048608 | tf_op jit(solution)/shard_map/ppermute | solution.py:180
  59.2 2.8 %shard_map.103 = bf16[4,288,512]{2,1,0:T(8,128)(2,1)S(1)} custom-call(bf16[512,1024]{1,0:T(8,128)(2,1)S(1)} %bitcast.14, bf16[512,1024]{1,0:T(8,128)(2,1)S(1)} %collective-permute-done.3.oth_ref, bf16[288,1024]{1,0:T(8,128)(2,1)S(1)} %get-tuple-element.38.w0, bf16[288,1024]{1,0:T(8,128)(2,1)S(1)} %collective-permute-done.1.w1, ...), custom_call_target="tpu_custom_call" | custom-call | flops 1200000000 | bytes 6291456 | tf_op jit(solution)/shard_map/pallas_call | solution.py:197
  62.0 19.3 %all_to_all.20.p_ref = bf16[4,288,512]{2,1,0:T(8,128)(2,1)S(1)} all-to-all(bf16[4,288,512]{2,1,0:T(8,128)(2,1)S(1)} %shard_map.103), channel_id=1, replica_groups={{0,2,4,6},{1,3,5,7},{8,10,12,14},{9,11,13,15},{16,18,20,22},{17,19,21,2..., dimensions={0} | all-to-all | bytes 2359296 | tf_op jit(solution)/shard_map/all_to_all | solution.py:174
  81.6 17.2 %all_to_all.21.g_ref = bf16[4,288,512]{2,1,0:T(8,128)(2,1)S(1)} all-to-all(bf16[4,288,512]{2,1,0:T(8,128)(2,1)S(1)} %shard_map.104), channel_id=1, replica_groups={{0,2,4,6},{1,3,5,7},{8,10,12,14},{9,11,13,15},{16,18,20,22},{17,19,21,2..., dimensions={0} | all-to-all | bytes 2359296 | tf_op jit(solution)/shard_map/all_to_all | solution.py:174
  98.8 3.2 %shard_map.105 = (bf16[288,1024]{1,0:T(8,128)(2,1)S(1)}, bf16[288,1024]{1,0:T(8,128)(2,1)}, bf16[288,1024]{1,0:T(8,128)(2,1)}, bf16[288,1024]{1,0:T(8,128)(2,1)}) custom-call(bf16[4,288,512]{2,1,0:T(8,128)(2,1)S(1)} %all_to_all.21.g_ref, bf16[512,1024]{1,0:T(8,128)(2,1)S(1)} %bitcast.15, bf16[512,1024]{1,0:T(8,128)(2,1)S(1)} %collective-permute-done.3.oth_ref), custom_call_target="tpu_custom_call" | custom-call | flops 1200000000 | bytes 6291456 | tf_op jit(solution)/shard_map/pallas_call | solution.py:200
  102.0 1.3 shard_map.106
  103.3 4.6 %collective-permute-start.4 = (bf16[512,512]{1,0:T(8,128)(2,1)S(1)}, bf16[512,512]{1,0:T(8,128)(2,1)S(1)}, u32[]{:S(2)}, u32[]{:S(2)}) collective-permute-start(bf16[512,512]{1,0:T(8,128)(2,1)S(1)} %get-tuple-element.48), channel_id=1, source_target_pairs={{0,1},{1,0},{2,3},{3,2},{4,5},{5,4},{6,7},{7,6},{8,9},{9,8},{10,11... | collective-permute-start | bytes 1572872 | tf_op jit(solution)/shard_map/ppermute | solution.py:180
  107.9 2.8 %collective-permute-start.5 = (bf16[288,1024]{1,0:T(8,128)(2,1)}, bf16[288,1024]{1,0:T(8,128)(2,1)S(1)}, u32[]{:S(2)}, u32[]{:S(2)}) collective-permute-start(bf16[288,1024]{1,0:T(8,128)(2,1)} %get-tuple-element.50), channel_id=1, source_target_pairs={{0,6},{1,7},{2,0},{3,1},{4,2},{5,3},{6,4},{7,5},{8,14},{9,15},{10,... | collective-permute-start | bytes 1769480 | tf_op jit(solution)/shard_map/ppermute | solution.py:177
  110.7 3.1 %collective-permute-start.6 = (bf16[288,1024]{1,0:T(8,128)(2,1)}, bf16[288,1024]{1,0:T(8,128)(2,1)S(1)}, u32[]{:S(2)}, u32[]{:S(2)}) collective-permute-start(bf16[288,1024]{1,0:T(8,128)(2,1)} %get-tuple-element.51), channel_id=1, source_target_pairs={{0,4},{1,5},{2,6},{3,7},{4,0},{5,1},{6,2},{7,3},{8,12},{9,13},{10,... | collective-permute-start | bytes 1769480 | tf_op jit(solution)/shard_map/ppermute | solution.py:177
  113.8 1.9 %collective-permute-start.7 = (bf16[288,1024]{1,0:T(8,128)(2,1)}, bf16[288,1024]{1,0:T(8,128)(2,1)S(1)}, u32[]{:S(2)}, u32[]{:S(2)}) collective-permute-start(bf16[288,1024]{1,0:T(8,128)(2,1)} %get-tuple-element.52), channel_id=1, source_target_pairs={{0,2},{1,3},{2,4},{3,5},{4,6},{5,7},{6,0},{7,1},{8,10},{9,11},{10,... | collective-permute-start | bytes 1769480 | tf_op jit(solution)/shard_map/ppermute | solution.py:177
  115.8 1.0 fusion
  116.7 12.4 %all-to-all-start.3 = ((bf16[64,8,512]{2,1,0:T(8,128)(2,1)}), bf16[64,8,512]{2,1,0:T(8,128)(2,1)}, u32[]{:S(2)}, u32[]{:S(2)}) async-start(bf16[64,8,512]{2,1,0:T(8,128)(2,1)} %fusion), calls=%async_computation.3 | async-start | bytes 1048576 | tf_op jit(solution)/shard_map/all_to_all | solution.py:211
  129.2 13.2 %collective-permute-done.7.b3 = bf16[288,1024]{1,0:T(8,128)(2,1)S(1)} collective-permute-done((bf16[288,1024]{1,0:T(8,128)(2,1)}, bf16[288,1024]{1,0:T(8,128)(2,1)S(1)}, u32[]{:S(2)}, u32[]{:S(2)}) %collective-permute-start.7) | collective-permute-done | bytes 589856 | tf_op jit(solution)/shard_map/ppermute | solution.py:177
  142.3 1.9 %shard_map.107 = (bf16[96,4096]{1,0:T(8,128)(2,1)}, bf16[96,4096]{1,0:T(8,128)(2,1)}, bf16[96,4096]{1,0:T(8,128)(2,1)}) custom-call(bf16[288,1024]{1,0:T(8,128)(2,1)S(1)} %copy-done.2, bf16[288,1024]{1,0:T(8,128)(2,1)S(1)} %collective-permute-done.5.b1, bf16[288,1024]{1,0:T(8,128)(2,1)S(1)} %collective-permute-done.6.b2, ...), custom_call_target="tpu_custom_call" | custom-call | flops 199999995904 | bytes 5242880 | tf_op jit(solution)/shard_map/pallas_call | solution.py:213
  144.2 2.2 %all-to-all-done.3 = bf16[64,8,512]{2,1,0:T(8,128)(2,1)} async-done(((bf16[64,8,512]{2,1,0:T(8,128)(2,1)}), bf16[64,8,512]{2,1,0:T(8,128)(2,1)}, u32[]{:S(2)}, u32[]{:S(2)}) %all-to-all-start.3) | async-done | bytes 524320 | tf_op jit(solution)/shard_map/all_to_all | solution.py:211
  146.4 1.9 %shard_map.108 = bf16[48,512]{1,0:T(8,128)(2,1)} custom-call(bf16[512,48]{1,0:T(8,128)(2,1)S(1)} %get-tuple-element.32.place_ref, bf16[512,512]{1,0:T(8,128)(2,1)} %bitcast.8.arrived_ref), custom_call_target="tpu_custom_call" | custom-call | flops 10000000 | bytes 1048576 | tf_op jit(solution)/shard_map/pallas_call | solution.py:219
  (12 shorter events, 1.1 us)
Async XLA Ops:
  4.9 0.8 copy-start
  5.7 48.6 %all-to-all-start = ((bf16[64,8,1024]{2,1,0:T(8,128)(2,1)}), bf16[64,8,1024]{2,1,0:T(8,128)(2,1)S(1)}, u32[]{:S(2)}, u32[]{:S(2)}) async-start(bf16[64,8,1024]{2,1,0:T(8,128)(2,1)} %bitcast.5), calls=%async_computation | async-start | bytes 2097152 | tf_op jit(solution)/shard_map/all_to_all | solution.py:191
  22.9 17.5 %collective-permute-start = (bf16[288,1024]{1,0:T(8,128)(2,1)}, bf16[288,1024]{1,0:T(8,128)(2,1)S(1)}, u32[]{:S(2)}, u32[]{:S(2)}) collective-permute-start(bf16[288,1024]{1,0:T(8,128)(2,1)} %get-tuple-element.34), channel_id=1, source_target_pairs={{0,4},{1,5},{2,6},{3,7},{4,0},{5,1},{6,2},{7,3},{8,12},{9,13},{10,... | collective-permute-start | bytes 1769480 | tf_op jit(solution)/shard_map/ppermute | solution.py:177
  27.6 26.8 %collective-permute-start.1 = (bf16[288,1024]{1,0:T(8,128)(2,1)}, bf16[288,1024]{1,0:T(8,128)(2,1)S(1)}, u32[]{:S(2)}, u32[]{:S(2)}) collective-permute-start(bf16[288,1024]{1,0:T(8,128)(2,1)} %get-tuple-element.35), channel_id=1, source_target_pairs={{0,2},{1,3},{2,4},{3,5},{4,6},{5,7},{6,0},{7,1},{8,10},{9,11},{10,... | collective-permute-start | bytes 1769480 | tf_op jit(solution)/shard_map/ppermute | solution.py:177
  29.8 24.6 %collective-permute-start.2 = (bf16[288,1024]{1,0:T(8,128)(2,1)}, bf16[288,1024]{1,0:T(8,128)(2,1)S(1)}, u32[]{:S(2)}, u32[]{:S(2)}) collective-permute-start(bf16[288,1024]{1,0:T(8,128)(2,1)} %copy-done), channel_id=1, source_target_pairs={{0,6},{1,7},{2,0},{3,1},{4,2},{5,3},{6,4},{7,5},{8,14},{9,15},{10,... | collective-permute-start | bytes 1769480 | tf_op jit(solution)/shard_map/ppermute | solution.py:177
  54.4 4.8 %collective-permute-start.3 = (bf16[512,1024]{1,0:T(8,128)(2,1)S(1)}, bf16[512,1024]{1,0:T(8,128)(2,1)S(1)}, u32[]{:S(2)}, u32[]{:S(2)}) collective-permute-start(bf16[512,1024]{1,0:T(8,128)(2,1)S(1)} %bitcast.13), channel_id=1, source_target_pairs={{0,1},{1,0},{2,3},{3,2},{4,5},{5,4},{6,7},{7,6},{8,9},{9,8},{10,11... | collective-permute-start | bytes 3145736 | tf_op jit(solution)/shard_map/ppermute | solution.py:180
  101.9 1.3 copy-start.1
  103.3 12.5 %collective-permute-start.4 = (bf16[512,512]{1,0:T(8,128)(2,1)S(1)}, bf16[512,512]{1,0:T(8,128)(2,1)S(1)}, u32[]{:S(2)}, u32[]{:S(2)}) collective-permute-start(bf16[512,512]{1,0:T(8,128)(2,1)S(1)} %get-tuple-element.48), channel_id=1, source_target_pairs={{0,1},{1,0},{2,3},{3,2},{4,5},{5,4},{6,7},{7,6},{8,9},{9,8},{10,11... | collective-permute-start | bytes 1572872 | tf_op jit(solution)/shard_map/ppermute | solution.py:180
  107.9 21.2 %collective-permute-start.5 = (bf16[288,1024]{1,0:T(8,128)(2,1)}, bf16[288,1024]{1,0:T(8,128)(2,1)S(1)}, u32[]{:S(2)}, u32[]{:S(2)}) collective-permute-start(bf16[288,1024]{1,0:T(8,128)(2,1)} %get-tuple-element.50), channel_id=1, source_target_pairs={{0,6},{1,7},{2,0},{3,1},{4,2},{5,3},{6,4},{7,5},{8,14},{9,15},{10,... | collective-permute-start | bytes 1769480 | tf_op jit(solution)/shard_map/ppermute | solution.py:177
  110.7 18.4 %collective-permute-start.6 = (bf16[288,1024]{1,0:T(8,128)(2,1)}, bf16[288,1024]{1,0:T(8,128)(2,1)S(1)}, u32[]{:S(2)}, u32[]{:S(2)}) collective-permute-start(bf16[288,1024]{1,0:T(8,128)(2,1)} %get-tuple-element.51), channel_id=1, source_target_pairs={{0,4},{1,5},{2,6},{3,7},{4,0},{5,1},{6,2},{7,3},{8,12},{9,13},{10,... | collective-permute-start | bytes 1769480 | tf_op jit(solution)/shard_map/ppermute | solution.py:177
  113.8 28.5 %collective-permute-start.7 = (bf16[288,1024]{1,0:T(8,128)(2,1)}, bf16[288,1024]{1,0:T(8,128)(2,1)S(1)}, u32[]{:S(2)}, u32[]{:S(2)}) collective-permute-start(bf16[288,1024]{1,0:T(8,128)(2,1)} %get-tuple-element.52), channel_id=1, source_target_pairs={{0,2},{1,3},{2,4},{3,5},{4,6},{5,7},{6,0},{7,1},{8,10},{9,11},{10,... | collective-permute-start | bytes 1769480 | tf_op jit(solution)/shard_map/ppermute | solution.py:177
  115.8 26.6 %copy-start.2 = (bf16[288,1024]{1,0:T(8,128)(2,1)S(1)}, bf16[288,1024]{1,0:T(8,128)(2,1)}, u32[]{:S(2)}) copy-start(bf16[288,1024]{1,0:T(8,128)(2,1)} %copy-done.1) | copy-start | bytes 1769476
  116.7 29.7 %all-to-all-start.3 = ((bf16[64,8,512]{2,1,0:T(8,128)(2,1)}), bf16[64,8,512]{2,1,0:T(8,128)(2,1)}, u32[]{:S(2)}, u32[]{:S(2)}) async-start(bf16[64,8,512]{2,1,0:T(8,128)(2,1)} %fusion), calls=%async_computation.3 | async-start | bytes 1048576 | tf_op jit(solution)/shard_map/all_to_all | solution.py:211

commit v5 on v4

--- a/solution.py
+++ b/solution.py
@@ -125,32 +125,40 @@
     copy.wait()
 
 
-def assemble_kernel(b0, b1, b2, b3, gg_ref, gu_ref, gd_ref, sems):
-    hid = gg_ref.shape[0]
-    feats = b0.shape[1]
-    chip = lax.axis_index("tensor") // 2
+def place_columns(blocks, outs, sems):
+    hid, feats = outs[0].shape[0], blocks[0][1].shape[1]
     copies = []
-    for s, b in enumerate((b0, b1, b2, b3)):
+    for i, (s, b) in enumerate(blocks):
+        chip = lax.axis_index("tensor") // 2
         start = pl.multiple_of(lax.rem(chip + s, X_CHIPS) * feats, feats)
-        for j, out in enumerate((gg_ref, gu_ref, gd_ref)):
+        for j, out in enumerate(outs):
             copies.append(pltpu.make_async_copy(
-                b.at[pl.ds(j * hid, hid), :], out.at[:, pl.ds(start, feats)], sems.at[s, j]))
+                b.at[pl.ds(j * hid, hid), :], out.at[:, pl.ds(start, feats)], sems.at[i, j]))
             copies[-1].start()
     for c in copies:
         c.wait()
 
 
+def first_columns_kernel(b0, b2, gg_ref, gu_ref, gd_ref, sems):
+    place_columns(((0, b0), (2, b2)), (gg_ref, gu_ref, gd_ref), sems)
+
+
+def last_columns_kernel(b1, b3, gg_in, gu_in, gd_in, gg_ref, gu_ref, gd_ref, sems):
+    place_columns(((1, b1), (3, b3)), (gg_ref, gu_ref, gd_ref), sems)
+
+
 def combine_kernel(place_ref, arrived_ref, out_ref):
     out_ref[...] = dot(place_ref[...], arrived_ref[...], 0, 0).astype(BF16)
 
 
-def call(kernel, outs, n_in, scratch=(), in_specs=None, out_specs=None, flops=0, nbytes=0):
+def call(kernel, outs, n_in, scratch=(), in_specs=None, out_specs=None, aliases=None, flops=0, nbytes=0):
     return pl.pallas_call(
         kernel,
-        out_shape=[jax.ShapeDtypeStruct(s, d) for s, d in outs],
+        out_shape=[o if isinstance(o, pl.MemoryRef) else jax.ShapeDtypeStruct(*o) for o in outs],
         in_specs=in_specs or [VMEM] * n_in,
         out_specs=out_specs or [VMEM] * len(outs),
         scratch_shapes=list(scratch),
+        input_output_aliases=aliases or {},
         compiler_params=pltpu.CompilerParams(vmem_limit_bytes=16 << 20),
         cost_estimate=pl.CostEstimate(flops=flops, bytes_accessed=nbytes, transcendentals=0),
     )
@@ -182,7 +190,7 @@
     wide = (3 * hid, chip_feats)
     sent, place, *blocks = call(
         dispatch_kernel,
-        [((slots, 2 * width), BF16), ((slots, toks), BF16)] + [(wide, BF16)] * X_CHIPS,
+        [((slots, 2 * width), BF16), ((slots, toks), BF16)] + [pltpu.HBM(wide, BF16)] * X_CHIPS,
         7,
         scratch=[pltpu.SemaphoreType.DMA((X_CHIPS, 3))],
         in_specs=[VMEM] * 4 + [HBM] * 3,
@@ -198,7 +206,7 @@
     (acts,) = call(act_kernel, [((X_CHIPS, 3 * hid, slots), BF16)], 1, flops=10**7, nbytes=2 << 20)(over_x(parts))
     gathered = (over_x(acts),)
     grads = call(
-        grad_kernel, [(wide, BF16)] * X_CHIPS, 3,
+        grad_kernel, [pltpu.HBM(wide, BF16)] * X_CHIPS, 3,
         scratch=[pltpu.VMEM(wide, BF16), pltpu.SemaphoreType.DMA(())],
         out_specs=[HBM] + [VMEM] * 3, flops=12 * 10**8, nbytes=6 << 20,
     )(*gathered, rows, other)
@@ -210,15 +218,22 @@
     row_grad = (keep + sibling(send).astype(F32)).astype(BF16)
     arrived = lax.all_to_all(row_grad.reshape(groups, CAP, width), "expert", 0, 0, tiled=True)
     got = {s: shift(grads[s], -s) for s in (2, 1, 3)}
+    whole = [pltpu.HBM((hid, feats), BF16)] * 3
     outs = call(
-        assemble_kernel, [((hid, feats), BF16)] * 3, 4,
-        scratch=[pltpu.SemaphoreType.DMA((X_CHIPS, 3))],
-        in_specs=[ANY] * 4, flops=2 * 10**11, nbytes=5 << 20,
-    )(grads[0], got[1], got[2], got[3])
-    arrived, *outs = lax.optimization_barrier((arrived, *outs))
+        first_columns_kernel, whole, 2,
+        scratch=[pltpu.SemaphoreType.DMA((2, 3))],
+        out_specs=[HBM] * 3, flops=10**10, nbytes=2 << 20,
+    )(grads[0], got[2])
     (grad_tokens,) = call(
         combine_kernel, [((toks, width), BF16)], 2, flops=10**7, nbytes=1 << 20,
     )(place, arrived.reshape(slots, width))
+    near, grad_tokens = lax.optimization_barrier((got[1], grad_tokens))
+    outs = call(
+        last_columns_kernel, whole, 5,
+        scratch=[pltpu.SemaphoreType.DMA((2, 3))],
+        in_specs=[VMEM] * 2 + [HBM] * 3, out_specs=[HBM] * 3,
+        aliases={2: 0, 3: 1, 4: 2}, nbytes=2 << 20,
+    )(near, got[3], *outs)
     return (grad_tokens, *(g.reshape(1, hid, feats) for g in outs))
 
 

time: 151 us -> 147 us (0.974); the launches traced: 148 us -> 146 us
  waiting for transfers between devices: 37.9 us -> 36 us
    ppermute x6, waiting for transfers between devices: 33.5 us -> 23.1 us  [shift(): lax.ppermute(v, 'tensor', [(i, (i + 2 * s) % n_tensor) for i in range(n_t...]
    all_to_all x1, waiting for transfers between devices: 2.17 us -> 10.6 us  [on_device(): lax.all_to_all(row_grad.reshape(groups, CAP, width), 'expert', 0, 0, tile...]
    pallas_call x2 -> x3, Pallas kernels: 5.06 us -> 5.7 us  [the longest x1 3.58 us: on_device(): call(grad_kernel, [pltpu.HBM(wide, BF16)] * X_CHIPS, 3, scratch=[pltpu.VM...]
where the time goes in v5:
time: 147 us; the launch traced here: 146 us
  starting transfers between devices  56.1 us (38%)
  blocking collectives  36.5 us (25%)
  waiting for transfers between devices  36 us (24%)
  Pallas kernels  15.6 us (11%)
    all_to_all x2, blocking collectives, over_x(): lax.all_to_all(v, 'tensor', 0, 0, axis_index_groups=same_core, tiled=True)  36.5 us
    ppermute x6, waiting for transfers between devices, shift(): lax.ppermute(v, 'tensor', [(i, (i + 2 * s) % n_tensor) for i in range(n_t...  23.1 us
    ppermute x6, starting transfers between devices, shift(): lax.ppermute(v, 'tensor', [(i, (i + 2 * s) % n_tensor) for i in range(n_t...  19.6 us
    all_to_all x1, starting transfers between devices, on_device(): lax.all_to_all(sent.reshape(groups, CAP, 2 * width), 'expert', 0, 0, tile...  17.3 us
    all_to_all x1, starting transfers between devices, on_device(): lax.all_to_all(row_grad.reshape(groups, CAP, width), 'expert', 0, 0, tile...  12.1 us
    all_to_all x1, waiting for transfers between devices, on_device(): lax.all_to_all(row_grad.reshape(groups, CAP, width), 'expert', 0, 0, tile...  10.6 us
    ppermute x2, starting transfers between devices, sibling(): return lax.ppermute(v, 'tensor', [(i, i ^ 1) for i in range(n_tensor)])  7.12 us
    pallas_call x1, Pallas kernels, on_device(): call(dispatch_kernel, [((slots, 2 * width), BF16), ((slots, toks), BF16)]...  4.7 us
  transfers between devices with their start and end apart: 10, of which 5 were waited for; matrix products, arithmetic and copies ran while one was open for 1% of the time, Pallas kernels for 1%

profile of v5, /device:TPU:1, one launch (start us, length us, event | category | flops | bytes accessed | tf_op | source)
XLA Modules:
  0.0 146.1 jit_solution(8318059507150831171)
XLA Ops:
  0.6 4.7 %shard_map.102 = (bf16[512,1024]{1,0:T(8,128)(2,1)}, bf16[512,48]{1,0:T(8,128)(2,1)S(1)}, bf16[288,1024]{1,0:T(8,128)(2,1)}, bf16[288,1024]{1,0:T(8,128)(2,1)}, ...) custom-call(s32[8,48]{1,0:T(8,128)} %bitcast.23, f32[8,48]{1,0:T(8,128)} %bitcast.24, bf16[48,512]{1,0:T(8,128)(2,1)} %tok_ref.1, ...), custom_call_target="tpu_custom_call" | custom-call | flops 100000000 | bytes 6291456 | tf_op jit(solution)/shard_map/pallas_call | solution.py:191
  5.3 17.3 %all-to-all-start = ((bf16[64,8,1024]{2,1,0:T(8,128)(2,1)}), bf16[64,8,1024]{2,1,0:T(8,128)(2,1)S(1)}, u32[]{:S(2)}, u32[]{:S(2)}) async-start(bf16[64,8,1024]{2,1,0:T(8,128)(2,1)} %bitcast.5), calls=%async_computation | async-start | bytes 2097152 | tf_op jit(solution)/shard_map/all_to_all | solution.py:199
  22.6 4.7 %collective-permute-start = (bf16[288,1024]{1,0:T(8,128)(2,1)}, bf16[288,1024]{1,0:T(8,128)(2,1)S(1)}, u32[]{:S(2)}, u32[]{:S(2)}) collective-permute-start(bf16[288,1024]{1,0:T(8,128)(2,1)} %get-tuple-element.34), channel_id=1, source_target_pairs={{0,4},{1,5},{2,6},{3,7},{4,0},{5,1},{6,2},{7,3},{8,12},{9,13},{10,... | collective-permute-start | bytes 1769480 | tf_op jit(solution)/shard_map/ppermute | solution.py:185
  27.3 2.2 %collective-permute-start.1 = (bf16[288,1024]{1,0:T(8,128)(2,1)}, bf16[288,1024]{1,0:T(8,128)(2,1)S(1)}, u32[]{:S(2)}, u32[]{:S(2)}) collective-permute-start(bf16[288,1024]{1,0:T(8,128)(2,1)} %get-tuple-element.35), channel_id=1, source_target_pairs={{0,2},{1,3},{2,4},{3,5},{4,6},{5,7},{6,0},{7,1},{8,10},{9,11},{10,... | collective-permute-start | bytes 1769480 | tf_op jit(solution)/shard_map/ppermute | solution.py:185
  29.5 4.3 %collective-permute-start.2 = (bf16[288,1024]{1,0:T(8,128)(2,1)}, bf16[288,1024]{1,0:T(8,128)(2,1)S(1)}, u32[]{:S(2)}, u32[]{:S(2)}) collective-permute-start(bf16[288,1024]{1,0:T(8,128)(2,1)} %get-tuple-element.36), channel_id=1, source_target_pairs={{0,6},{1,7},{2,0},{3,1},{4,2},{5,3},{6,4},{7,5},{8,14},{9,15},{10,... | collective-permute-start | bytes 1769480 | tf_op jit(solution)/shard_map/ppermute | solution.py:185
  33.8 6.4 %collective-permute-done.w2 = bf16[288,1024]{1,0:T(8,128)(2,1)S(1)} collective-permute-done((bf16[288,1024]{1,0:T(8,128)(2,1)}, bf16[288,1024]{1,0:T(8,128)(2,1)S(1)}, u32[]{:S(2)}, u32[]{:S(2)}) %collective-permute-start) | collective-permute-done | bytes 589856 | tf_op jit(solution)/shard_map/ppermute | solution.py:185
  40.2 14.0 %collective-permute-done.1.w1 = bf16[288,1024]{1,0:T(8,128)(2,1)S(1)} collective-permute-done((bf16[288,1024]{1,0:T(8,128)(2,1)}, bf16[288,1024]{1,0:T(8,128)(2,1)S(1)}, u32[]{:S(2)}, u32[]{:S(2)}) %collective-permute-start.1) | collective-permute-done | bytes 589856 | tf_op jit(solution)/shard_map/ppermute | solution.py:185
  54.1 2.5 %collective-permute-start.3 = (bf16[512,1024]{1,0:T(8,128)(2,1)S(1)}, bf16[512,1024]{1,0:T(8,128)(2,1)S(1)}, u32[]{:S(2)}, u32[]{:S(2)}) collective-permute-start(bf16[512,1024]{1,0:T(8,128)(2,1)S(1)} %bitcast.13), channel_id=1, source_target_pairs={{0,1},{1,0},{2,3},{3,2},{4,5},{5,4},{6,7},{7,6},{8,9},{9,8},{10,11... | collective-permute-start | bytes 3145736 | tf_op jit(solution)/shard_map/ppermute | solution.py:188
  56.7 2.3 %collective-permute-done.3.oth_ref = bf16[512,1024]{1,0:T(8,128)(2,1)S(1)} collective-permute-done((bf16[512,1024]{1,0:T(8,128)(2,1)S(1)}, bf16[512,1024]{1,0:T(8,128)(2,1)S(1)}, u32[]{:S(2)}, u32[]{:S(2)}) %collective-permute-start.3) | collective-permute-done | bytes 1048608 | tf_op jit(solution)/shard_map/ppermute | solution.py:188
  58.9 2.8 %shard_map.103 = bf16[4,288,512]{2,1,0:T(8,128)(2,1)S(1)} custom-call(bf16[512,1024]{1,0:T(8,128)(2,1)S(1)} %bitcast.14, bf16[512,1024]{1,0:T(8,128)(2,1)S(1)} %collective-permute-done.3.oth_ref, bf16[288,1024]{1,0:T(8,128)(2,1)S(1)} %copy-done, bf16[288,1024]{1,0:T(8,128)(2,1)S(1)} %collective-permute-done.1.w1, ...), custom_call_target="tpu_custom_call" | custom-call | flops 1200000000 | bytes 6291456 | tf_op jit(solution)/shard_map/pallas_call | solution.py:205
  61.7 19.4 %all_to_all.20.p_ref = bf16[4,288,512]{2,1,0:T(8,128)(2,1)S(1)} all-to-all(bf16[4,288,512]{2,1,0:T(8,128)(2,1)S(1)} %shard_map.103), channel_id=1, replica_groups={{0,2,4,6},{1,3,5,7},{8,10,12,14},{9,11,13,15},{16,18,20,22},{17,19,21,2..., dimensions={0} | all-to-all | bytes 2359296 | tf_op jit(solution)/shard_map/all_to_all | solution.py:182
  81.3 17.2 %all_to_all.21.g_ref = bf16[4,288,512]{2,1,0:T(8,128)(2,1)S(1)} all-to-all(bf16[4,288,512]{2,1,0:T(8,128)(2,1)S(1)} %shard_map.104), channel_id=1, replica_groups={{0,2,4,6},{1,3,5,7},{8,10,12,14},{9,11,13,15},{16,18,20,22},{17,19,21,2..., dimensions={0} | all-to-all | bytes 2359296 | tf_op jit(solution)/shard_map/all_to_all | solution.py:182
  98.5 3.6 %shard_map.105 = (bf16[288,1024]{1,0:T(8,128)(2,1)}, bf16[288,1024]{1,0:T(8,128)(2,1)}, bf16[288,1024]{1,0:T(8,128)(2,1)}, bf16[288,1024]{1,0:T(8,128)(2,1)}) custom-call(bf16[4,288,512]{2,1,0:T(8,128)(2,1)S(1)} %all_to_all.21.g_ref, bf16[512,1024]{1,0:T(8,128)(2,1)S(1)} %bitcast.15, bf16[512,1024]{1,0:T(8,128)(2,1)S(1)} %collective-permute-done.3.oth_ref), custom_call_target="tpu_custom_call" | custom-call | flops 1200000000 | bytes 6291456 | tf_op jit(solution)/shard_map/pallas_call | solution.py:208
  102.1 1.3 shard_map.106
  103.5 4.6 %collective-permute-start.5 = (bf16[512,512]{1,0:T(8,128)(2,1)S(1)}, bf16[512,512]{1,0:T(8,128)(2,1)S(1)}, u32[]{:S(2)}, u32[]{:S(2)}) collective-permute-start(bf16[512,512]{1,0:T(8,128)(2,1)S(1)} %get-tuple-element.50), channel_id=1, source_target_pairs={{0,1},{1,0},{2,3},{3,2},{4,5},{5,4},{6,7},{7,6},{8,9},{9,8},{10,11... | collective-permute-start | bytes 1572872 | tf_op jit(solution)/shard_map/ppermute | solution.py:188
  108.1 2.4 %collective-permute-start.7 = (bf16[288,1024]{1,0:T(8,128)(2,1)}, bf16[288,1024]{1,0:T(8,128)(2,1)S(1)}, u32[]{:S(2)}, u32[]{:S(2)}) collective-permute-start(bf16[288,1024]{1,0:T(8,128)(2,1)} %get-tuple-element.55), channel_id=1, source_target_pairs={{0,4},{1,5},{2,6},{3,7},{4,0},{5,1},{6,2},{7,3},{8,12},{9,13},{10,... | collective-permute-start | bytes 1769480 | tf_op jit(solution)/shard_map/ppermute | solution.py:185
  110.5 1.0 fusion
  111.5 12.1 %all-to-all-start.3 = ((bf16[64,8,512]{2,1,0:T(8,128)(2,1)}), bf16[64,8,512]{2,1,0:T(8,128)(2,1)S(1)}, u32[]{:S(2)}, u32[]{:S(2)}) async-start(bf16[64,8,512]{2,1,0:T(8,128)(2,1)} %fusion), calls=%async_computation.3 | async-start | bytes 1048576 | tf_op jit(solution)/shard_map/all_to_all | solution.py:219
  123.7 4.1 %collective-permute-start.4 = (bf16[288,1024]{1,0:T(8,128)(2,1)}, bf16[288,1024]{1,0:T(8,128)(2,1)S(1)}, u32[]{:S(2)}, u32[]{:S(2)}) collective-permute-start(bf16[288,1024]{1,0:T(8,128)(2,1)} %get-tuple-element.46), channel_id=1, source_target_pairs={{0,6},{1,7},{2,0},{3,1},{4,2},{5,3},{6,4},{7,5},{8,14},{9,15},{10,... | collective-permute-start | bytes 1769480 | tf_op jit(solution)/shard_map/ppermute | solution.py:185
  127.7 1.9 %collective-permute-start.6 = (bf16[288,1024]{1,0:T(8,128)(2,1)}, bf16[288,1024]{1,0:T(8,128)(2,1)S(1)}, u32[]{:S(2)}, u32[]{:S(2)}) collective-permute-start(bf16[288,1024]{1,0:T(8,128)(2,1)} %get-tuple-element.53), channel_id=1, source_target_pairs={{0,2},{1,3},{2,4},{3,5},{4,6},{5,7},{6,0},{7,1},{8,10},{9,11},{10,... | collective-permute-start | bytes 1769480 | tf_op jit(solution)/shard_map/ppermute | solution.py:185
  129.7 1.1 shard_map.108
  130.7 10.6 %all-to-all-done.3 = bf16[64,8,512]{2,1,0:T(8,128)(2,1)S(1)} async-done(((bf16[64,8,512]{2,1,0:T(8,128)(2,1)}), bf16[64,8,512]{2,1,0:T(8,128)(2,1)S(1)}, u32[]{:S(2)}, u32[]{:S(2)}) %all-to-all-start.3) | async-done | bytes 524320 | tf_op jit(solution)/shard_map/all_to_all | solution.py:219
  142.2 2.8 %collective-permute-done.6.b3 = bf16[288,1024]{1,0:T(8,128)(2,1)S(1)} collective-permute-done((bf16[288,1024]{1,0:T(8,128)(2,1)}, bf16[288,1024]{1,0:T(8,128)(2,1)S(1)}, u32[]{:S(2)}, u32[]{:S(2)}) %collective-permute-start.6) | collective-permute-done | bytes 589856 | tf_op jit(solution)/shard_map/ppermute | solution.py:185
  145.0 1.1 shard_map.109
  (11 shorter events, 1.1 us)
Async XLA Ops:
  5.3 53.6 %copy-start = (bf16[288,1024]{1,0:T(8,128)(2,1)S(1)}, bf16[288,1024]{1,0:T(8,128)(2,1)}, u32[]{:S(2)}) copy-start(bf16[288,1024]{1,0:T(8,128)(2,1)} %get-tuple-element.38.w0) | copy-start | bytes 1769476
  5.3 48.8 %all-to-all-start = ((bf16[64,8,1024]{2,1,0:T(8,128)(2,1)}), bf16[64,8,1024]{2,1,0:T(8,128)(2,1)S(1)}, u32[]{:S(2)}, u32[]{:S(2)}) async-start(bf16[64,8,1024]{2,1,0:T(8,128)(2,1)} %bitcast.5), calls=%async_computation | async-start | bytes 2097152 | tf_op jit(solution)/shard_map/all_to_all | solution.py:199
  22.6 17.5 %collective-permute-start = (bf16[288,1024]{1,0:T(8,128)(2,1)}, bf16[288,1024]{1,0:T(8,128)(2,1)S(1)}, u32[]{:S(2)}, u32[]{:S(2)}) collective-permute-start(bf16[288,1024]{1,0:T(8,128)(2,1)} %get-tuple-element.34), channel_id=1, source_target_pairs={{0,4},{1,5},{2,6},{3,7},{4,0},{5,1},{6,2},{7,3},{8,12},{9,13},{10,... | collective-permute-start | bytes 1769480 | tf_op jit(solution)/shard_map/ppermute | solution.py:185
  27.3 26.8 %collective-permute-start.1 = (bf16[288,1024]{1,0:T(8,128)(2,1)}, bf16[288,1024]{1,0:T(8,128)(2,1)S(1)}, u32[]{:S(2)}, u32[]{:S(2)}) collective-permute-start(bf16[288,1024]{1,0:T(8,128)(2,1)} %get-tuple-element.35), channel_id=1, source_target_pairs={{0,2},{1,3},{2,4},{3,5},{4,6},{5,7},{6,0},{7,1},{8,10},{9,11},{10,... | collective-permute-start | bytes 1769480 | tf_op jit(solution)/shard_map/ppermute | solution.py:185
  29.5 24.6 %collective-permute-start.2 = (bf16[288,1024]{1,0:T(8,128)(2,1)}, bf16[288,1024]{1,0:T(8,128)(2,1)S(1)}, u32[]{:S(2)}, u32[]{:S(2)}) collective-permute-start(bf16[288,1024]{1,0:T(8,128)(2,1)} %get-tuple-element.36), channel_id=1, source_target_pairs={{0,6},{1,7},{2,0},{3,1},{4,2},{5,3},{6,4},{7,5},{8,14},{9,15},{10,... | collective-permute-start | bytes 1769480 | tf_op jit(solution)/shard_map/ppermute | solution.py:185
  54.1 4.8 %collective-permute-start.3 = (bf16[512,1024]{1,0:T(8,128)(2,1)S(1)}, bf16[512,1024]{1,0:T(8,128)(2,1)S(1)}, u32[]{:S(2)}, u32[]{:S(2)}) collective-permute-start(bf16[512,1024]{1,0:T(8,128)(2,1)S(1)} %bitcast.13), channel_id=1, source_target_pairs={{0,1},{1,0},{2,3},{3,2},{4,5},{5,4},{6,7},{7,6},{8,9},{9,8},{10,11... | collective-permute-start | bytes 3145736 | tf_op jit(solution)/shard_map/ppermute | solution.py:188
  103.5 7.1 %collective-permute-start.5 = (bf16[512,512]{1,0:T(8,128)(2,1)S(1)}, bf16[512,512]{1,0:T(8,128)(2,1)S(1)}, u32[]{:S(2)}, u32[]{:S(2)}) collective-permute-start(bf16[512,512]{1,0:T(8,128)(2,1)S(1)} %get-tuple-element.50), channel_id=1, source_target_pairs={{0,1},{1,0},{2,3},{3,2},{4,5},{5,4},{6,7},{7,6},{8,9},{9,8},{10,11... | collective-permute-start | bytes 1572872 | tf_op jit(solution)/shard_map/ppermute | solution.py:188
  108.1 21.6 %collective-permute-start.7 = (bf16[288,1024]{1,0:T(8,128)(2,1)}, bf16[288,1024]{1,0:T(8,128)(2,1)S(1)}, u32[]{:S(2)}, u32[]{:S(2)}) collective-permute-start(bf16[288,1024]{1,0:T(8,128)(2,1)} %get-tuple-element.55), channel_id=1, source_target_pairs={{0,4},{1,5},{2,6},{3,7},{4,0},{5,1},{6,2},{7,3},{8,12},{9,13},{10,... | collective-permute-start | bytes 1769480 | tf_op jit(solution)/shard_map/ppermute | solution.py:185
  110.5 19.1 %copy-start.1 = (bf16[288,1024]{1,0:T(8,128)(2,1)S(1)}, bf16[288,1024]{1,0:T(8,128)(2,1)}, u32[]{:S(2)}) copy-start(bf16[288,1024]{1,0:T(8,128)(2,1)} %get-tuple-element.54.b0) | copy-start | bytes 1769476
  111.5 29.9 %all-to-all-start.3 = ((bf16[64,8,512]{2,1,0:T(8,128)(2,1)}), bf16[64,8,512]{2,1,0:T(8,128)(2,1)S(1)}, u32[]{:S(2)}, u32[]{:S(2)}) async-start(bf16[64,8,512]{2,1,0:T(8,128)(2,1)} %fusion), calls=%async_computation.3 | async-start | bytes 1048576 | tf_op jit(solution)/shard_map/all_to_all | solution.py:219
  123.7 18.6 %collective-permute-start.4 = (bf16[288,1024]{1,0:T(8,128)(2,1)}, bf16[288,1024]{1,0:T(8,128)(2,1)S(1)}, u32[]{:S(2)}, u32[]{:S(2)}) collective-permute-start(bf16[288,1024]{1,0:T(8,128)(2,1)} %get-tuple-element.46), channel_id=1, source_target_pairs={{0,6},{1,7},{2,0},{3,1},{4,2},{5,3},{6,4},{7,5},{8,14},{9,15},{10,... | collective-permute-start | bytes 1769480 | tf_op jit(solution)/shard_map/ppermute | solution.py:185
  127.7 17.3 %collective-permute-start.6 = (bf16[288,1024]{1,0:T(8,128)(2,1)}, bf16[288,1024]{1,0:T(8,128)(2,1)S(1)}, u32[]{:S(2)}, u32[]{:S(2)}) collective-permute-start(bf16[288,1024]{1,0:T(8,128)(2,1)} %get-tuple-element.53), channel_id=1, source_target_pairs={{0,2},{1,3},{2,4},{3,5},{4,6},{5,7},{6,0},{7,1},{8,10},{9,11},{10,... | collective-permute-start | bytes 1769480 | tf_op jit(solution)/shard_map/ppermute | solution.py:185

commit v6 on v5

--- a/solution.py
+++ b/solution.py
@@ -139,12 +139,12 @@
         c.wait()
 
 
-def first_columns_kernel(b0, b2, gg_ref, gu_ref, gd_ref, sems):
-    place_columns(((0, b0), (2, b2)), (gg_ref, gu_ref, gd_ref), sems)
-
-
-def last_columns_kernel(b1, b3, gg_in, gu_in, gd_in, gg_ref, gu_ref, gd_ref, sems):
-    place_columns(((1, b1), (3, b3)), (gg_ref, gu_ref, gd_ref), sems)
+def first_columns_kernel(b2, b3, gg_ref, gu_ref, gd_ref, sems):
+    place_columns(((2, b2), (3, b3)), (gg_ref, gu_ref, gd_ref), sems)
+
+
+def last_columns_kernel(b0, b1, gg_in, gu_in, gd_in, gg_ref, gu_ref, gd_ref, sems):
+    place_columns(((0, b0), (1, b1)), (gg_ref, gu_ref, gd_ref), sems)
 
 
 def combine_kernel(place_ref, arrived_ref, out_ref):
@@ -223,7 +223,7 @@
         first_columns_kernel, whole, 2,
         scratch=[pltpu.SemaphoreType.DMA((2, 3))],
         out_specs=[HBM] * 3, flops=10**10, nbytes=2 << 20,
-    )(grads[0], got[2])
+    )(got[2], got[3])
     (grad_tokens,) = call(
         combine_kernel, [((toks, width), BF16)], 2, flops=10**7, nbytes=1 << 20,
     )(place, arrived.reshape(slots, width))
@@ -233,7 +233,7 @@
         scratch=[pltpu.SemaphoreType.DMA((2, 3))],
         in_specs=[VMEM] * 2 + [HBM] * 3, out_specs=[HBM] * 3,
         aliases={2: 0, 3: 1, 4: 2}, nbytes=2 << 20,
-    )(near, got[3], *outs)
+    )(grads[0], near, *outs)
     return (grad_tokens, *(g.reshape(1, hid, feats) for g in outs))
 
 

time: 147 us -> 148 us (level)
    all_to_all x1, waiting for transfers between devices: 10.6 us -> 3.24 us  [on_device(): lax.all_to_all(row_grad.reshape(groups, CAP, width), 'expert', 0, 0, tile...]
    ppermute x6, waiting for transfers between devices: 23.1 us -> 29.6 us  [shift(): lax.ppermute(v, 'tensor', [(i, (i + 2 * s) % n_tensor) for i in range(n_t...]
where the time goes in v6:
time: 148 us; the launch traced here: 146 us
  starting transfers between devices  56.7 us (38%)
  blocking collectives  36.5 us (25%)
  waiting for transfers between devices  35.1 us (24%)
  Pallas kernels  15.6 us (11%)
    all_to_all x2, blocking collectives, over_x(): lax.all_to_all(v, 'tensor', 0, 0, axis_index_groups=same_core, tiled=True)  36.5 us
    ppermute x6, waiting for transfers between devices, shift(): lax.ppermute(v, 'tensor', [(i, (i + 2 * s) % n_tensor) for i in range(n_t...  29.6 us
    ppermute x6, starting transfers between devices, shift(): lax.ppermute(v, 'tensor', [(i, (i + 2 * s) % n_tensor) for i in range(n_t...  20.2 us
    all_to_all x1, starting transfers between devices, on_device(): lax.all_to_all(sent.reshape(groups, CAP, 2 * width), 'expert', 0, 0, tile...  17.3 us
    all_to_all x1, starting transfers between devices, on_device(): lax.all_to_all(row_grad.reshape(groups, CAP, width), 'expert', 0, 0, tile...  12.1 us
    ppermute x2, starting transfers between devices, sibling(): return lax.ppermute(v, 'tensor', [(i, i ^ 1) for i in range(n_tensor)])  7.12 us
    pallas_call x1, Pallas kernels, on_device(): call(dispatch_kernel, [((slots, 2 * width), BF16), ((slots, toks), BF16)]...  4.7 us
    pallas_call x1, Pallas kernels, on_device(): call(grad_kernel, [pltpu.HBM(wide, BF16)] * X_CHIPS, 3, scratch=[pltpu.VM...  3.59 us
  transfers between devices with their start and end apart: 10, of which 5 were waited for; matrix products, arithmetic and copies ran while one was open for 1% of the time, Pallas kernels for 1%

profile of v6, /device:TPU:1, one launch (start us, length us, event | category | flops | bytes accessed | tf_op | source)
XLA Modules:
  0.0 145.8 jit_solution(2784287495754392856)
XLA Ops:
  0.6 4.7 %shard_map.102 = (bf16[512,1024]{1,0:T(8,128)(2,1)}, bf16[512,48]{1,0:T(8,128)(2,1)S(1)}, bf16[288,1024]{1,0:T(8,128)(2,1)}, bf16[288,1024]{1,0:T(8,128)(2,1)}, ...) custom-call(s32[8,48]{1,0:T(8,128)} %bitcast.23, f32[8,48]{1,0:T(8,128)} %bitcast.24, bf16[48,512]{1,0:T(8,128)(2,1)} %tok_ref.1, ...), custom_call_target="tpu_custom_call" | custom-call | flops 100000000 | bytes 6291456 | tf_op jit(solution)/shard_map/pallas_call | solution.py:191
  5.3 17.3 %all-to-all-start = ((bf16[64,8,1024]{2,1,0:T(8,128)(2,1)}), bf16[64,8,1024]{2,1,0:T(8,128)(2,1)S(1)}, u32[]{:S(2)}, u32[]{:S(2)}) async-start(bf16[64,8,1024]{2,1,0:T(8,128)(2,1)} %bitcast.5), calls=%async_computation | async-start | bytes 2097152 | tf_op jit(solution)/shard_map/all_to_all | solution.py:199
  22.6 4.7 %collective-permute-start = (bf16[288,1024]{1,0:T(8,128)(2,1)}, bf16[288,1024]{1,0:T(8,128)(2,1)S(1)}, u32[]{:S(2)}, u32[]{:S(2)}) collective-permute-start(bf16[288,1024]{1,0:T(8,128)(2,1)} %get-tuple-element.34), channel_id=1, source_target_pairs={{0,4},{1,5},{2,6},{3,7},{4,0},{5,1},{6,2},{7,3},{8,12},{9,13},{10,... | collective-permute-start | bytes 1769480 | tf_op jit(solution)/shard_map/ppermute | solution.py:185
  27.3 2.2 %collective-permute-start.1 = (bf16[288,1024]{1,0:T(8,128)(2,1)}, bf16[288,1024]{1,0:T(8,128)(2,1)S(1)}, u32[]{:S(2)}, u32[]{:S(2)}) collective-permute-start(bf16[288,1024]{1,0:T(8,128)(2,1)} %get-tuple-element.35), channel_id=1, source_target_pairs={{0,2},{1,3},{2,4},{3,5},{4,6},{5,7},{6,0},{7,1},{8,10},{9,11},{10,... | collective-permute-start | bytes 1769480 | tf_op jit(solution)/shard_map/ppermute | solution.py:185
  29.5 4.3 %collective-permute-start.2 = (bf16[288,1024]{1,0:T(8,128)(2,1)}, bf16[288,1024]{1,0:T(8,128)(2,1)S(1)}, u32[]{:S(2)}, u32[]{:S(2)}) collective-permute-start(bf16[288,1024]{1,0:T(8,128)(2,1)} %get-tuple-element.36), channel_id=1, source_target_pairs={{0,6},{1,7},{2,0},{3,1},{4,2},{5,3},{6,4},{7,5},{8,14},{9,15},{10,... | collective-permute-start | bytes 1769480 | tf_op jit(solution)/shard_map/ppermute | solution.py:185
  33.8 6.4 %collective-permute-done.w2 = bf16[288,1024]{1,0:T(8,128)(2,1)S(1)} collective-permute-done((bf16[288,1024]{1,0:T(8,128)(2,1)}, bf16[288,1024]{1,0:T(8,128)(2,1)S(1)}, u32[]{:S(2)}, u32[]{:S(2)}) %collective-permute-start) | collective-permute-done | bytes 589856 | tf_op jit(solution)/shard_map/ppermute | solution.py:185
  40.2 14.0 %collective-permute-done.1.w1 = bf16[288,1024]{1,0:T(8,128)(2,1)S(1)} collective-permute-done((bf16[288,1024]{1,0:T(8,128)(2,1)}, bf16[288,1024]{1,0:T(8,128)(2,1)S(1)}, u32[]{:S(2)}, u32[]{:S(2)}) %collective-permute-start.1) | collective-permute-done | bytes 589856 | tf_op jit(solution)/shard_map/ppermute | solution.py:185
  54.1 2.5 %collective-permute-start.3 = (bf16[512,1024]{1,0:T(8,128)(2,1)S(1)}, bf16[512,1024]{1,0:T(8,128)(2,1)S(1)}, u32[]{:S(2)}, u32[]{:S(2)}) collective-permute-start(bf16[512,1024]{1,0:T(8,128)(2,1)S(1)} %bitcast.13), channel_id=1, source_target_pairs={{0,1},{1,0},{2,3},{3,2},{4,5},{5,4},{6,7},{7,6},{8,9},{9,8},{10,11... | collective-permute-start | bytes 3145736 | tf_op jit(solution)/shard_map/ppermute | solution.py:188
  56.7 2.3 %collective-permute-done.3.oth_ref = bf16[512,1024]{1,0:T(8,128)(2,1)S(1)} collective-permute-done((bf16[512,1024]{1,0:T(8,128)(2,1)S(1)}, bf16[512,1024]{1,0:T(8,128)(2,1)S(1)}, u32[]{:S(2)}, u32[]{:S(2)}) %collective-permute-start.3) | collective-permute-done | bytes 1048608 | tf_op jit(solution)/shard_map/ppermute | solution.py:188
  58.9 2.8 %shard_map.103 = bf16[4,288,512]{2,1,0:T(8,128)(2,1)S(1)} custom-call(bf16[512,1024]{1,0:T(8,128)(2,1)S(1)} %bitcast.14, bf16[512,1024]{1,0:T(8,128)(2,1)S(1)} %collective-permute-done.3.oth_ref, bf16[288,1024]{1,0:T(8,128)(2,1)S(1)} %copy-done, bf16[288,1024]{1,0:T(8,128)(2,1)S(1)} %collective-permute-done.1.w1, ...), custom_call_target="tpu_custom_call" | custom-call | flops 1200000000 | bytes 6291456 | tf_op jit(solution)/shard_map/pallas_call | solution.py:205
  61.7 19.4 %all_to_all.20.p_ref = bf16[4,288,512]{2,1,0:T(8,128)(2,1)S(1)} all-to-all(bf16[4,288,512]{2,1,0:T(8,128)(2,1)S(1)} %shard_map.103), channel_id=1, replica_groups={{0,2,4,6},{1,3,5,7},{8,10,12,14},{9,11,13,15},{16,18,20,22},{17,19,21,2..., dimensions={0} | all-to-all | bytes 2359296 | tf_op jit(solution)/shard_map/all_to_all | solution.py:182
  81.3 17.2 %all_to_all.21.g_ref = bf16[4,288,512]{2,1,0:T(8,128)(2,1)S(1)} all-to-all(bf16[4,288,512]{2,1,0:T(8,128)(2,1)S(1)} %shard_map.104), channel_id=1, replica_groups={{0,2,4,6},{1,3,5,7},{8,10,12,14},{9,11,13,15},{16,18,20,22},{17,19,21,2..., dimensions={0} | all-to-all | bytes 2359296 | tf_op jit(solution)/shard_map/all_to_all | solution.py:182
  98.5 3.6 %shard_map.105 = (bf16[288,1024]{1,0:T(8,128)(2,1)}, bf16[288,1024]{1,0:T(8,128)(2,1)}, bf16[288,1024]{1,0:T(8,128)(2,1)}, bf16[288,1024]{1,0:T(8,128)(2,1)}) custom-call(bf16[4,288,512]{2,1,0:T(8,128)(2,1)S(1)} %all_to_all.21.g_ref, bf16[512,1024]{1,0:T(8,128)(2,1)S(1)} %bitcast.15, bf16[512,1024]{1,0:T(8,128)(2,1)S(1)} %collective-permute-done.3.oth_ref), custom_call_target="tpu_custom_call" | custom-call | flops 1200000000 | bytes 6291456 | tf_op jit(solution)/shard_map/pallas_call | solution.py:208
  102.1 1.3 shard_map.106
  103.5 4.6 %collective-permute-start.5 = (bf16[512,512]{1,0:T(8,128)(2,1)S(1)}, bf16[512,512]{1,0:T(8,128)(2,1)S(1)}, u32[]{:S(2)}, u32[]{:S(2)}) collective-permute-start(bf16[512,512]{1,0:T(8,128)(2,1)S(1)} %get-tuple-element.50), channel_id=1, source_target_pairs={{0,1},{1,0},{2,3},{3,2},{4,5},{5,4},{6,7},{7,6},{8,9},{9,8},{10,11... | collective-permute-start | bytes 1572872 | tf_op jit(solution)/shard_map/ppermute | solution.py:188
  108.1 2.5 %collective-permute-start.6 = (bf16[288,1024]{1,0:T(8,128)(2,1)}, bf16[288,1024]{1,0:T(8,128)(2,1)S(1)}, u32[]{:S(2)}, u32[]{:S(2)}) collective-permute-start(bf16[288,1024]{1,0:T(8,128)(2,1)} %get-tuple-element.54), channel_id=1, source_target_pairs={{0,4},{1,5},{2,6},{3,7},{4,0},{5,1},{6,2},{7,3},{8,12},{9,13},{10,... | collective-permute-start | bytes 1769480 | tf_op jit(solution)/shard_map/ppermute | solution.py:185
  110.5 2.8 %collective-permute-start.7 = (bf16[288,1024]{1,0:T(8,128)(2,1)}, bf16[288,1024]{1,0:T(8,128)(2,1)S(1)}, u32[]{:S(2)}, u32[]{:S(2)}) collective-permute-start(bf16[288,1024]{1,0:T(8,128)(2,1)} %get-tuple-element.55), channel_id=1, source_target_pairs={{0,2},{1,3},{2,4},{3,5},{4,6},{5,7},{6,0},{7,1},{8,10},{9,11},{10,... | collective-permute-start | bytes 1769480 | tf_op jit(solution)/shard_map/ppermute | solution.py:185
  113.4 1.0 fusion
  114.3 12.1 %all-to-all-start.3 = ((bf16[64,8,512]{2,1,0:T(8,128)(2,1)}), bf16[64,8,512]{2,1,0:T(8,128)(2,1)S(1)}, u32[]{:S(2)}, u32[]{:S(2)}) async-start(bf16[64,8,512]{2,1,0:T(8,128)(2,1)} %fusion), calls=%async_computation.3 | async-start | bytes 1048576 | tf_op jit(solution)/shard_map/all_to_all | solution.py:219
  126.5 3.8 %collective-permute-start.4 = (bf16[288,1024]{1,0:T(8,128)(2,1)}, bf16[288,1024]{1,0:T(8,128)(2,1)S(1)}, u32[]{:S(2)}, u32[]{:S(2)}) collective-permute-start(bf16[288,1024]{1,0:T(8,128)(2,1)} %get-tuple-element.46), channel_id=1, source_target_pairs={{0,6},{1,7},{2,0},{3,1},{4,2},{5,3},{6,4},{7,5},{8,14},{9,15},{10,... | collective-permute-start | bytes 1769480 | tf_op jit(solution)/shard_map/ppermute | solution.py:185
  130.3 9.3 %collective-permute-done.7.b3 = bf16[288,1024]{1,0:T(8,128)(2,1)S(1)} collective-permute-done((bf16[288,1024]{1,0:T(8,128)(2,1)}, bf16[288,1024]{1,0:T(8,128)(2,1)S(1)}, u32[]{:S(2)}, u32[]{:S(2)}) %collective-permute-start.7) | collective-permute-done | bytes 589856 | tf_op jit(solution)/shard_map/ppermute | solution.py:185
  139.6 1.1 shard_map.108
  140.6 3.2 %all-to-all-done.3 = bf16[64,8,512]{2,1,0:T(8,128)(2,1)S(1)} async-done(((bf16[64,8,512]{2,1,0:T(8,128)(2,1)}), bf16[64,8,512]{2,1,0:T(8,128)(2,1)S(1)}, u32[]{:S(2)}, u32[]{:S(2)}) %all-to-all-start.3) | async-done | bytes 524320 | tf_op jit(solution)/shard_map/all_to_all | solution.py:219
  144.7 1.1 shard_map.109
  (11 shorter events, 1.1 us)
Async XLA Ops:
  5.3 53.6 %copy-start = (bf16[288,1024]{1,0:T(8,128)(2,1)S(1)}, bf16[288,1024]{1,0:T(8,128)(2,1)}, u32[]{:S(2)}) copy-start(bf16[288,1024]{1,0:T(8,128)(2,1)} %get-tuple-element.38.w0) | copy-start | bytes 1769476
  5.3 48.8 %all-to-all-start = ((bf16[64,8,1024]{2,1,0:T(8,128)(2,1)}), bf16[64,8,1024]{2,1,0:T(8,128)(2,1)S(1)}, u32[]{:S(2)}, u32[]{:S(2)}) async-start(bf16[64,8,1024]{2,1,0:T(8,128)(2,1)} %bitcast.5), calls=%async_computation | async-start | bytes 2097152 | tf_op jit(solution)/shard_map/all_to_all | solution.py:199
  22.6 17.5 %collective-permute-start = (bf16[288,1024]{1,0:T(8,128)(2,1)}, bf16[288,1024]{1,0:T(8,128)(2,1)S(1)}, u32[]{:S(2)}, u32[]{:S(2)}) collective-permute-start(bf16[288,1024]{1,0:T(8,128)(2,1)} %get-tuple-element.34), channel_id=1, source_target_pairs={{0,4},{1,5},{2,6},{3,7},{4,0},{5,1},{6,2},{7,3},{8,12},{9,13},{10,... | collective-permute-start | bytes 1769480 | tf_op jit(solution)/shard_map/ppermute | solution.py:185
  27.3 26.8 %collective-permute-start.1 = (bf16[288,1024]{1,0:T(8,128)(2,1)}, bf16[288,1024]{1,0:T(8,128)(2,1)S(1)}, u32[]{:S(2)}, u32[]{:S(2)}) collective-permute-start(bf16[288,1024]{1,0:T(8,128)(2,1)} %get-tuple-element.35), channel_id=1, source_target_pairs={{0,2},{1,3},{2,4},{3,5},{4,6},{5,7},{6,0},{7,1},{8,10},{9,11},{10,... | collective-permute-start | bytes 1769480 | tf_op jit(solution)/shard_map/ppermute | solution.py:185
  29.5 24.6 %collective-permute-start.2 = (bf16[288,1024]{1,0:T(8,128)(2,1)}, bf16[288,1024]{1,0:T(8,128)(2,1)S(1)}, u32[]{:S(2)}, u32[]{:S(2)}) collective-permute-start(bf16[288,1024]{1,0:T(8,128)(2,1)} %get-tuple-element.36), channel_id=1, source_target_pairs={{0,6},{1,7},{2,0},{3,1},{4,2},{5,3},{6,4},{7,5},{8,14},{9,15},{10,... | collective-permute-start | bytes 1769480 | tf_op jit(solution)/shard_map/ppermute | solution.py:185
  54.1 4.8 %collective-permute-start.3 = (bf16[512,1024]{1,0:T(8,128)(2,1)S(1)}, bf16[512,1024]{1,0:T(8,128)(2,1)S(1)}, u32[]{:S(2)}, u32[]{:S(2)}) collective-permute-start(bf16[512,1024]{1,0:T(8,128)(2,1)S(1)} %bitcast.13), channel_id=1, source_target_pairs={{0,1},{1,0},{2,3},{3,2},{4,5},{5,4},{6,7},{7,6},{8,9},{9,8},{10,11... | collective-permute-start | bytes 3145736 | tf_op jit(solution)/shard_map/ppermute | solution.py:188
  103.5 9.9 %collective-permute-start.5 = (bf16[512,512]{1,0:T(8,128)(2,1)S(1)}, bf16[512,512]{1,0:T(8,128)(2,1)S(1)}, u32[]{:S(2)}, u32[]{:S(2)}) collective-permute-start(bf16[512,512]{1,0:T(8,128)(2,1)S(1)} %get-tuple-element.50), channel_id=1, source_target_pairs={{0,1},{1,0},{2,3},{3,2},{4,5},{5,4},{6,7},{7,6},{8,9},{9,8},{10,11... | collective-permute-start | bytes 1572872 | tf_op jit(solution)/shard_map/ppermute | solution.py:188
  108.1 22.2 %collective-permute-start.6 = (bf16[288,1024]{1,0:T(8,128)(2,1)}, bf16[288,1024]{1,0:T(8,128)(2,1)S(1)}, u32[]{:S(2)}, u32[]{:S(2)}) collective-permute-start(bf16[288,1024]{1,0:T(8,128)(2,1)} %get-tuple-element.54), channel_id=1, source_target_pairs={{0,4},{1,5},{2,6},{3,7},{4,0},{5,1},{6,2},{7,3},{8,12},{9,13},{10,... | collective-permute-start | bytes 1769480 | tf_op jit(solution)/shard_map/ppermute | solution.py:185
  110.5 29.1 %collective-permute-start.7 = (bf16[288,1024]{1,0:T(8,128)(2,1)}, bf16[288,1024]{1,0:T(8,128)(2,1)S(1)}, u32[]{:S(2)}, u32[]{:S(2)}) collective-permute-start(bf16[288,1024]{1,0:T(8,128)(2,1)} %get-tuple-element.55), channel_id=1, source_target_pairs={{0,2},{1,3},{2,4},{3,5},{4,6},{5,7},{6,0},{7,1},{8,10},{9,11},{10,... | collective-permute-start | bytes 1769480 | tf_op jit(solution)/shard_map/ppermute | solution.py:185
  114.3 29.5 %all-to-all-start.3 = ((bf16[64,8,512]{2,1,0:T(8,128)(2,1)}), bf16[64,8,512]{2,1,0:T(8,128)(2,1)S(1)}, u32[]{:S(2)}, u32[]{:S(2)}) async-start(bf16[64,8,512]{2,1,0:T(8,128)(2,1)} %fusion), calls=%async_computation.3 | async-start | bytes 1048576 | tf_op jit(solution)/shard_map/all_to_all | solution.py:219
  126.5 18.2 %copy-start.1 = (bf16[288,1024]{1,0:T(8,128)(2,1)S(1)}, bf16[288,1024]{1,0:T(8,128)(2,1)}, u32[]{:S(2)}) copy-start(bf16[288,1024]{1,0:T(8,128)(2,1)} %get-tuple-element.52.b0) | copy-start | bytes 1769476
  126.5 18.2 %collective-permute-start.4 = (bf16[288,1024]{1,0:T(8,128)(2,1)}, bf16[288,1024]{1,0:T(8,128)(2,1)S(1)}, u32[]{:S(2)}, u32[]{:S(2)}) collective-permute-start(bf16[288,1024]{1,0:T(8,128)(2,1)} %get-tuple-element.46), channel_id=1, source_target_pairs={{0,6},{1,7},{2,0},{3,1},{4,2},{5,3},{6,4},{7,5},{8,14},{9,15},{10,... | collective-permute-start | bytes 1769480 | tf_op jit(solution)/shard_map/ppermute | solution.py:185
